TPU v7x, 32 devices: a whole 2x2x4 slice. The times are simulated.
32 devices in a mesh: dp: 4 (over y, core), expert: 8 (over z, x).
Axes of the slice: x: 2, y: 2, z: 4, core: 2. Of those that a mesh axis runs over, the one named last changes fastest.
Arguments:
- latents: bfloat16 [4096, 2048], P(('dp', 'expert')), may hold values from -6 to 6
- expert_ids: int32 [4096, 6], P(('dp', 'expert')), may hold values from 0 to 31, as said below
- gate_weights: float32 [4096, 6], P(('dp', 'expert')), may hold values from 0.05 to 0.5
- capacity: int32 [4, 32], P('dp'), may hold values from 12 to 24, as said below
- hot_expert: int32 [4], P('dp'), may hold values from 0 to 31
- w_gate: bfloat16 [32, 2048, 704], P('expert'), may hold values from -0.125 to 0.125
- w_up: bfloat16 [32, 2048, 704], P('expert'), may hold values from -0.125 to 0.125
- w_down: bfloat16 [32, 704, 2048], P('expert'), may hold values from -0.21875 to 0.21875
- shared_gate: bfloat16 [2048, 2048], P(None, 'dp'), may hold values from -0.125 to 0.125
- shared_up: bfloat16 [2048, 2048], P(None, 'dp'), may hold values from -0.125 to 0.125
- shared_down: bfloat16 [2048, 2048], P('dp'), may hold values from -0.125 to 0.125
Outputs:
- mixed: bfloat16 [4096, 2048], P(('dp', 'expert'))
Inputs may be any that keep to these rules, and one draw needn't show every extreme that they name: `expert_ids`: A token names 6 different experts. In every block of 128 token rows the hot expert of the block's data group is named in exactly 40 assignments, and every other expert in at most 24. `capacity`: each data group's row holds the value 24 in at least one column.
All inputs are finite; a program needn't handle non-finite values.
Results may differ from a plain program's by a relative error of at most 0.0095.
Values may be sent and summed in bfloat16 or wider, within the bound.
No kernel may reach another device: no remote copies, remote signals or barrier semaphores. Data moves between devices by JAX's collectives and lax.ppermute only.
A program may use at most 128 MiB of HBM per device.

v0:
```python
import jax
import jax.numpy as jnp
from jax import lax
from jax.sharding import PartitionSpec as P

CAP = 40


def expert_block(rows, w_gate, w_up, w_down):
    gate = jnp.einsum("sacd,adf->sacf", rows, w_gate, preferred_element_type=jnp.float32)
    upper = jnp.einsum("sacd,adf->sacf", rows, w_up, preferred_element_type=jnp.float32)
    hidden = (jax.nn.silu(gate) * upper).astype(jnp.bfloat16)
    return jnp.einsum("sacf,afd->sacd", hidden, w_down, preferred_element_type=jnp.float32).astype(
        jnp.bfloat16
    )


def pack_rows(source, slots, total):
    width = source.shape[1]
    buffer = jnp.zeros((total + 1, width), jnp.bfloat16).at[slots].set(source)
    return buffer[:total]


def on_device(
    latents,
    expert_ids,
    gate_weights,
    capacity,
    hot_expert,
    w_gate,
    w_up,
    w_down,
    shared_gate,
    shared_up,
    shared_down,
):
    tok_dev = latents.shape[0]
    width = latents.shape[1]
    top = expert_ids.shape[1]
    experts = capacity.shape[1]
    local_experts = w_gate.shape[0]
    groups = lax.axis_size("expert")
    piece = lax.all_gather(latents, "dp", axis=0, tiled=True)
    gate = jnp.dot(piece, shared_gate, preferred_element_type=jnp.float32)
    upper = jnp.dot(piece, shared_up, preferred_element_type=jnp.float32)
    hidden = (jax.nn.silu(gate) * upper).astype(jnp.bfloat16)
    shared = lax.psum_scatter(
        jnp.dot(hidden, shared_down, preferred_element_type=jnp.float32).astype(jnp.bfloat16),
        "dp",
        scatter_dimension=0,
        tiled=True,
    ).astype(jnp.float32)
    flat = expert_ids.reshape(-1)
    gates = gate_weights.reshape(-1)
    labels = jnp.arange(experts, dtype=jnp.int32)
    onehot = (flat[:, None] == labels[None, :]).astype(jnp.int32)
    rank = jnp.sum((jnp.cumsum(onehot, axis=0) - onehot) * onehot, axis=1)
    hot = hot_expert[0]
    limit = jnp.where(labels == hot, CAP, capacity[0])
    bound = jnp.sum(onehot * limit[None, :], axis=1)
    kept = rank < bound
    token_of = jnp.arange(tok_dev * top, dtype=jnp.int32) // top
    source = latents[token_of]
    total = experts * CAP
    slot = jnp.where(kept, flat * CAP + rank, total)
    send = pack_rows(source, slot, total).reshape(groups, local_experts, CAP, width)
    out = expert_block(
        lax.all_to_all(send, "expert", split_axis=0, concat_axis=0, tiled=True),
        w_gate,
        w_up,
        w_down,
    )
    back = lax.all_to_all(out, "expert", split_axis=0, concat_axis=0, tiled=True)
    picked = back.reshape(total, width)[jnp.minimum(slot, total - 1)]
    picked = jnp.where(kept[:, None], picked, jnp.zeros_like(picked))
    routed = (gates[:, None] * picked.astype(jnp.float32)).reshape(tok_dev, top, width).sum(axis=1)
    return (shared + routed).astype(jnp.bfloat16)


def solution(mesh):
    placed = (
        P(("dp", "expert"), None),
        P(("dp", "expert"), None),
        P(("dp", "expert"), None),
        P("dp", None),
        P("dp"),
        P("expert", None, None),
        P("expert", None, None),
        P("expert", None, None),
        P(None, "dp"),
        P(None, "dp"),
        P("dp", None),
    )
    return jax.shard_map(
        on_device, mesh=mesh, in_specs=placed, out_specs=P(("dp", "expert"), None), check_vma=False
    )
```

profile of v0, /device:TPU:0, one launch (start us, length us, event | category | flops | bytes accessed | tf_op | source)
XLA Modules:
  0.0 353.6 jit_solution(10920231519552775778)
XLA Ops:
  6.5 0.9 copy.21
  7.5 0.1 eq.42
  7.6 0.1 eq.38
  7.8 0.7 broadcast_multiply_fusion
  8.5 1.7 reduce-window.6
  10.2 0.3 slice_reduce_fusion
  11.2 0.1 copy.24
  11.3 0.1 mul.65
  11.5 0.7 fusion.35
  12.1 0.1 fusion.30
  12.3 31.4 %scatter_custom_fusion = bf16[1281,2048]{1,0:T(8,128)(2,1)} fusion(s32[768]{0:T(1024)S(1)} %get-tuple-element.8, bf16[128,2048]{1,0:T(8,128)(2,1)} %param.11, s32[1024]{0:T(1024)S(1)} %pad_clamp_fusion.1, bf16[]{:T(256)} %constant.15.clone.1), kind=kCustom, calls=%fused_computation.20 | custom fusion | bytes 5247488 | tf_op jit(solution)/shard_map/scatter | solution.py:20
  43.7 2.5 slice-done
  46.2 122.8 %all_to_all.10 = bf16[8,4,40,2048]{3,2,1,0:T(8,128)(2,1)} all-to-all(bf16[8,4,40,2048]{3,2,1,0:T(8,128)(2,1)S(1)} %bitcast.75), channel_id=1, replica_groups=mesh['dp'=4,'expert'=8] {'expert'}, dimensions={0} | all-to-all | bytes 10485760 | tf_op jit(solution)/shard_map/all_to_all | solution.py:68
  169.0 12.1 %fusion.2 = f32[4,8,40,704]{3,2,1,0:T(8,128)} fusion(bf16[4,2048,704]{1,2,0:T(8,128)(2,1)} %param.17, bf16[8,4,40,2048]{3,2,1,0:T(8,128)(2,1)} %all_to_all.10), kind=kOutput, calls=%fused_computation.5 | convolution fusion | flops 3690987520 | bytes 20381696 | tf_op jit(solution)/shard_map/sacd,adf->sacf/dot_general | solution.py:11
  181.1 16.1 %convert_bitcast_fusion = bf16[8,4,40,2048]{3,2,0,1:T(8,128)(2,1)} fusion(bf16[4,704,2048]{2,1,0:T(8,128)(2,1)} %param.18, f32[4,8,40,704]{3,2,1,0:T(8,128)} %fusion.2, bf16[4,2048,704]{1,2,0:T(8,128)(2,1)} %param.16, bf16[8,4,40,2048]{3,2,1,0:T(8,128)(2,1)} %all_to_all.10), kind=kOutput, calls=%fused_computation.10 | convolution fusion | flops 7390003200 | bytes 37158912 | tf_op jit(solution)/shard_map/sacf,afd->sacd/dot_general | solution.py:13
  197.2 5.7 %copy.27 = bf16[8,4,40,2048]{3,2,1,0:T(8,128)(2,1)} copy(bf16[8,4,40,2048]{3,2,0,1:T(8,128)(2,1)} %convert_bitcast_fusion) | data formatting | bytes 10485760 | tf_op jit(solution)/shard_map/convert_element_type | solution.py:13
  202.9 4.6 %all-to-all-start.1 = ((bf16[8,4,40,2048]{3,2,1,0:T(8,128)(2,1)}), bf16[8,4,40,2048]{3,2,1,0:T(8,128)(2,1)}, u32[]{:S(2)}, u32[]{:S(2)}) async-start(bf16[8,4,40,2048]{3,2,1,0:T(8,128)(2,1)} %copy.27), calls=%async_computation.2 | async-start | bytes 10485760 | tf_op jit(solution)/shard_map/all_to_all | solution.py:73
  207.6 0.0 all-gather.2.cloned.1.call-start
  207.6 0.7 all-gather.2.cloned.1.call-update
  208.3 0.3 reduce-scatter.2.cloned.1.call-start
  208.6 25.4 %all-gather.2.cloned.1.call-done = bf16[512,2048]{1,0:T(8,128)(2,1)} async-done(((bf16[128,2048]{1,0:T(8,128)(2,1)}), bf16[512,2048]{1,0:T(8,128)(2,1)}) %all-gather.2.cloned.1.call-update) | async-done | bytes 2097168 | tf_op jit(solution)/shard_map/all_gather | solution.py:43
  233.9 3.5 fusion.38
  237.4 6.0 %convolution_convert_fusion = bf16[512,2048]{1,0:T(8,128)(2,1)} fusion(bf16[512,2048]{1,0:T(8,128)(2,1)S(1)} %copy-done, bf16[512,2048]{1,0:T(8,128)(2,1)} %all-gather.2.cloned.1.call-done, bf16[2048,512]{1,0:T(8,128)(2,1)} %param.20, f32[512,512]{1,0:T(8,128)S(1)} %fusion.38), kind=kOutput, calls=%fused_computation.22 | convolution fusion | flops 2150105088 | bytes 9437184 | tf_op jit(solution)/shard_map/dot_general | solution.py:48
  243.4 0.0 reduce-scatter.2.cloned.1.call-update
  243.5 0.2 lt.53
  243.6 0.1 copy.20
  243.8 78.6 %all-to-all-done.1 = bf16[8,4,40,2048]{3,2,1,0:T(8,128)(2,1)} async-done(((bf16[8,4,40,2048]{3,2,1,0:T(8,128)(2,1)}), bf16[8,4,40,2048]{3,2,1,0:T(8,128)(2,1)}, u32[]{:S(2)}, u32[]{:S(2)}) %all-to-all-start.1) | async-done | bytes 5242912 | tf_op jit(solution)/shard_map/all_to_all | solution.py:73
  322.4 10.3 %gather_fusion = bf16[768,2048]{1,0:T(8,128)(2,1)} fusion(bf16[1280,2048]{1,0:T(8,128)(2,1)} %bitcast.13, s32[1024]{0:T(1024)S(1)} %pad_clamp_fusion), kind=kCustom, calls=%fused_computation.1 | custom fusion | bytes 6294528 | tf_op jit(solution)/shard_map/gather | solution.py:74
  332.6 6.3 %gather.10 = bf16[128,6,2048]{2,1,0:T(8,128)(2,1)} reshape(bf16[768,2048]{1,0:T(8,128)(2,1)} %gather_fusion) | data formatting | bytes 6291456 | tf_op jit(solution)/shard_map/gather | solution.py:74
  338.9 6.0 %multiply_reduce_fusion = f32[128,2048]{1,0:T(8,128)S(1)} fusion(bf16[128,6,2048]{2,1,0:T(8,128)(2,1)} %gather.10, f32[128,6]{1,0:T(8,128)S(1)} %copy.20, pred[128,6]{1,0:T(8,128)(4,1)S(1)} %lt.53), kind=kLoop, calls=%fused_computation.9 | loop fusion | flops 6029312 | bytes 4198144 | tf_op jit(solution)/shard_map/reduce_sum | solution.py:76
  344.8 0.0 reduce-scatter.2.cloned.1.call-done
  344.9 1.9 add_convert_fusion
  (12 shorter events, 0.1 us)
Async XLA Ops:
  6.5 230.9 %copy-start = (bf16[512,2048]{1,0:T(8,128)(2,1)S(1)}, bf16[512,2048]{1,0:T(8,128)(2,1)}, u32[]{:S(2)}) copy-start(bf16[512,2048]{1,0:T(8,128)(2,1)} %param.21) | copy-start | bytes 6291460
  43.7 2.5 slice-start
  202.9 119.4 %all-to-all-start.1 = ((bf16[8,4,40,2048]{3,2,1,0:T(8,128)(2,1)}), bf16[8,4,40,2048]{3,2,1,0:T(8,128)(2,1)}, u32[]{:S(2)}, u32[]{:S(2)}) async-start(bf16[8,4,40,2048]{3,2,1,0:T(8,128)(2,1)} %copy.27), calls=%async_computation.2 | async-start | bytes 10485760 | tf_op jit(solution)/shard_map/all_to_all | solution.py:73
  207.6 26.4 %all-gather.2.cloned.1.call-start = ((), (), s32[]{:S(2)}) async-start(), calls=%async_computation.3 | async-start | bytes 2621440 | tf_op jit(solution)/shard_map/all_gather | solution.py:43
  208.3 136.5 %reduce-scatter.2.cloned.1.call-start = ((), (), s32[]{:S(2)}) async-start(), calls=%async_computation.4 | async-start | bytes 2621440 | tf_op jit(solution)/shard_map/reduce_scatter | solution.py:47
  237.4 6.2 %copy-start.1 = (f32[128,6]{0,1:T(8,128)S(1)}, f32[128,6]{0,1:T(8,128)}, u32[]{:S(2)}) copy-start(f32[128,6]{0,1:T(8,128)} %param.13) | copy-start | bytes 9220
Sparse Core Ops, SparseCore 0:
  210.0 23.9 all-gather.1
  243.6 31.4 reduce-scatter.1
where the time goes:
time: 354 us
  blocking collectives  123 us (35%)
  waiting for transfers between devices  105 us (30%)
  local copies, waits for them, and re-layouts  58.1 us (16%)
  matrix products  37.7 us (11%)
  between operations  14.2 us (4%)
  other arithmetic  11.2 us (3%)
  starting transfers between devices  4.94 us (1%)
    all_to_all x1, blocking collectives, on_device(): lax.all_to_all(send, 'expert', split_axis=0, concat_axis=0, tiled=True)  123 us
    all_to_all x1, waiting for transfers between devices, on_device(): lax.all_to_all(out, 'expert', split_axis=0, concat_axis=0, tiled=True)  78.6 us
    scatter x1, local copies, waits for them, and re-layouts, pack_rows(): buffer = jnp.zeros((total + 1, width), jnp.bfloat16).at[slots].set(source)  31.4 us
    all_gather x1, waiting for transfers between devices, on_device(): piece = lax.all_gather(latents, 'dp', axis=0, tiled=True)  25.4 us
    gather x2, local copies, waits for them, and re-layouts, on_device(): picked = back.reshape(total, width)[jnp.minimum(slot, total - 1)]  16.5 us
    dot_general x1, matrix products, expert_block(): jnp.einsum('sacf,afd->sacd', hidden, w_down, preferred_element_type=jnp.f...  16.1 us
    dot_general x1, matrix products, expert_block(): jnp.einsum('sacd,adf->sacf', rows, w_up, preferred_element_type=jnp.float32)  12.1 us
  transfers between devices with their start and end apart: 3, of which 2 were waited for; matrix products, arithmetic and copies ran while one was open for 9% of the time, Pallas kernels for 0%

commit v1 on v0

v1 whole, which is shorter than its diff:
```python
import functools

import jax
import jax.numpy as jnp
from jax import lax
from jax.experimental import pallas as pl
from jax.experimental.pallas import tpu as pltpu
from jax.sharding import PartitionSpec as P

HOT_SLOTS = 40
SLOTS = 24
EXTRA = HOT_SLOTS - SLOTS
BF16 = jnp.bfloat16
F32 = jnp.float32
ANY = pl.BlockSpec(memory_space=pl.ANY)
VMEM = pl.BlockSpec(memory_space=pltpu.VMEM)
SMEM = pl.BlockSpec(memory_space=pltpu.SMEM)


def ring_of(count):
    return list(range(0, count, 2)) + list(range(count - 1, 0, -2))


def offsets_of(count):
    order = [0, count // 2]
    for hop in range(1, count // 2):
        order += [hop, count - hop]
    return order


def dot(a, b):
    return jnp.dot(a, b, preferred_element_type=F32)


def routing(expert_ids, gate_weights, capacity, hot_expert, experts):
    tokens, top = expert_ids.shape
    ids, gates = expert_ids.T, gate_weights.T
    labels = jnp.arange(experts, dtype=jnp.int32)[:, None]
    chosen = jnp.zeros((experts, tokens), jnp.bool_)
    weight = jnp.zeros((experts, tokens), F32)
    for k in range(top):
        here = ids[k][None, :] == labels
        chosen = chosen | here
        weight = weight + jnp.where(here, gates[k][None, :], 0.0)
    place = jnp.arange(tokens, dtype=jnp.int32)
    earlier = (place[:, None] < place[None, :]).astype(BF16)
    rank = dot(chosen.astype(BF16), earlier)
    limit = jnp.where(labels == hot_expert[0], HOT_SLOTS, capacity[0][:, None]).astype(F32)
    kept = chosen & (rank < limit)
    return jnp.stack([jnp.where(kept, rank, -1.0), jnp.where(kept, weight, 0.0)], axis=1)


def experts_kernel(count, local, idx, meta, *refs):
    half = 64
    pairs = count // 2
    offsets = offsets_of(count)
    units = {}
    at = 0
    for o in range(count):
        units[o] = refs[at : at + (1 if o == 0 else 2)]
        at += len(units[o])
    w_gate, w_up, w_down = refs[at : at + 3]
    at += 3
    outs = [refs[at + 2 * o : at + 2 * o + 2] for o in range(count)]
    at += 2 * count
    x, wg, wu, wd, rows, rows_x, eo, sel, scale, scale_x, sem_x, sem_w, sem_o = refs[at:]
    wide = 2 * SLOTS
    wide_x = 2 * EXTRA
    hot = idx[count]

    loads = []
    for slot, o in enumerate(offsets):
        mine = []
        for h, unit in enumerate(units[o]):
            length = unit.shape[0]
            copy = pltpu.make_async_copy(unit, x.at[slot, pl.ds(h * length, length)], sem_x.at[slot, h])
            copy.start()
            mine.append(copy)
        loads.append(mine)
    weights = []
    for e in range(local):
        mine = []
        for k, (source, target) in enumerate(((w_gate, wg), (w_up, wu), (w_down, wd))):
            copy = pltpu.make_async_copy(source.at[e], target.at[e], sem_w.at[e, k])
            copy.start()
            mine.append(copy)
        weights.append(mine)

    lane = lax.broadcasted_iota(jnp.int32, (1, 256), 1)
    second = (lane >= 128).astype(F32)
    for p in range(pairs):
        for slot in (2 * p, 2 * p + 1):
            for copy in loads[slot]:
                copy.wait()
        info = [meta[idx[offsets[2 * p + i]]] for i in range(2)]
        blocks = []
        for e in range(local):
            rank = jnp.concatenate([info[0][2 * e : 2 * e + 1], info[1][2 * e : 2 * e + 1]], axis=1)
            gate = jnp.concatenate([info[0][2 * e + 1 : 2 * e + 2], info[1][2 * e + 1 : 2 * e + 2]], axis=1)
            key = jnp.where((rank >= 0) & (rank < SLOTS), rank + SLOTS * second, -1.0).astype(jnp.int32)
            pick = (lax.broadcasted_iota(jnp.int32, (wide, 256), 0) == key).astype(F32)
            blocks.append(pick)
            scale[e, pl.ds(p * wide, wide), :] = jnp.broadcast_to(
                jnp.sum(pick * gate, axis=1, keepdims=True), (wide, 128)
            )
            here = hot == e
            key_x = jnp.where((rank >= SLOTS) & here, rank - SLOTS + EXTRA * second, -1.0).astype(jnp.int32)
            pick_x = (lax.broadcasted_iota(jnp.int32, (wide_x, 256), 0) == key_x).astype(F32)
            gate_x = jnp.sum(pick_x * gate, axis=1, keepdims=True)
            if e == 0:
                extra, extra_gate = pick_x, gate_x
            else:
                extra, extra_gate = extra + pick_x, extra_gate + gate_x
        scale_x[pl.ds(p * wide_x, wide_x), :] = jnp.broadcast_to(extra_gate, (wide_x, 128))
        blocks.append(extra)
        pick = jnp.concatenate(blocks, axis=0).astype(BF16)
        sel[p] = pick
        pair = x[2 * p : 2 * p + 2].reshape(256, x.shape[2])
        got = dot(pick, pair).astype(BF16)
        for e in range(local):
            rows[e, pl.ds(p * wide, wide), :] = got[e * wide : (e + 1) * wide]
        rows_x[pl.ds(p * wide_x, wide_x), :] = got[local * wide :]
        eo[p, pl.ds(local * wide, wide_x), :] = jnp.zeros((wide_x, x.shape[2]), BF16)

    def hidden_of(e, tokens, weight):
        gate = dot(tokens, wg[e])
        upper = dot(tokens, wu[e])
        return (gate / (1.0 + jnp.exp(-gate)) * upper * weight).astype(BF16)

    for e in range(local):
        weights[e][0].wait()
        weights[e][1].wait()
        hidden = hidden_of(e, rows[e], scale[e][:, :1])
        weights[e][2].wait()
        out = dot(hidden, wd[e]).astype(BF16)
        for p in range(pairs):
            eo[p, pl.ds(e * wide, wide), :] = out[p * wide : (p + 1) * wide]

        @pl.when(hot == e)
        def _():
            more = dot(hidden_of(e, rows_x[...], scale_x[...][:, :1]), wd[e]).astype(BF16)
            for p in range(pairs):
                eo[p, pl.ds(local * wide, wide_x), :] = more[p * wide_x : (p + 1) * wide_x]

    stores = []
    for p in range(pairs):
        total = lax.dot_general(sel[p], eo[p], (((0,), (0,)), ((), ())), preferred_element_type=F32)
        x[2 * p : 2 * p + 2] = total.astype(BF16).reshape(2, 128, x.shape[2])
        for slot in (2 * p, 2 * p + 1):
            for h in range(2):
                copy = pltpu.make_async_copy(
                    x.at[slot, pl.ds(h * half, half)], outs[offsets[slot]][h], sem_o.at[slot, h]
                )
                copy.start()
                stores.append(copy)
    for copy in stores:
        copy.wait()


def run_experts(count, local, idx, meta, blocks, w_gate, w_up, w_down):
    width, hidden = w_gate.shape[1:]
    wide, wide_x = 2 * SLOTS, 2 * EXTRA
    pairs = count // 2
    high = local * wide + wide_x
    flat = [unit for o in range(count) for unit in blocks[o]]
    flops = 2 * 3 * width * hidden * count * (local * SLOTS + EXTRA) + 4 * count * 128 * high * width
    return pl.pallas_call(
        functools.partial(experts_kernel, count, local),
        out_shape=[jax.ShapeDtypeStruct((64, width), BF16)] * (2 * count),
        in_specs=[SMEM, VMEM] + [ANY] * (len(flat) + 3),
        out_specs=[ANY] * (2 * count),
        scratch_shapes=[
            pltpu.VMEM((count, 128, width), BF16),
            pltpu.VMEM((local, width, hidden), BF16),
            pltpu.VMEM((local, width, hidden), BF16),
            pltpu.VMEM((local, hidden, width), BF16),
            pltpu.VMEM((local, pairs * wide, width), BF16),
            pltpu.VMEM((pairs * wide_x, width), BF16),
            pltpu.VMEM((pairs, high, width), BF16),
            pltpu.VMEM((pairs, high, 256), BF16),
            pltpu.VMEM((local, pairs * wide, 128), F32),
            pltpu.VMEM((pairs * wide_x, 128), F32),
            pltpu.SemaphoreType.DMA((count, 2)),
            pltpu.SemaphoreType.DMA((local, 3)),
            pltpu.SemaphoreType.DMA((count, 2)),
        ],
        cost_estimate=pl.CostEstimate(
            flops=flops,
            transcendentals=count * local * SLOTS * hidden,
            bytes_accessed=2 * (3 * local * width * hidden + 2 * count * 128 * width),
        ),
        compiler_params=pltpu.CompilerParams(vmem_limit_bytes=60 << 20),
        name="routed_experts",
    )(idx, meta, *flat, w_gate, w_up, w_down)


def shared_kernel(first, second, w_gate, w_up, w_down, out_first, out_second):
    tokens = jnp.concatenate([first[...], second[...]], axis=0)
    gate = dot(tokens, w_gate[...])
    upper = dot(tokens, w_up[...])
    hidden = (gate / (1.0 + jnp.exp(-gate)) * upper).astype(BF16)
    out = dot(hidden, w_down[...]).astype(BF16)
    rows = first.shape[0]
    out_first[...] = out[:rows]
    out_second[...] = out[rows:]


def run_shared(first, second, w_gate, w_up, w_down):
    rows, width = first.shape
    hidden = w_gate.shape[1]
    return pl.pallas_call(
        shared_kernel,
        out_shape=[jax.ShapeDtypeStruct((rows, width), BF16)] * 2,
        in_specs=[VMEM] * 5,
        out_specs=[VMEM] * 2,
        cost_estimate=pl.CostEstimate(
            flops=2 * 3 * 2 * rows * width * hidden,
            transcendentals=2 * rows * hidden,
            bytes_accessed=2 * (3 * width * hidden + 4 * rows * width),
        ),
        compiler_params=pltpu.CompilerParams(vmem_limit_bytes=48 << 20),
        name="shared_experts",
    )(first, second, w_gate, w_up, w_down)


def on_device(
    latents,
    expert_ids,
    gate_weights,
    capacity,
    hot_expert,
    w_gate,
    w_up,
    w_down,
    shared_gate,
    shared_up,
    shared_down,
):
    tokens, width = latents.shape
    half = tokens // 2
    experts = capacity.shape[1]
    local = w_gate.shape[0]
    count = lax.axis_size("expert")
    n_dp = lax.axis_size("dp")
    ring = ring_of(count)
    forward = [(ring[i], ring[(i + 1) % count]) for i in range(count)]
    backward = [(b, a) for a, b in forward]
    mid = count // 2

    own = [latents[:half], latents[half:]]
    blocks = {o: [None, None] for o in range(count)}
    for h in range(2):
        up, down = own[h], own[h]
        for hop in range(1, mid + 1):
            if hop < mid or h == 0:
                up = lax.ppermute(up, "expert", forward)
                blocks[hop][h] = up
            if hop < mid or h == 1:
                down = lax.ppermute(down, "expert", backward)
                blocks[count - hop][h] = down
    blocks[0] = [latents]

    info = routing(expert_ids, gate_weights, capacity, hot_expert, experts)
    meta = lax.all_to_all(
        info.reshape(count, 2 * local, tokens), "expert", split_axis=0, concat_axis=0, tiled=True
    )
    me = lax.axis_index("expert")
    table = []
    for e in range(count):
        at = ring.index(e)
        table.append([ring[(at - o) % count] for o in range(count)])
    idx = jnp.array(table, jnp.int32)[me]
    idx = jnp.concatenate([idx, (hot_expert - me * local).astype(jnp.int32)])

    bits = [1 << b for b in range(n_dp.bit_length() - 1)]
    near = {0: latents}
    for bit in reversed(bits):
        swap = [(d, d ^ bit) for d in range(n_dp)]
        for r in list(near):
            near[r ^ bit] = lax.ppermute(near[r], "dp", swap)
    part = {}
    for r in range(0, n_dp, 2):
        part[r], part[r + 1] = run_shared(near[r], near[r + 1], shared_gate, shared_up, shared_down)
    for bit in bits:
        swap = [(d, d ^ bit) for d in range(n_dp)]
        for r in sorted(part):
            if r & bit:
                came = lax.ppermute(part.pop(r), "dp", swap)
                total = part[r ^ bit].astype(F32) + came.astype(F32)
                part[r ^ bit] = total if len(bits) and bit == bits[-1] else total.astype(BF16)
    shared = part[0]

    flat = run_experts(count, local, idx, meta, blocks, w_gate, w_up, w_down)
    done = {o: [flat[2 * o], flat[2 * o + 1]] for o in range(count)}

    result = []
    for h in range(2):
        pieces = [done[0][h]]
        for step, perm, long in ((-1, forward, h == 0), (1, backward, h == 1)):
            start = mid if long else mid - 1
            acc = done[(step * start) % count][h]
            for k in range(start, 0, -1):
                came = lax.ppermute(acc, "expert", perm)
                if k > 1:
                    acc = (came.astype(F32) + done[(step * (k - 1)) % count][h].astype(F32)).astype(BF16)
            pieces.append(came)
        total = shared[h * half : (h + 1) * half].astype(F32)
        for piece in pieces:
            total = total + piece.astype(F32)
        result.append(total.astype(BF16))
    return jnp.concatenate(result, axis=0)


def solution(mesh):
    placed = (
        P(("dp", "expert"), None),
        P(("dp", "expert"), None),
        P(("dp", "expert"), None),
        P("dp", None),
        P("dp"),
        P("expert", None, None),
        P("expert", None, None),
        P("expert", None, None),
        P(None, "dp"),
        P(None, "dp"),
        P("dp", None),
    )
    return jax.shard_map(
        on_device, mesh=mesh, in_specs=placed, out_specs=P(("dp", "expert"), None), check_vma=False
    )
```

time: 354 us -> 157 us (0.44)
  blocking collectives: 123 us -> 0 us
  waiting for transfers between devices: 105 us -> 33.6 us
  starting transfers between devices: 4.94 us -> 46.2 us
  matrix products: 37.7 us -> 0.1 us
  Pallas kernels: 0 us -> 33.4 us
  local copies, waits for them, and re-layouts: 58.1 us -> 37.6 us
  between operations: 14.2 us -> 1.01 us
  other arithmetic: 11.2 us -> 3.5 us
    all_to_all x1 -> x0, blocking collectives: 123 us -> none  [on_device(): lax.all_to_all(send, 'expert', split_axis=0, concat_axis=0, tiled=True)]
    all_to_all x1, waiting for transfers between devices: 78.6 us -> 0.01 us  [on_device(): lax.all_to_all(info.reshape(count, 2 * local, tokens), 'expert', split_ax...]
    ppermute x0 -> x34, starting transfers between devices: none -> 40 us  [the longest x14 20 us: on_device(): came = lax.ppermute(acc, 'expert', perm)]
    dot_general x4 -> x1, matrix products: 37.7 us -> 0.1 us  [dot(): return jnp.dot(a, b, preferred_element_type=F32)]
    ppermute x0 -> x34, waiting for transfers between devices: none -> 33.6 us  [the longest x14 19.8 us: on_device(): came = lax.ppermute(acc, 'expert', perm)]
    pallas_call x0 -> x3, Pallas kernels: none -> 33.4 us  [the longest x1 24.8 us: run_experts(): pl.pallas_call(functools.partial(experts_kernel, count, local), out_shape...]
    unnamed x6 -> x46, local copies, waits for them, and re-layouts: 1.07 us -> 33.4 us
    scatter x1 -> x0, local copies, waits for them, and re-layouts: 31.4 us -> none  [pack_rows(): buffer = jnp.zeros((total + 1, width), jnp.bfloat16).at[slots].set(source)]
  transfers between devices with their start and end apart: 3 -> 35, of which waited for: 2 -> 15; matrix products, arithmetic and copies ran while one was open for 9% -> 25% of each run, Pallas kernels for 0% -> 21%
where the time goes in v1:
time: 157 us; the launch traced here: 155 us
  starting transfers between devices  46.2 us (29%)
  local copies, waits for them, and re-layouts  37.6 us (24%)
  waiting for transfers between devices  33.6 us (21%)
  Pallas kernels  33.4 us (21%)
  other arithmetic  3.5 us (2%)
    unnamed x46, local copies, waits for them, and re-layouts  33.4 us
    pallas_call x1, Pallas kernels, run_experts(): pl.pallas_call(functools.partial(experts_kernel, count, local), out_shape...  24.8 us
    ppermute x14, starting transfers between devices, on_device(): came = lax.ppermute(acc, 'expert', perm)  20 us
    ppermute x14, waiting for transfers between devices, on_device(): came = lax.ppermute(acc, 'expert', perm)  19.8 us
    ppermute x7, starting transfers between devices, on_device(): up = lax.ppermute(up, 'expert', forward)  15.8 us
    ppermute x7, waiting for transfers between devices, on_device(): up = lax.ppermute(up, 'expert', forward)  13.6 us
    pallas_call x2, Pallas kernels, run_shared(): pl.pallas_call(shared_kernel, out_shape=[jax.ShapeDtypeStruct((rows, widt...  8.67 us
    all_to_all x1, starting transfers between devices, on_device(): lax.all_to_all(info.reshape(count, 2 * local, tokens), 'expert', split_ax...  6.25 us
  transfers between devices with their start and end apart: 35, of which 15 were waited for; matrix products, arithmetic and copies ran while one was open for 25% of the time, Pallas kernels for 21%

profile of v1, /device:TPU:0, one launch (start us, length us, event | category | flops | bytes accessed | tf_op | source)
XLA Modules:
  0.0 155.5 jit_solution(18037365342368097188)
XLA Ops:
  1.1 3.1 %collective-permute-start.6 = (bf16[64,2048]{1,0:T(8,128)(2,1)S(1)}, bf16[64,2048]{1,0:T(8,128)(2,1)S(1)}, u32[]{:S(2)}, u32[]{:S(2)}) collective-permute-start(bf16[64,2048]{1,0:T(8,128)(2,1)S(1)} %get-tuple-element.48), channel_id=1, source_target_pairs={{0,2},{2,4},{4,6},{6,7},{7,5},{5,3},{3,1},{1,0},{8,10},{10,12},{12... | collective-permute-start | bytes 786440 | tf_op jit(solution)/shard_map/ppermute | solution.py:256
  4.1 2.0 %collective-permute-start.7 = (bf16[64,2048]{1,0:T(8,128)(2,1)S(1)}, bf16[64,2048]{1,0:T(8,128)(2,1)S(1)}, u32[]{:S(2)}, u32[]{:S(2)}) collective-permute-start(bf16[64,2048]{1,0:T(8,128)(2,1)S(1)} %get-tuple-element.47), channel_id=1, source_target_pairs={{0,2},{2,4},{4,6},{6,7},{7,5},{5,3},{3,1},{1,0},{8,10},{10,12},{12... | collective-permute-start | bytes 786440 | tf_op jit(solution)/shard_map/ppermute | solution.py:256
  6.2 2.0 %collective-permute-start.2 = (bf16[128,2048]{1,0:T(8,128)(2,1)}, bf16[128,2048]{1,0:T(8,128)(2,1)}, u32[]{:S(2)}, u32[]{:S(2)}) collective-permute-start(bf16[128,2048]{1,0:T(8,128)(2,1)} %refs_0_.1), channel_id=1, source_target_pairs={{0,16},{8,24},{16,0},{24,8},{1,17},{9,25},{17,1},{25,9},{2,18},{10... | collective-permute-start | bytes 1572872 | tf_op jit(solution)/shard_map/ppermute | solution.py:280
  8.1 3.1 %collective-permute-done.6.refs_1_ = bf16[64,2048]{1,0:T(8,128)(2,1)S(1)} collective-permute-done((bf16[64,2048]{1,0:T(8,128)(2,1)S(1)}, bf16[64,2048]{1,0:T(8,128)(2,1)S(1)}, u32[]{:S(2)}, u32[]{:S(2)}) %collective-permute-start.6) | collective-permute-done | bytes 262176 | tf_op jit(solution)/shard_map/ppermute | solution.py:256
  11.2 2.1 %collective-permute-start.8 = (bf16[64,2048]{1,0:T(8,128)(2,1)S(1)}, bf16[64,2048]{1,0:T(8,128)(2,1)S(1)}, u32[]{:S(2)}, u32[]{:S(2)}) collective-permute-start(bf16[64,2048]{1,0:T(8,128)(2,1)S(1)} %collective-permute-done.6.refs_1_), channel_id=1, source_target_pairs={{0,2},{2,4},{4,6},{6,7},{7,5},{5,3},{3,1},{1,0},{8,10},{10,12},{12... | collective-permute-start | bytes 786440 | tf_op jit(solution)/shard_map/ppermute | solution.py:256
  16.8 2.1 %collective-permute-start.9 = (bf16[64,2048]{1,0:T(8,128)(2,1)S(1)}, bf16[64,2048]{1,0:T(8,128)(2,1)}, u32[]{:S(2)}, u32[]{:S(2)}) collective-permute-start(bf16[64,2048]{1,0:T(8,128)(2,1)S(1)} %collective-permute-done.7.refs_2_), channel_id=1, source_target_pairs={{0,2},{2,4},{4,6},{6,7},{7,5},{5,3},{3,1},{1,0},{8,10},{10,12},{12... | collective-permute-start | bytes 786440 | tf_op jit(solution)/shard_map/ppermute | solution.py:256
  19.0 3.4 %collective-permute-done.8.refs_3_ = bf16[64,2048]{1,0:T(8,128)(2,1)S(1)} collective-permute-done((bf16[64,2048]{1,0:T(8,128)(2,1)S(1)}, bf16[64,2048]{1,0:T(8,128)(2,1)S(1)}, u32[]{:S(2)}, u32[]{:S(2)}) %collective-permute-start.8) | collective-permute-done | bytes 262176 | tf_op jit(solution)/shard_map/ppermute | solution.py:256
  22.4 2.1 %collective-permute-start.10 = (bf16[64,2048]{1,0:T(8,128)(2,1)S(1)}, bf16[64,2048]{1,0:T(8,128)(2,1)}, u32[]{:S(2)}, u32[]{:S(2)}) collective-permute-start(bf16[64,2048]{1,0:T(8,128)(2,1)S(1)} %collective-permute-done.8.refs_3_), channel_id=1, source_target_pairs={{0,2},{2,4},{4,6},{6,7},{7,5},{5,3},{3,1},{1,0},{8,10},{10,12},{12... | collective-permute-start | bytes 786440 | tf_op jit(solution)/shard_map/ppermute | solution.py:256
  25.4 2.7 %collective-permute-done.9.refs_4_ = bf16[64,2048]{1,0:T(8,128)(2,1)} collective-permute-done((bf16[64,2048]{1,0:T(8,128)(2,1)S(1)}, bf16[64,2048]{1,0:T(8,128)(2,1)}, u32[]{:S(2)}, u32[]{:S(2)}) %collective-permute-start.9) | collective-permute-done | bytes 262176 | tf_op jit(solution)/shard_map/ppermute | solution.py:256
  28.2 2.1 %collective-permute-start.11 = (bf16[64,2048]{1,0:T(8,128)(2,1)}, bf16[64,2048]{1,0:T(8,128)(2,1)}, u32[]{:S(2)}, u32[]{:S(2)}) collective-permute-start(bf16[64,2048]{1,0:T(8,128)(2,1)} %collective-permute-done.9.refs_4_), channel_id=1, source_target_pairs={{0,2},{2,4},{4,6},{6,7},{7,5},{5,3},{3,1},{1,0},{8,10},{10,12},{12... | collective-permute-start | bytes 786440 | tf_op jit(solution)/shard_map/ppermute | solution.py:256
  30.3 3.4 %collective-permute-done.10.refs_5_ = bf16[64,2048]{1,0:T(8,128)(2,1)} collective-permute-done((bf16[64,2048]{1,0:T(8,128)(2,1)S(1)}, bf16[64,2048]{1,0:T(8,128)(2,1)}, u32[]{:S(2)}, u32[]{:S(2)}) %collective-permute-start.10) | collective-permute-done | bytes 262176 | tf_op jit(solution)/shard_map/ppermute | solution.py:256
  33.8 2.1 %collective-permute-start.12 = (bf16[64,2048]{1,0:T(8,128)(2,1)}, bf16[64,2048]{1,0:T(8,128)(2,1)}, u32[]{:S(2)}, u32[]{:S(2)}) collective-permute-start(bf16[64,2048]{1,0:T(8,128)(2,1)} %collective-permute-done.10.refs_5_), channel_id=1, source_target_pairs={{0,2},{2,4},{4,6},{6,7},{7,5},{5,3},{3,1},{1,0},{8,10},{10,12},{12... | collective-permute-start | bytes 786440 | tf_op jit(solution)/shard_map/ppermute | solution.py:256
  36.6 6.3 %all-to-all-start = ((f32[8,8,128]{2,1,0:T(8,128)}), f32[8,8,128]{2,1,0:T(8,128)S(1)}, u32[]{:S(2)}, u32[]{:S(2)}) async-start(f32[8,8,128]{2,1,0:T(8,128)} %bitcast.20), calls=%async_computation | async-start | bytes 65536 | tf_op jit(solution)/shard_map/all_to_all | solution.py:264
  42.8 16.3 %copy.14.refs_15_ = bf16[4,2048,704]{2,1,0:T(8,128)(2,1)} copy(bf16[4,2048,704]{1,2,0:T(8,128)(2,1)} %param.17) | data formatting | bytes 23068672 | tf_op args[5]
  59.2 16.4 %copy.15.refs_16_ = bf16[4,2048,704]{2,1,0:T(8,128)(2,1)} copy(bf16[4,2048,704]{1,2,0:T(8,128)(2,1)} %param.18) | data formatting | bytes 23068672 | tf_op args[6]
  78.2 24.8 %routed_experts.1 = (bf16[64,2048]{1,0:T(8,128)(2,1)}, bf16[64,2048]{1,0:T(8,128)(2,1)}, bf16[64,2048]{1,0:T(8,128)(2,1)}, bf16[64,2048]{1,0:T(8,128)(2,1)}, bf1...) custom-call(s32[9]{0:T(128)} %pad_add_fusion.idx, ...), custom_call_target="tpu_custom_call" | custom-call | flops 9630121984 | bytes 42991616 | tf_op jit(solution)/shard_map/routed_experts/pallas_call | solution.py:167
  103.0 2.1 %collective-permute-start.27 = (bf16[64,2048]{1,0:T(8,128)(2,1)}, bf16[64,2048]{1,0:T(8,128)(2,1)S(1)}, u32[]{:S(2)}, u32[]{:S(2)}) collective-permute-start(bf16[64,2048]{1,0:T(8,128)(2,1)} %get-tuple-element.38), channel_id=1, source_target_pairs={{0,2},{2,4},{4,6},{6,7},{7,5},{5,3},{3,1},{1,0},{8,10},{10,12},{12... | collective-permute-start | bytes 786440 | tf_op jit(solution)/shard_map/ppermute | solution.py:303
  105.1 4.2 %shared_experts.2 = (bf16[128,2048]{1,0:T(8,128)(2,1)S(1)}, bf16[128,2048]{1,0:T(8,128)(2,1)S(1)}) custom-call(bf16[128,2048]{1,0:T(8,128)(2,1)S(1)} %copy-done.2, bf16[128,2048]{1,0:T(8,128)(2,1)} %collective-permute-done.second, bf16[2048,512]{1,0:T(8,128)(2,1)S(1)} %copy-done, bf16[2048,512]{1,0:T(8,128)(2,1)} %w_up.3, bf16[512,2048]{1,0:T(8,128)(2,1)} %w_down.3), custom_call_target="tpu_custom_call" | custom-call | flops 1610612736 | bytes 8388608 | tf_op jit(solution)/shard_map/shared_experts/pallas_call | solution.py:211
  109.5 1.7 %collective-permute-start.30 = (bf16[64,2048]{1,0:T(8,128)(2,1)}, bf16[64,2048]{1,0:T(8,128)(2,1)S(1)}, u32[]{:S(2)}, u32[]{:S(2)}) collective-permute-start(bf16[64,2048]{1,0:T(8,128)(2,1)} %get-tuple-element.41), channel_id=1, source_target_pairs={{2,0},{4,2},{6,4},{7,6},{5,7},{3,5},{1,3},{0,1},{10,8},{12,10},{14... | collective-permute-start | bytes 786440 | tf_op jit(solution)/shard_map/ppermute | solution.py:303
  111.6 1.6 %collective-permute-start.24 = (bf16[64,2048]{1,0:T(8,128)(2,1)}, bf16[64,2048]{1,0:T(8,128)(2,1)S(1)}, u32[]{:S(2)}, u32[]{:S(2)}) collective-permute-start(bf16[64,2048]{1,0:T(8,128)(2,1)} %get-tuple-element.34), channel_id=1, source_target_pairs={{2,0},{4,2},{6,4},{7,6},{5,7},{3,5},{1,3},{0,1},{10,8},{12,10},{14... | collective-permute-start | bytes 786440 | tf_op jit(solution)/shard_map/ppermute | solution.py:303
  113.2 4.4 %shared_experts.3 = (bf16[128,2048]{1,0:T(8,128)(2,1)S(1)}, bf16[128,2048]{1,0:T(8,128)(2,1)S(1)}) custom-call(bf16[128,2048]{1,0:T(8,128)(2,1)} %collective-permute-done.2.first, bf16[128,2048]{1,0:T(8,128)(2,1)} %collective-permute-done.3.second, bf16[2048,512]{1,0:T(8,128)(2,1)S(1)} %copy-done, bf16[2048,512]{1,0:T(8,128)(2,1)} %w_up.3, ...), custom_call_target="tpu_custom_call" | custom-call | flops 1610612736 | bytes 8388608 | tf_op jit(solution)/shard_map/shared_experts/pallas_call | solution.py:211
  118.9 2.1 %collective-permute-start.28 = (bf16[64,2048]{1,0:T(8,128)(2,1)S(1)}, bf16[64,2048]{1,0:T(8,128)(2,1)S(1)}, u32[]{:S(2)}, u32[]{:S(2)}) collective-permute-start(bf16[64,2048]{1,0:T(8,128)(2,1)S(1)} %add_convert_fusion.6), channel_id=1, source_target_pairs={{0,2},{2,4},{4,6},{6,7},{7,5},{5,3},{3,1},{1,0},{8,10},{10,12},{12... | collective-permute-start | bytes 786440 | tf_op jit(solution)/shard_map/ppermute | solution.py:303
  121.7 2.8 %collective-permute-done.24 = bf16[64,2048]{1,0:T(8,128)(2,1)S(1)} collective-permute-done((bf16[64,2048]{1,0:T(8,128)(2,1)}, bf16[64,2048]{1,0:T(8,128)(2,1)S(1)}, u32[]{:S(2)}, u32[]{:S(2)}) %collective-permute-start.24) | collective-permute-done | bytes 262176 | tf_op jit(solution)/shard_map/ppermute | solution.py:303
  124.5 2.1 %collective-permute-start.21 = (bf16[64,2048]{1,0:T(8,128)(2,1)S(1)}, bf16[64,2048]{1,0:T(8,128)(2,1)S(1)}, u32[]{:S(2)}, u32[]{:S(2)}) collective-permute-start(bf16[64,2048]{1,0:T(8,128)(2,1)S(1)} %add_convert_fusion.11), channel_id=1, source_target_pairs={{0,2},{2,4},{4,6},{6,7},{7,5},{5,3},{3,1},{1,0},{8,10},{10,12},{12... | collective-permute-start | bytes 786440 | tf_op jit(solution)/shard_map/ppermute | solution.py:303
  128.5 1.9 %collective-permute-done.31 = bf16[64,2048]{1,0:T(8,128)(2,1)S(1)} collective-permute-done((bf16[64,2048]{1,0:T(8,128)(2,1)S(1)}, bf16[64,2048]{1,0:T(8,128)(2,1)S(1)}, u32[]{:S(2)}, u32[]{:S(2)}) %collective-permute-start.31) | collective-permute-done | bytes 262176 | tf_op jit(solution)/shard_map/ppermute | solution.py:303
  130.4 2.0 %collective-permute-start.29 = (bf16[64,2048]{1,0:T(8,128)(2,1)S(1)}, bf16[64,2048]{1,0:T(8,128)(2,1)S(1)}, u32[]{:S(2)}, u32[]{:S(2)}) collective-permute-start(bf16[64,2048]{1,0:T(8,128)(2,1)S(1)} %add_convert_fusion.5), channel_id=1, source_target_pairs={{0,2},{2,4},{4,6},{6,7},{7,5},{5,3},{3,1},{1,0},{8,10},{10,12},{12... | collective-permute-start | bytes 786440 | tf_op jit(solution)/shard_map/ppermute | solution.py:303
  136.0 2.0 %collective-permute-start.22 = (bf16[64,2048]{1,0:T(8,128)(2,1)S(1)}, bf16[64,2048]{1,0:T(8,128)(2,1)S(1)}, u32[]{:S(2)}, u32[]{:S(2)}) collective-permute-start(bf16[64,2048]{1,0:T(8,128)(2,1)S(1)} %add_convert_fusion.10), channel_id=1, source_target_pairs={{0,2},{2,4},{4,6},{6,7},{7,5},{5,3},{3,1},{1,0},{8,10},{10,12},{12... | collective-permute-start | bytes 786440 | tf_op jit(solution)/shard_map/ppermute | solution.py:303
  138.1 2.8 %collective-permute-done.32 = bf16[64,2048]{1,0:T(8,128)(2,1)S(1)} collective-permute-done((bf16[64,2048]{1,0:T(8,128)(2,1)S(1)}, bf16[64,2048]{1,0:T(8,128)(2,1)S(1)}, u32[]{:S(2)}, u32[]{:S(2)}) %collective-permute-start.32) | collective-permute-done | bytes 262176 | tf_op jit(solution)/shard_map/ppermute | solution.py:303
  140.9 1.6 %collective-permute-start.26 = (bf16[64,2048]{1,0:T(8,128)(2,1)S(1)}, bf16[64,2048]{1,0:T(8,128)(2,1)S(1)}, u32[]{:S(2)}, u32[]{:S(2)}) collective-permute-start(bf16[64,2048]{1,0:T(8,128)(2,1)S(1)} %add_convert_fusion.7), channel_id=1, source_target_pairs={{2,0},{4,2},{6,4},{7,6},{5,7},{3,5},{1,3},{0,1},{10,8},{12,10},{14... | collective-permute-start | bytes 786440 | tf_op jit(solution)/shard_map/ppermute | solution.py:303
  143.5 1.7 %collective-permute-start.33 = (bf16[64,2048]{1,0:T(8,128)(2,1)S(1)}, bf16[64,2048]{1,0:T(8,128)(2,1)S(1)}, u32[]{:S(2)}, u32[]{:S(2)}) collective-permute-start(bf16[64,2048]{1,0:T(8,128)(2,1)S(1)} %add_convert_fusion.2), channel_id=1, source_target_pairs={{2,0},{4,2},{6,4},{7,6},{5,7},{3,5},{1,3},{0,1},{10,8},{12,10},{14... | collective-permute-start | bytes 786440 | tf_op jit(solution)/shard_map/ppermute | solution.py:303
  145.9 4.2 %collective-permute-done.26 = bf16[64,2048]{1,0:T(8,128)(2,1)S(1)} collective-permute-done((bf16[64,2048]{1,0:T(8,128)(2,1)S(1)}, bf16[64,2048]{1,0:T(8,128)(2,1)S(1)}, u32[]{:S(2)}, u32[]{:S(2)}) %collective-permute-start.26) | collective-permute-done | bytes 262176 | tf_op jit(solution)/shard_map/ppermute | solution.py:303
  150.1 4.2 %collective-permute-done.33 = bf16[64,2048]{1,0:T(8,128)(2,1)S(1)} collective-permute-done((bf16[64,2048]{1,0:T(8,128)(2,1)S(1)}, bf16[64,2048]{1,0:T(8,128)(2,1)S(1)}, u32[]{:S(2)}, u32[]{:S(2)}) %collective-permute-start.33) | collective-permute-done | bytes 262176 | tf_op jit(solution)/shard_map/ppermute | solution.py:303
  (110 shorter events, 18.7 us)
Async XLA Ops:
  1.1 10.1 %collective-permute-start.6 = (bf16[64,2048]{1,0:T(8,128)(2,1)S(1)}, bf16[64,2048]{1,0:T(8,128)(2,1)S(1)}, u32[]{:S(2)}, u32[]{:S(2)}) collective-permute-start(bf16[64,2048]{1,0:T(8,128)(2,1)S(1)} %get-tuple-element.48), channel_id=1, source_target_pairs={{0,2},{2,4},{4,6},{6,7},{7,5},{5,3},{3,1},{1,0},{8,10},{10,12},{12... | collective-permute-start | bytes 786440 | tf_op jit(solution)/shard_map/ppermute | solution.py:256
  4.1 9.2 %collective-permute-start.13 = (bf16[64,2048]{1,0:T(8,128)(2,1)S(1)}, bf16[64,2048]{1,0:T(8,128)(2,1)S(1)}, u32[]{:S(2)}, u32[]{:S(2)}) collective-permute-start(bf16[64,2048]{1,0:T(8,128)(2,1)S(1)} %get-tuple-element.47), channel_id=1, source_target_pairs={{2,0},{4,2},{6,4},{7,6},{5,7},{3,5},{1,3},{0,1},{10,8},{12,10},{14... | collective-permute-start | bytes 786440 | tf_op jit(solution)/shard_map/ppermute | solution.py:259
  4.1 12.7 %collective-permute-start.7 = (bf16[64,2048]{1,0:T(8,128)(2,1)S(1)}, bf16[64,2048]{1,0:T(8,128)(2,1)S(1)}, u32[]{:S(2)}, u32[]{:S(2)}) collective-permute-start(bf16[64,2048]{1,0:T(8,128)(2,1)S(1)} %get-tuple-element.47), channel_id=1, source_target_pairs={{0,2},{2,4},{4,6},{6,7},{7,5},{5,3},{3,1},{1,0},{8,10},{10,12},{12... | collective-permute-start | bytes 786440 | tf_op jit(solution)/shard_map/ppermute | solution.py:256
  6.2 12.8 %collective-permute-start.17 = (bf16[64,2048]{1,0:T(8,128)(2,1)S(1)}, bf16[64,2048]{1,0:T(8,128)(2,1)S(1)}, u32[]{:S(2)}, u32[]{:S(2)}) collective-permute-start(bf16[64,2048]{1,0:T(8,128)(2,1)S(1)} %get-tuple-element.48), channel_id=1, source_target_pairs={{2,0},{4,2},{6,4},{7,6},{5,7},{3,5},{1,3},{0,1},{10,8},{12,10},{14... | collective-permute-start | bytes 786440 | tf_op jit(solution)/shard_map/ppermute | solution.py:259
  6.2 70.8 %collective-permute-start.2 = (bf16[128,2048]{1,0:T(8,128)(2,1)}, bf16[128,2048]{1,0:T(8,128)(2,1)}, u32[]{:S(2)}, u32[]{:S(2)}) collective-permute-start(bf16[128,2048]{1,0:T(8,128)(2,1)} %refs_0_.1), channel_id=1, source_target_pairs={{0,16},{8,24},{16,0},{24,8},{1,17},{9,25},{17,1},{25,9},{2,18},{10... | collective-permute-start | bytes 1572872 | tf_op jit(solution)/shard_map/ppermute | solution.py:280
  11.2 11.2 %collective-permute-start.8 = (bf16[64,2048]{1,0:T(8,128)(2,1)S(1)}, bf16[64,2048]{1,0:T(8,128)(2,1)S(1)}, u32[]{:S(2)}, u32[]{:S(2)}) collective-permute-start(bf16[64,2048]{1,0:T(8,128)(2,1)S(1)} %collective-permute-done.6.refs_1_), channel_id=1, source_target_pairs={{0,2},{2,4},{4,6},{6,7},{7,5},{5,3},{3,1},{1,0},{8,10},{10,12},{12... | collective-permute-start | bytes 786440 | tf_op jit(solution)/shard_map/ppermute | solution.py:256
  13.4 11.2 %collective-permute-start.14 = (bf16[64,2048]{1,0:T(8,128)(2,1)S(1)}, bf16[64,2048]{1,0:T(8,128)(2,1)S(1)}, u32[]{:S(2)}, u32[]{:S(2)}) collective-permute-start(bf16[64,2048]{1,0:T(8,128)(2,1)S(1)} %collective-permute-done.13.refs_14_), channel_id=1, source_target_pairs={{2,0},{4,2},{6,4},{7,6},{5,7},{3,5},{1,3},{0,1},{10,8},{12,10},{14... | collective-permute-start | bytes 786440 | tf_op jit(solution)/shard_map/ppermute | solution.py:259
  16.8 11.3 %collective-permute-start.9 = (bf16[64,2048]{1,0:T(8,128)(2,1)S(1)}, bf16[64,2048]{1,0:T(8,128)(2,1)}, u32[]{:S(2)}, u32[]{:S(2)}) collective-permute-start(bf16[64,2048]{1,0:T(8,128)(2,1)S(1)} %collective-permute-done.7.refs_2_), channel_id=1, source_target_pairs={{0,2},{2,4},{4,6},{6,7},{7,5},{5,3},{3,1},{1,0},{8,10},{10,12},{12... | collective-permute-start | bytes 786440 | tf_op jit(solution)/shard_map/ppermute | solution.py:256
  19.0 11.3 %collective-permute-start.18 = (bf16[64,2048]{1,0:T(8,128)(2,1)S(1)}, bf16[64,2048]{1,0:T(8,128)(2,1)}, u32[]{:S(2)}, u32[]{:S(2)}) collective-permute-start(bf16[64,2048]{1,0:T(8,128)(2,1)S(1)} %collective-permute-done.17.refs_13_), channel_id=1, source_target_pairs={{2,0},{4,2},{6,4},{7,6},{5,7},{3,5},{1,3},{0,1},{10,8},{12,10},{14... | collective-permute-start | bytes 786440 | tf_op jit(solution)/shard_map/ppermute | solution.py:259
  22.4 11.3 %collective-permute-start.10 = (bf16[64,2048]{1,0:T(8,128)(2,1)S(1)}, bf16[64,2048]{1,0:T(8,128)(2,1)}, u32[]{:S(2)}, u32[]{:S(2)}) collective-permute-start(bf16[64,2048]{1,0:T(8,128)(2,1)S(1)} %collective-permute-done.8.refs_3_), channel_id=1, source_target_pairs={{0,2},{2,4},{4,6},{6,7},{7,5},{5,3},{3,1},{1,0},{8,10},{10,12},{12... | collective-permute-start | bytes 786440 | tf_op jit(solution)/shard_map/ppermute | solution.py:256
  24.6 11.3 %collective-permute-start.15 = (bf16[64,2048]{1,0:T(8,128)(2,1)S(1)}, bf16[64,2048]{1,0:T(8,128)(2,1)}, u32[]{:S(2)}, u32[]{:S(2)}) collective-permute-start(bf16[64,2048]{1,0:T(8,128)(2,1)S(1)} %collective-permute-done.14.refs_12_), channel_id=1, source_target_pairs={{2,0},{4,2},{6,4},{7,6},{5,7},{3,5},{1,3},{0,1},{10,8},{12,10},{14... | collective-permute-start | bytes 786440 | tf_op jit(solution)/shard_map/ppermute | solution.py:259
  28.2 48.9 %collective-permute-start.11 = (bf16[64,2048]{1,0:T(8,128)(2,1)}, bf16[64,2048]{1,0:T(8,128)(2,1)}, u32[]{:S(2)}, u32[]{:S(2)}) collective-permute-start(bf16[64,2048]{1,0:T(8,128)(2,1)} %collective-permute-done.9.refs_4_), channel_id=1, source_target_pairs={{0,2},{2,4},{4,6},{6,7},{7,5},{5,3},{3,1},{1,0},{8,10},{10,12},{12... | collective-permute-start | bytes 786440 | tf_op jit(solution)/shard_map/ppermute | solution.py:256
  30.3 47.2 %collective-permute-start.19 = (bf16[64,2048]{1,0:T(8,128)(2,1)}, bf16[64,2048]{1,0:T(8,128)(2,1)}, u32[]{:S(2)}, u32[]{:S(2)}) collective-permute-start(bf16[64,2048]{1,0:T(8,128)(2,1)} %collective-permute-done.18.refs_11_), channel_id=1, source_target_pairs={{2,0},{4,2},{6,4},{7,6},{5,7},{3,5},{1,3},{0,1},{10,8},{12,10},{14... | collective-permute-start | bytes 786440 | tf_op jit(solution)/shard_map/ppermute | solution.py:259
  33.8 43.8 %collective-permute-start.12 = (bf16[64,2048]{1,0:T(8,128)(2,1)}, bf16[64,2048]{1,0:T(8,128)(2,1)}, u32[]{:S(2)}, u32[]{:S(2)}) collective-permute-start(bf16[64,2048]{1,0:T(8,128)(2,1)} %collective-permute-done.10.refs_5_), channel_id=1, source_target_pairs={{0,2},{2,4},{4,6},{6,7},{7,5},{5,3},{3,1},{1,0},{8,10},{10,12},{12... | collective-permute-start | bytes 786440 | tf_op jit(solution)/shard_map/ppermute | solution.py:256
  36.0 41.6 %collective-permute-start.16 = (bf16[64,2048]{1,0:T(8,128)(2,1)}, bf16[64,2048]{1,0:T(8,128)(2,1)}, u32[]{:S(2)}, u32[]{:S(2)}) collective-permute-start(bf16[64,2048]{1,0:T(8,128)(2,1)} %collective-permute-done.15.refs_10_), channel_id=1, source_target_pairs={{2,0},{4,2},{6,4},{7,6},{5,7},{3,5},{1,3},{0,1},{10,8},{12,10},{14... | collective-permute-start | bytes 786440 | tf_op jit(solution)/shard_map/ppermute | solution.py:259
  36.6 41.0 %all-to-all-start = ((f32[8,8,128]{2,1,0:T(8,128)}), f32[8,8,128]{2,1,0:T(8,128)S(1)}, u32[]{:S(2)}, u32[]{:S(2)}) async-start(f32[8,8,128]{2,1,0:T(8,128)} %bitcast.20), calls=%async_computation | async-start | bytes 65536 | tf_op jit(solution)/shard_map/all_to_all | solution.py:264
  77.0 28.1 %collective-permute-start = (bf16[128,2048]{1,0:T(8,128)(2,1)S(1)}, bf16[128,2048]{1,0:T(8,128)(2,1)}, u32[]{:S(2)}, u32[]{:S(2)}) collective-permute-start(bf16[128,2048]{1,0:T(8,128)(2,1)S(1)} %copy-done.1), channel_id=1, source_target_pairs={{0,8},{8,0},{16,24},{24,16},{1,9},{9,1},{17,25},{25,17},{2,10},{10... | collective-permute-start | bytes 1572872 | tf_op jit(solution)/shard_map/ppermute | solution.py:280
  77.1 34.5 %collective-permute-start.3 = (bf16[128,2048]{1,0:T(8,128)(2,1)}, bf16[128,2048]{1,0:T(8,128)(2,1)}, u32[]{:S(2)}, u32[]{:S(2)}) collective-permute-start(bf16[128,2048]{1,0:T(8,128)(2,1)} %collective-permute-done.2.first), channel_id=1, source_target_pairs={{0,8},{8,0},{16,24},{24,16},{1,9},{9,1},{17,25},{25,17},{2,10},{10... | collective-permute-start | bytes 1572872 | tf_op jit(solution)/shard_map/ppermute | solution.py:280
  103.0 14.6 %collective-permute-start.27 = (bf16[64,2048]{1,0:T(8,128)(2,1)}, bf16[64,2048]{1,0:T(8,128)(2,1)S(1)}, u32[]{:S(2)}, u32[]{:S(2)}) collective-permute-start(bf16[64,2048]{1,0:T(8,128)(2,1)} %get-tuple-element.38), channel_id=1, source_target_pairs={{0,2},{2,4},{4,6},{6,7},{7,5},{5,3},{3,1},{1,0},{8,10},{10,12},{12... | collective-permute-start | bytes 786440 | tf_op jit(solution)/shard_map/ppermute | solution.py:303
  109.4 35.9 %collective-permute-start.1 = (bf16[128,2048]{1,0:T(8,128)(2,1)S(1)}, bf16[128,2048]{1,0:T(8,128)(2,1)S(1)}, u32[]{:S(2)}, u32[]{:S(2)}) collective-permute-start(bf16[128,2048]{1,0:T(8,128)(2,1)S(1)} %get-tuple-element.26), channel_id=1, source_target_pairs={{0,8},{8,0},{16,24},{24,16},{1,9},{9,1},{17,25},{25,17},{2,10},{10... | collective-permute-start | bytes 1572872 | tf_op jit(solution)/shard_map/ppermute | solution.py:288
  109.5 9.4 %collective-permute-start.30 = (bf16[64,2048]{1,0:T(8,128)(2,1)}, bf16[64,2048]{1,0:T(8,128)(2,1)S(1)}, u32[]{:S(2)}, u32[]{:S(2)}) collective-permute-start(bf16[64,2048]{1,0:T(8,128)(2,1)} %get-tuple-element.41), channel_id=1, source_target_pairs={{2,0},{4,2},{6,4},{7,6},{5,7},{3,5},{1,3},{0,1},{10,8},{12,10},{14... | collective-permute-start | bytes 786440 | tf_op jit(solution)/shard_map/ppermute | solution.py:303
  111.2 9.9 %collective-permute-start.20 = (bf16[64,2048]{1,0:T(8,128)(2,1)}, bf16[64,2048]{1,0:T(8,128)(2,1)S(1)}, u32[]{:S(2)}, u32[]{:S(2)}) collective-permute-start(bf16[64,2048]{1,0:T(8,128)(2,1)} %get-tuple-element.30), channel_id=1, source_target_pairs={{0,2},{2,4},{4,6},{6,7},{7,5},{5,3},{3,1},{1,0},{8,10},{10,12},{12... | collective-permute-start | bytes 786440 | tf_op jit(solution)/shard_map/ppermute | solution.py:303
  111.6 12.9 %collective-permute-start.24 = (bf16[64,2048]{1,0:T(8,128)(2,1)}, bf16[64,2048]{1,0:T(8,128)(2,1)S(1)}, u32[]{:S(2)}, u32[]{:S(2)}) collective-permute-start(bf16[64,2048]{1,0:T(8,128)(2,1)} %get-tuple-element.34), channel_id=1, source_target_pairs={{2,0},{4,2},{6,4},{7,6},{5,7},{3,5},{1,3},{0,1},{10,8},{12,10},{14... | collective-permute-start | bytes 786440 | tf_op jit(solution)/shard_map/ppermute | solution.py:303
  117.6 9.0 %collective-permute-start.4 = (bf16[128,2048]{1,0:T(8,128)(2,1)S(1)}, bf16[128,2048]{1,0:T(8,128)(2,1)S(1)}, u32[]{:S(2)}, u32[]{:S(2)}) collective-permute-start(bf16[128,2048]{1,0:T(8,128)(2,1)S(1)} %get-tuple-element.28), channel_id=1, source_target_pairs={{0,8},{8,0},{16,24},{24,16},{1,9},{9,1},{17,25},{25,17},{2,10},{10... | collective-permute-start | bytes 1572872 | tf_op jit(solution)/shard_map/ppermute | solution.py:288
  121.1 9.3 %collective-permute-start.31 = (bf16[64,2048]{1,0:T(8,128)(2,1)S(1)}, bf16[64,2048]{1,0:T(8,128)(2,1)S(1)}, u32[]{:S(2)}, u32[]{:S(2)}) collective-permute-start(bf16[64,2048]{1,0:T(8,128)(2,1)S(1)} %add_convert_fusion.4), channel_id=1, source_target_pairs={{2,0},{4,2},{6,4},{7,6},{5,7},{3,5},{1,3},{0,1},{10,8},{12,10},{14... | collective-permute-start | bytes 786440 | tf_op jit(solution)/shard_map/ppermute | solution.py:303
  124.5 8.3 %collective-permute-start.21 = (bf16[64,2048]{1,0:T(8,128)(2,1)S(1)}, bf16[64,2048]{1,0:T(8,128)(2,1)S(1)}, u32[]{:S(2)}, u32[]{:S(2)}) collective-permute-start(bf16[64,2048]{1,0:T(8,128)(2,1)S(1)} %add_convert_fusion.11), channel_id=1, source_target_pairs={{0,2},{2,4},{4,6},{6,7},{7,5},{5,3},{3,1},{1,0},{8,10},{10,12},{12... | collective-permute-start | bytes 786440 | tf_op jit(solution)/shard_map/ppermute | solution.py:303
  126.7 9.3 %collective-permute-start.25 = (bf16[64,2048]{1,0:T(8,128)(2,1)S(1)}, bf16[64,2048]{1,0:T(8,128)(2,1)S(1)}, u32[]{:S(2)}, u32[]{:S(2)}) collective-permute-start(bf16[64,2048]{1,0:T(8,128)(2,1)S(1)} %add_convert_fusion.8), channel_id=1, source_target_pairs={{2,0},{4,2},{6,4},{7,6},{5,7},{3,5},{1,3},{0,1},{10,8},{12,10},{14... | collective-permute-start | bytes 786440 | tf_op jit(solution)/shard_map/ppermute | solution.py:303
  127.0 18.7 %collective-permute-start.5 = (bf16[128,2048]{1,0:T(8,128)(2,1)S(1)}, bf16[128,2048]{1,0:T(8,128)(2,1)S(1)}, u32[]{:S(2)}, u32[]{:S(2)}) collective-permute-start(bf16[128,2048]{1,0:T(8,128)(2,1)S(1)} %add_convert_fusion), channel_id=1, source_target_pairs={{0,16},{8,24},{16,0},{24,8},{1,17},{9,25},{17,1},{25,9},{2,18},{10... | collective-permute-start | bytes 1572872 | tf_op jit(solution)/shard_map/ppermute | solution.py:288
  130.4 15.5 %collective-permute-start.29 = (bf16[64,2048]{1,0:T(8,128)(2,1)S(1)}, bf16[64,2048]{1,0:T(8,128)(2,1)S(1)}, u32[]{:S(2)}, u32[]{:S(2)}) collective-permute-start(bf16[64,2048]{1,0:T(8,128)(2,1)S(1)} %add_convert_fusion.5), channel_id=1, source_target_pairs={{0,2},{2,4},{4,6},{6,7},{7,5},{5,3},{3,1},{1,0},{8,10},{10,12},{12... | collective-permute-start | bytes 786440 | tf_op jit(solution)/shard_map/ppermute | solution.py:303
  140.9 9.2 %collective-permute-start.26 = (bf16[64,2048]{1,0:T(8,128)(2,1)S(1)}, bf16[64,2048]{1,0:T(8,128)(2,1)S(1)}, u32[]{:S(2)}, u32[]{:S(2)}) collective-permute-start(bf16[64,2048]{1,0:T(8,128)(2,1)S(1)} %add_convert_fusion.7), channel_id=1, source_target_pairs={{2,0},{4,2},{6,4},{7,6},{5,7},{3,5},{1,3},{0,1},{10,8},{12,10},{14... | collective-permute-start | bytes 786440 | tf_op jit(solution)/shard_map/ppermute | solution.py:303
  143.5 10.8 %collective-permute-start.33 = (bf16[64,2048]{1,0:T(8,128)(2,1)S(1)}, bf16[64,2048]{1,0:T(8,128)(2,1)S(1)}, u32[]{:S(2)}, u32[]{:S(2)}) collective-permute-start(bf16[64,2048]{1,0:T(8,128)(2,1)S(1)} %add_convert_fusion.2), channel_id=1, source_target_pairs={{2,0},{4,2},{6,4},{7,6},{5,7},{3,5},{1,3},{0,1},{10,8},{12,10},{14... | collective-permute-start | bytes 786440 | tf_op jit(solution)/shard_map/ppermute | solution.py:303
  145.4 9.0 %collective-permute-start.23 = (bf16[64,2048]{1,0:T(8,128)(2,1)S(1)}, bf16[64,2048]{1,0:T(8,128)(2,1)S(1)}, u32[]{:S(2)}, u32[]{:S(2)}) collective-permute-start(bf16[64,2048]{1,0:T(8,128)(2,1)S(1)} %add_convert_fusion.9), channel_id=1, source_target_pairs={{0,2},{2,4},{4,6},{6,7},{7,5},{5,3},{3,1},{1,0},{8,10},{10,12},{12... | collective-permute-start | bytes 786440 | tf_op jit(solution)/shard_map/ppermute | solution.py:303
  (25 other events, 557.6 us)

commit v2 on v1

v2 whole, which is shorter than its diff:
```python
import functools

import jax
import jax.numpy as jnp
from jax import lax
from jax.experimental import pallas as pl
from jax.experimental.pallas import tpu as pltpu
from jax.sharding import PartitionSpec as P

HOT_SLOTS = 40
SLOTS = 24
EXTRA = HOT_SLOTS - SLOTS
BF16 = jnp.bfloat16
F32 = jnp.float32
HBM = pl.BlockSpec(memory_space=pltpu.HBM)
VMEM = pl.BlockSpec(memory_space=pltpu.VMEM)
SMEM = pl.BlockSpec(memory_space=pltpu.SMEM)


def ring_of(count):
    return list(range(0, count, 2)) + list(range(count - 1, 0, -2))


def offsets_of(count):
    order = [0, count // 2]
    for hop in range(1, count // 2):
        order += [hop, count - hop]
    return order


def dot(a, b):
    return jnp.dot(a, b, preferred_element_type=F32)


def dot_t(a, b):
    return lax.dot_general(a, b, (((1,), (1,)), ((), ())), preferred_element_type=F32)


def dot_l(a, b):
    return lax.dot_general(a, b, (((0,), (0,)), ((), ())), preferred_element_type=F32)


def routing(expert_ids, gate_weights, capacity, hot_expert, experts):
    tokens, top = expert_ids.shape
    ids, gates = expert_ids.T, gate_weights.T
    labels = jnp.arange(experts, dtype=jnp.int32)[:, None]
    chosen = jnp.zeros((experts, tokens), jnp.bool_)
    weight = jnp.zeros((experts, tokens), F32)
    for k in range(top):
        here = ids[k][None, :] == labels
        chosen = chosen | here
        weight = weight + jnp.where(here, gates[k][None, :], 0.0)
    place = jnp.arange(tokens, dtype=jnp.int32)
    earlier = (place[:, None] < place[None, :]).astype(BF16)
    rank = dot(chosen.astype(BF16), earlier)
    limit = jnp.where(labels == hot_expert[0], HOT_SLOTS, capacity[0][:, None]).astype(F32)
    kept = chosen & (rank < limit)
    return jnp.stack([jnp.where(kept, rank, -1.0), jnp.where(kept, weight, 0.0)], axis=1)


def experts_kernel(offsets, groups, sizes, fetch, chained, final, idx, meta, *refs):
    refs = list(refs)
    units = [[refs.pop(0) for _ in range(size)] for size in sizes]
    held = [[refs.pop(0) for _ in range(3)] for _ in groups]
    before = [refs.pop(0) for _ in range(2)] if chained else None
    if final:
        outs = [[refs.pop(0) for _ in range(2)] for _ in offsets]
    else:
        sel, eo = refs.pop(0), refs.pop(0)
    if fetch:
        source, held = held[0], [[refs.pop(0) for _ in range(3)]]
    if final:
        sel, eo = refs.pop(0), refs.pop(0)
    x, rows, scale, sem_x, sem_o, sem_w = refs
    experts = [e for group in groups for e in group]

    def fetching(i, k):
        return pltpu.make_async_copy(source[k].at[experts[0] + i], held[0][k].at[i], sem_w.at[i, k])

    pairs = len(offsets) // 2
    width = x.shape[2]
    wide, wide_x = 2 * SLOTS, 2 * EXTRA
    base = pairs * wide
    full = pairs * (wide + wide_x)
    many = len(experts)
    hot = idx[idx.shape[0] - 1]

    loads = []
    for slot, mine in enumerate(units):
        for h, unit in enumerate(mine):
            length = unit.shape[0]
            copy = pltpu.make_async_copy(unit, x.at[slot, pl.ds(h * length, length)], sem_x.at[slot, h])
            copy.start()
            loads.append(copy)
    if fetch:
        for i in range(len(experts)):
            for k in range(3):
                fetching(i, k).start()

    lane = lax.broadcasted_iota(jnp.int32, (1, 256), 1)
    second = (lane >= 128).astype(F32)
    for p in range(pairs):
        info = [meta[idx[offsets[2 * p + i]]] for i in range(2)]
        blocks = []
        for i, e in enumerate(experts):
            rank = jnp.concatenate([info[0][2 * e : 2 * e + 1], info[1][2 * e : 2 * e + 1]], axis=1)
            gate = jnp.concatenate([info[0][2 * e + 1 : 2 * e + 2], info[1][2 * e + 1 : 2 * e + 2]], axis=1)
            key = jnp.where((rank >= 0) & (rank < SLOTS), rank + SLOTS * second, -1.0).astype(jnp.int32)
            pick = (lax.broadcasted_iota(jnp.int32, (wide, 256), 0) == key).astype(F32)
            blocks.append(pick)
            scale[i, pl.ds(p * wide, wide), :] = jnp.broadcast_to(
                jnp.sum(pick * gate, axis=1, keepdims=True), (wide, 128)
            )
            key_x = jnp.where((rank >= SLOTS) & (hot == e), rank - SLOTS + EXTRA * second, -1.0)
            pick_x = (lax.broadcasted_iota(jnp.int32, (wide_x, 256), 0) == key_x.astype(jnp.int32)).astype(F32)
            scale[i, pl.ds(base + p * wide_x, wide_x), :] = jnp.broadcast_to(
                jnp.sum(pick_x * gate, axis=1, keepdims=True), (wide_x, 128)
            )
            extra = pick_x if i == 0 else extra + pick_x
        blocks.append(extra)
        sel[p] = jnp.concatenate(blocks, axis=0).astype(BF16)
        eo[p, pl.ds(many * wide, wide_x), :] = jnp.zeros((wide_x, width), BF16)

    for copy in loads:
        copy.wait()
    for p in range(pairs):
        pair = x[2 * p : 2 * p + 2].reshape(256, width)
        got = dot(sel[p], pair).astype(BF16)
        for i, e in enumerate(experts):
            rows[i, pl.ds(p * wide, wide), :] = got[i * wide : (i + 1) * wide]

            @pl.when(hot == e)
            def _():
                rows[i, pl.ds(base + p * wide_x, wide_x), :] = got[many * wide :]

    def run(at, group, inside, length):
        wg, wu, wd = held[group]
        tokens = rows[at, :length]
        gate = dot_t(tokens, wg[inside])
        upper = dot_t(tokens, wu[inside])
        hidden = (gate / (1.0 + jnp.exp(-gate)) * upper * scale[at, :length][:, :1]).astype(BF16)
        if fetch:
            fetching(inside, 2).wait()
        out = dot(hidden, wd[inside]).astype(BF16)
        for p in range(pairs):
            eo[p, pl.ds(pl.multiple_of(at * wide, wide), wide), :] = out[p * wide : (p + 1) * wide]
            if length > base:
                eo[p, pl.ds(many * wide, wide_x), :] = out[base + p * wide_x : base + (p + 1) * wide_x]

    done = 0
    for group, members in enumerate(groups):

        def body(inside, carry):
            if fetch:
                fetching(inside, 0).wait()
                fetching(inside, 1).wait()

            @pl.when(hot == members[0] + inside)
            def _():
                run(done + inside, group, inside, full)

            @pl.when(hot != members[0] + inside)
            def _():
                run(done + inside, group, inside, base)

            return carry

        lax.fori_loop(0, len(members), body, 0)
        done += len(members)

    if not final:
        return
    stores = []
    for p in range(pairs):
        total = dot_l(sel[p], eo[p])
        if chained:
            total = total + dot_l(before[0][p], before[1][p])
        x[2 * p : 2 * p + 2] = total.astype(BF16).reshape(2, 128, width)
        for slot in (2 * p, 2 * p + 1):
            for h in range(2):
                copy = pltpu.make_async_copy(x.at[slot, pl.ds(h * 64, 64)], outs[slot][h], sem_o.at[slot, h])
                copy.start()
                stores.append(copy)
    for copy in stores:
        copy.wait()


def run_experts(offsets, groups, idx, meta, blocks, weights, fetch=False, before=None, final=True):
    hidden, width = weights[0][2].shape[1:]
    wide, wide_x = 2 * SLOTS, 2 * EXTRA
    pairs = len(offsets) // 2
    many = sum(len(group) for group in groups)
    high = many * wide + wide_x
    full = pairs * (wide + wide_x)
    flat = [unit for o in offsets for unit in blocks[o]]
    sizes = tuple(len(blocks[o]) for o in offsets)
    chain = [((pairs, high, 256), BF16), ((pairs, high, width), BF16)]
    scratch = [
        pltpu.VMEM((len(offsets), 128, width), BF16),
        pltpu.VMEM((many, full, width), BF16),
        pltpu.VMEM((many, full, 128), F32),
        pltpu.SemaphoreType.DMA((len(offsets), 2)),
        pltpu.SemaphoreType.DMA((len(offsets), 2)),
        pltpu.SemaphoreType.DMA((many, 3)),
    ]
    if final:
        out_shape = [pltpu.HBM((64, width), BF16)] * (2 * len(offsets))
        out_specs = [HBM] * (2 * len(offsets))
        scratch = [pltpu.VMEM(*c) for c in chain] + scratch
    else:
        out_shape = [pltpu.VMEM(*c) for c in chain]
        out_specs = [VMEM] * 2
    if fetch:
        out_shape = out_shape + [pltpu.VMEM((many, hidden, width), BF16)] * 3
        out_specs = out_specs + [VMEM] * 3
    flat = [pltpu.with_memory_space_constraint(unit, pltpu.HBM) for unit in flat]
    room = len(offsets) * 128 * width * 2 + many * full * (2 * width + 512) + pairs * high * (2 * width + 512)
    room += full * (6 * width + 10 * hidden)
    before = list(before or ())
    held = [w for group in weights for w in group]
    held = [pltpu.with_memory_space_constraint(w, pltpu.HBM if fetch else pltpu.VMEM) for w in held]
    before = [pltpu.with_memory_space_constraint(w, pltpu.VMEM) for w in before]
    flops = 2 * 3 * width * hidden * many * pairs * wide + 4 * len(offsets) * 128 * high * width
    return pl.pallas_call(
        functools.partial(experts_kernel, offsets, groups, sizes, fetch, bool(before), final),
        out_shape=out_shape,
        in_specs=[SMEM, VMEM] + [HBM] * len(flat) + [HBM if fetch else VMEM] * len(held) + [VMEM] * len(before),
        out_specs=out_specs,
        scratch_shapes=scratch,
        cost_estimate=pl.CostEstimate(
            flops=flops,
            transcendentals=many * pairs * wide * hidden,
            bytes_accessed=2 * (2 * len(offsets) * 128 * width + (3 * many * hidden * width if fetch else 0)),
        ),
        compiler_params=pltpu.CompilerParams(vmem_limit_bytes=room),
        name="routed_experts",
    )(idx, meta, *flat, *held, *before)


def shared_kernel(first, second, w_gate, w_up, w_down, out_first, out_second):
    tokens = jnp.concatenate([first[...], second[...]], axis=0)
    gate = dot(tokens, w_gate[...])
    upper = dot(tokens, w_up[...])
    hidden = (gate / (1.0 + jnp.exp(-gate)) * upper).astype(BF16)
    out = dot(hidden, w_down[...]).astype(BF16)
    rows = first.shape[0]
    out_first[...] = out[:rows]
    out_second[...] = out[rows:]


def run_shared(first, second, w_gate, w_up, w_down):
    rows, width = first.shape
    hidden = w_gate.shape[1]
    return pl.pallas_call(
        shared_kernel,
        out_shape=[jax.ShapeDtypeStruct((rows, width), BF16)] * 2,
        in_specs=[VMEM] * 5,
        out_specs=[VMEM] * 2,
        cost_estimate=pl.CostEstimate(
            flops=2 * 3 * 2 * rows * width * hidden,
            transcendentals=2 * rows * hidden,
            bytes_accessed=2 * (3 * width * hidden + 4 * rows * width),
        ),
        compiler_params=pltpu.CompilerParams(vmem_limit_bytes=48 << 20),
        name="shared_experts",
    )(first, second, w_gate, w_up, w_down)


def on_device(
    latents,
    expert_ids,
    gate_weights,
    capacity,
    hot_expert,
    w_gate,
    w_up,
    w_down,
    shared_gate,
    shared_up,
    shared_down,
):
    tokens, width = latents.shape
    half = tokens // 2
    experts = capacity.shape[1]
    local = w_gate.shape[0]
    count = lax.axis_size("expert")
    n_dp = lax.axis_size("dp")
    ring = ring_of(count)
    forward = [(ring[i], ring[(i + 1) % count]) for i in range(count)]
    backward = [(b, a) for a, b in forward]
    mid = count // 2

    own = [latents[:half], latents[half:]]
    blocks = {o: [None, None] for o in range(count)}
    for h in range(2):
        up, down = own[h], own[h]
        for hop in range(1, mid + 1):
            if hop < mid or h == 0:
                up = lax.ppermute(up, "expert", forward)
                blocks[hop][h] = up
            if hop < mid or h == 1:
                down = lax.ppermute(down, "expert", backward)
                blocks[count - hop][h] = down
    blocks[0] = [latents]

    info = routing(expert_ids, gate_weights, capacity, hot_expert, experts)
    meta = lax.all_to_all(
        info.reshape(count, 2 * local, tokens), "expert", split_axis=0, concat_axis=0, tiled=True
    )
    me = lax.axis_index("expert")
    table = []
    for e in range(count):
        at = ring.index(e)
        table.append([ring[(at - o) % count] for o in range(count)])
    idx = jnp.array(table, jnp.int32)[me]
    idx = jnp.concatenate([idx, (hot_expert - me * local).astype(jnp.int32)])

    bits = [1 << b for b in range(n_dp.bit_length() - 1)]
    near = {0: latents}
    for bit in reversed(bits):
        swap = [(d, d ^ bit) for d in range(n_dp)]
        for r in list(near):
            near[r ^ bit] = lax.ppermute(near[r], "dp", swap)
    part = {}
    for r in range(0, n_dp, 2):
        part[r], part[r + 1] = run_shared(near[r], near[r + 1], shared_gate, shared_up, shared_down)
    for bit in bits:
        swap = [(d, d ^ bit) for d in range(n_dp)]
        for r in sorted(part):
            if r & bit:
                came = lax.ppermute(part.pop(r), "dp", swap)
                total = part[r ^ bit].astype(F32) + came.astype(F32)
                part[r ^ bit] = total if len(bits) and bit == bits[-1] else total.astype(BF16)
    shared = part[0]

    weights = [jnp.swapaxes(w_gate, 1, 2), jnp.swapaxes(w_up, 1, 2), w_down]
    order = offsets_of(count)
    early, late = tuple(order[2:-2]), tuple(order[-2:] + order[:2])
    some = (local + 1) // 2
    groups = [g for g in (tuple(range(some)), tuple(range(some, local))) if g]
    held, chain = [], None
    for i, group in enumerate(groups):
        last = i == len(groups) - 1
        got = list(
            run_experts(early, [group], idx, meta, blocks, [weights], fetch=True, before=chain, final=last)
        )
        held.append(got[-3:])
        chain = flat = got[:-3]
    flat = flat + list(run_experts(late, groups, idx, meta, blocks, held))
    done = {}
    for i, o in enumerate(early + late):
        done[o] = [flat[2 * i], flat[2 * i + 1]]

    result = []
    for h in range(2):
        pieces = [done[0][h]]
        for step, perm, long in ((-1, forward, h == 0), (1, backward, h == 1)):
            start = mid if long else mid - 1
            acc = done[(step * start) % count][h]
            for k in range(start, 0, -1):
                came = lax.ppermute(acc, "expert", perm)
                if k > 1:
                    acc = (came.astype(F32) + done[(step * (k - 1)) % count][h].astype(F32)).astype(BF16)
            pieces.append(came)
        total = shared[h * half : (h + 1) * half].astype(F32)
        for piece in pieces:
            total = total + piece.astype(F32)
        result.append(total.astype(BF16))
    return jnp.concatenate(result, axis=0)


def solution(mesh):
    placed = (
        P(("dp", "expert"), None),
        P(("dp", "expert"), None),
        P(("dp", "expert"), None),
        P("dp", None),
        P("dp"),
        P("expert", None, None),
        P("expert", None, None),
        P("expert", None, None),
        P(None, "dp"),
        P(None, "dp"),
        P("dp", None),
    )
    return jax.shard_map(
        on_device, mesh=mesh, in_specs=placed, out_specs=P(("dp", "expert"), None), check_vma=False
    )
```

time: 157 us -> 138 us (0.88)
  local copies, waits for them, and re-layouts: 37.6 us -> 7.56 us
  Pallas kernels: 33.4 us -> 51.7 us
  starting transfers between devices: 46.2 us -> 40.4 us
    unnamed x46 -> x62, local copies, waits for them, and re-layouts: 33.4 us -> 3.34 us
    pallas_call x1 -> x3, Pallas kernels: 24.8 us -> 43.4 us  [run_experts(): pl.pallas_call(functools.partial(experts_kernel, offsets, groups, sizes,...]
    ppermute x7, waiting for transfers between devices: 13.6 us -> 7.13 us  [on_device(): up = lax.ppermute(up, 'expert', forward)]
    ppermute x14, starting transfers between devices: 20 us -> 15.4 us  [on_device(): came = lax.ppermute(acc, 'expert', perm)]
    ppermute x7, starting transfers between devices: 15.8 us -> 12.4 us  [on_device(): up = lax.ppermute(up, 'expert', forward)]
    ppermute x7, starting transfers between devices: 0.04 us -> 2.75 us  [on_device(): down = lax.ppermute(down, 'expert', backward)]
    ppermute x7, waiting for transfers between devices: 0.18 us -> 2.77 us  [on_device(): down = lax.ppermute(down, 'expert', backward)]
    ppermute x14, waiting for transfers between devices: 19.8 us -> 22 us  [on_device(): came = lax.ppermute(acc, 'expert', perm)]
  transfers between devices with their start and end apart: 35 -> 35, of which waited for: 15 -> 14; matrix products, arithmetic and copies ran while one was open for 25% -> 4% of each run, Pallas kernels for 21% -> 38%
where the time goes in v2:
time: 138 us
  Pallas kernels  51.7 us (37%)
  starting transfers between devices  40.4 us (29%)
  waiting for transfers between devices  33.9 us (25%)
  local copies, waits for them, and re-layouts  7.56 us (5%)
  other arithmetic  2.87 us (2%)
    pallas_call x3, Pallas kernels, run_experts(): pl.pallas_call(functools.partial(experts_kernel, offsets, groups, sizes,...  43.4 us
    ppermute x14, waiting for transfers between devices, on_device(): came = lax.ppermute(acc, 'expert', perm)  22 us
    ppermute x14, starting transfers between devices, on_device(): came = lax.ppermute(acc, 'expert', perm)  15.4 us
    ppermute x7, starting transfers between devices, on_device(): up = lax.ppermute(up, 'expert', forward)  12.4 us
    pallas_call x2, Pallas kernels, run_shared(): pl.pallas_call(shared_kernel, out_shape=[jax.ShapeDtypeStruct((rows, widt...  8.22 us
    ppermute x7, waiting for transfers between devices, on_device(): up = lax.ppermute(up, 'expert', forward)  7.13 us
    all_to_all x1, starting transfers between devices, on_device(): lax.all_to_all(info.reshape(count, 2 * local, tokens), 'expert', split_ax...  6.06 us
    unnamed x62, local copies, waits for them, and re-layouts  3.34 us
  transfers between devices with their start and end apart: 35, of which 14 were waited for; matrix products, arithmetic and copies ran while one was open for 4% of the time, Pallas kernels for 38%

profile of v2, /device:TPU:0, one launch (start us, length us, event | category | flops | bytes accessed | tf_op | source)
XLA Modules:
  0.0 137.7 jit_solution(13799148599635944049)
XLA Ops:
  1.1 3.1 %collective-permute-start.9 = (bf16[64,2048]{1,0:T(8,128)(2,1)S(1)}, bf16[64,2048]{1,0:T(8,128)(2,1)S(1)}, u32[]{:S(2)}, u32[]{:S(2)}) collective-permute-start(bf16[64,2048]{1,0:T(8,128)(2,1)S(1)} %get-tuple-element.63), channel_id=1, source_target_pairs={{0,2},{2,4},{4,6},{6,7},{7,5},{5,3},{3,1},{1,0},{8,10},{10,12},{12... | collective-permute-start | bytes 786440 | tf_op jit(solution)/shard_map/ppermute | solution.py:299
  4.1 1.9 %collective-permute-start.12 = (bf16[64,2048]{1,0:T(8,128)(2,1)S(1)}, bf16[64,2048]{1,0:T(8,128)(2,1)S(1)}, u32[]{:S(2)}, u32[]{:S(2)}) collective-permute-start(bf16[64,2048]{1,0:T(8,128)(2,1)S(1)} %get-tuple-element.64), channel_id=1, source_target_pairs={{2,0},{4,2},{6,4},{7,6},{5,7},{3,5},{1,3},{0,1},{10,8},{12,10},{14... | collective-permute-start | bytes 786440 | tf_op jit(solution)/shard_map/ppermute | solution.py:302
  6.2 1.9 %collective-permute-start.2 = (bf16[128,2048]{1,0:T(8,128)(2,1)}, bf16[128,2048]{1,0:T(8,128)(2,1)S(1)}, u32[]{:S(2)}, u32[]{:S(2)}) collective-permute-start(bf16[128,2048]{1,0:T(8,128)(2,1)} %refs_4_.1), channel_id=1, source_target_pairs={{0,16},{8,24},{16,0},{24,8},{1,17},{9,25},{17,1},{25,9},{2,18},{10... | collective-permute-start | bytes 1572872 | tf_op jit(solution)/shard_map/ppermute | solution.py:323
  10.6 2.8 %collective-permute-done.15.refs_3_ = bf16[64,2048]{1,0:T(8,128)(2,1)S(1)} collective-permute-done((bf16[64,2048]{1,0:T(8,128)(2,1)S(1)}, bf16[64,2048]{1,0:T(8,128)(2,1)S(1)}, u32[]{:S(2)}, u32[]{:S(2)}) %collective-permute-start.15) | collective-permute-done | bytes 262176 | tf_op jit(solution)/shard_map/ppermute | solution.py:302
  13.4 2.6 %collective-permute-done.6.refs_0_ = bf16[64,2048]{1,0:T(8,128)(2,1)S(1)} collective-permute-done((bf16[64,2048]{1,0:T(8,128)(2,1)S(1)}, bf16[64,2048]{1,0:T(8,128)(2,1)S(1)}, u32[]{:S(2)}, u32[]{:S(2)}) %collective-permute-start.6) | collective-permute-done | bytes 262176 | tf_op jit(solution)/shard_map/ppermute | solution.py:299
  16.0 1.8 %collective-permute-start.7 = (bf16[64,2048]{1,0:T(8,128)(2,1)S(1)}, bf16[64,2048]{1,0:T(8,128)(2,1)S(1)}, u32[]{:S(2)}, u32[]{:S(2)}) collective-permute-start(bf16[64,2048]{1,0:T(8,128)(2,1)S(1)} %collective-permute-done.6.refs_0_), channel_id=1, source_target_pairs={{0,2},{2,4},{4,6},{6,7},{7,5},{5,3},{3,1},{1,0},{8,10},{10,12},{12... | collective-permute-start | bytes 786440 | tf_op jit(solution)/shard_map/ppermute | solution.py:299
  18.6 1.6 %collective-permute-start.10 = (bf16[64,2048]{1,0:T(8,128)(2,1)S(1)}, bf16[64,2048]{1,0:T(8,128)(2,1)S(1)}, u32[]{:S(2)}, u32[]{:S(2)}) collective-permute-start(bf16[64,2048]{1,0:T(8,128)(2,1)S(1)} %collective-permute-done.9.refs_1_), channel_id=1, source_target_pairs={{0,2},{2,4},{4,6},{6,7},{7,5},{5,3},{3,1},{1,0},{8,10},{10,12},{12... | collective-permute-start | bytes 786440 | tf_op jit(solution)/shard_map/ppermute | solution.py:299
  20.7 4.5 %collective-permute-done.7.refs_4_ = bf16[64,2048]{1,0:T(8,128)(2,1)S(1)} collective-permute-done((bf16[64,2048]{1,0:T(8,128)(2,1)S(1)}, bf16[64,2048]{1,0:T(8,128)(2,1)S(1)}, u32[]{:S(2)}, u32[]{:S(2)}) %collective-permute-start.7) | collective-permute-done | bytes 262176 | tf_op jit(solution)/shard_map/ppermute | solution.py:299
  25.2 1.8 %collective-permute-start.8 = (bf16[64,2048]{1,0:T(8,128)(2,1)S(1)}, bf16[64,2048]{1,0:T(8,128)(2,1)S(1)}, u32[]{:S(2)}, u32[]{:S(2)}) collective-permute-start(bf16[64,2048]{1,0:T(8,128)(2,1)S(1)} %collective-permute-done.7.refs_4_), channel_id=1, source_target_pairs={{0,2},{2,4},{4,6},{6,7},{7,5},{5,3},{3,1},{1,0},{8,10},{10,12},{12... | collective-permute-start | bytes 786440 | tf_op jit(solution)/shard_map/ppermute | solution.py:299
  27.9 6.1 %all-to-all-start = ((f32[8,8,128]{2,1,0:T(8,128)}), f32[8,8,128]{2,1,0:T(8,128)S(1)}, u32[]{:S(2)}, u32[]{:S(2)}) async-start(f32[8,8,128]{2,1,0:T(8,128)} %bitcast.20), calls=%async_computation | async-start | bytes 65536 | tf_op jit(solution)/shard_map/all_to_all | solution.py:307
  34.7 2.0 %collective-permute-start.11 = (bf16[64,2048]{1,0:T(8,128)(2,1)S(1)}, bf16[64,2048]{1,0:T(8,128)(2,1)S(1)}, u32[]{:S(2)}, u32[]{:S(2)}) collective-permute-start(bf16[64,2048]{1,0:T(8,128)(2,1)S(1)} %collective-permute-done.10.refs_5_), channel_id=1, source_target_pairs={{0,2},{2,4},{4,6},{6,7},{7,5},{5,3},{3,1},{1,0},{8,10},{10,12},{12... | collective-permute-start | bytes 786440 | tf_op jit(solution)/shard_map/ppermute | solution.py:299
  36.8 1.9 %collective-permute-start.18 = (bf16[64,2048]{1,0:T(8,128)(2,1)S(1)}, bf16[64,2048]{1,0:T(8,128)(2,1)}, u32[]{:S(2)}, u32[]{:S(2)}) collective-permute-start(bf16[64,2048]{1,0:T(8,128)(2,1)S(1)} %collective-permute-done.8.refs_0_), channel_id=1, source_target_pairs={{0,2},{2,4},{4,6},{6,7},{7,5},{5,3},{3,1},{1,0},{8,10},{10,12},{12... | collective-permute-start | bytes 786440 | tf_op jit(solution)/shard_map/ppermute | solution.py:299
  38.9 2.1 %all-to-all-done.meta = f32[8,8,128]{2,1,0:T(8,128)S(1)} async-done(((f32[8,8,128]{2,1,0:T(8,128)}), f32[8,8,128]{2,1,0:T(8,128)S(1)}, u32[]{:S(2)}, u32[]{:S(2)}) %all-to-all-start) | async-done | bytes 32800 | tf_op jit(solution)/shard_map/all_to_all | solution.py:307
  41.0 11.9 %routed_experts.3 = (bf16[2,128,256]{2,1,0:T(8,128)(2,1)S(1)}, bf16[2,128,2048]{2,1,0:T(8,128)(2,1)S(1)}, bf16[2,704,2048]{2,1,0:T(8,128)(2,1)S(1)}, bf16[2,704,...) custom-call(s32[9]{0:T(128)S(1)} %pad_add_fusion.idx, f32[8,8,128]{2,1,0:T(8,128)S(1)} %all-to-all-done.meta, ...), custom_call_target="tpu_custom_call" | custom-call | flops 2197815296 | bytes 21495808 | tf_op jit(solution)/shard_map/routed_experts/pallas_call | solution.py:224
  53.1 16.6 %routed_experts.4 = (bf16[64,2048]{1,0:T(8,128)(2,1)}, bf16[64,2048]{1,0:T(8,128)(2,1)}, bf16[64,2048]{1,0:T(8,128)(2,1)}, bf16[64,2048]{1,0:T(8,128)(2,1)}, bf1...) custom-call(s32[9]{0:T(128)S(1)} %pad_add_fusion.idx, ...), custom_call_target="tpu_custom_call" | custom-call | flops 2197815296 | bytes 21495808 | tf_op jit(solution)/shard_map/routed_experts/pallas_call | solution.py:224
  70.5 2.6 %copy-done.2 = bf16[2,704,2048]{2,1,0:T(8,128)(2,1)S(1)} copy-done((bf16[2,704,2048]{2,1,0:T(8,128)(2,1)S(1)}, bf16[2,704,2048]{2,1,0:T(8,128)(2,1)}, u32[]{:S(2)}) %copy-start.2) | copy-done | bytes 5767192
  73.1 14.9 %routed_experts.5 = (bf16[64,2048]{1,0:T(8,128)(2,1)}, bf16[64,2048]{1,0:T(8,128)(2,1)}, bf16[64,2048]{1,0:T(8,128)(2,1)}, bf16[64,2048]{1,0:T(8,128)(2,1)}, bf1...) custom-call(s32[9]{0:T(128)S(1)} %pad_add_fusion.idx, ...), custom_call_target="tpu_custom_call" | custom-call | flops 4261412864 | bytes 4194304 | tf_op jit(solution)/shard_map/routed_experts/pallas_call | solution.py:224
  88.3 4.1 %shared_experts.2 = (bf16[128,2048]{1,0:T(8,128)(2,1)S(1)}, bf16[128,2048]{1,0:T(8,128)(2,1)S(1)}) custom-call(bf16[128,2048]{1,0:T(8,128)(2,1)S(1)} %copy-done.4, bf16[128,2048]{1,0:T(8,128)(2,1)S(1)} %collective-permute-done.second, bf16[2048,512]{1,0:T(8,128)(2,1)S(1)} %copy-done, bf16[2048,512]{1,0:T(8,128)(2,1)} %w_up.3, bf16[512,2048]{1,0:T(8,128)(2,1)} %w_down.3), custom_call_target="tpu_custom_call" | custom-call | flops 1610612736 | bytes 8388608 | tf_op jit(solution)/shard_map/shared_experts/pallas_call | solution.py:254
  92.5 1.8 %collective-permute-start.30 = (bf16[64,2048]{1,0:T(8,128)(2,1)S(1)}, bf16[64,2048]{1,0:T(8,128)(2,1)S(1)}, u32[]{:S(2)}, u32[]{:S(2)}) collective-permute-start(bf16[64,2048]{1,0:T(8,128)(2,1)S(1)} %copy-done.30), channel_id=1, source_target_pairs={{2,0},{4,2},{6,4},{7,6},{5,7},{3,5},{1,3},{0,1},{10,8},{12,10},{14... | collective-permute-start | bytes 786440 | tf_op jit(solution)/shard_map/ppermute | solution.py:361
  94.7 1.8 %collective-permute-start.24 = (bf16[64,2048]{1,0:T(8,128)(2,1)S(1)}, bf16[64,2048]{1,0:T(8,128)(2,1)S(1)}, u32[]{:S(2)}, u32[]{:S(2)}) collective-permute-start(bf16[64,2048]{1,0:T(8,128)(2,1)S(1)} %copy-done.28), channel_id=1, source_target_pairs={{2,0},{4,2},{6,4},{7,6},{5,7},{3,5},{1,3},{0,1},{10,8},{12,10},{14... | collective-permute-start | bytes 786440 | tf_op jit(solution)/shard_map/ppermute | solution.py:361
  96.5 4.1 %shared_experts.3 = (bf16[128,2048]{1,0:T(8,128)(2,1)S(1)}, bf16[128,2048]{1,0:T(8,128)(2,1)S(1)}) custom-call(bf16[128,2048]{1,0:T(8,128)(2,1)S(1)} %collective-permute-done.2.first, bf16[128,2048]{1,0:T(8,128)(2,1)S(1)} %collective-permute-done.3.second, bf16[2048,512]{1,0:T(8,128)(2,1)S(1)} %copy-done, bf16[2048,512]{1,0:T(8,128)(2,1)} %w_up.3, ...), custom_call_target="tpu_custom_call" | custom-call | flops 1610612736 | bytes 8388608 | tf_op jit(solution)/shard_map/shared_experts/pallas_call | solution.py:254
  103.9 3.4 %collective-permute-done.24 = bf16[64,2048]{1,0:T(8,128)(2,1)S(1)} collective-permute-done((bf16[64,2048]{1,0:T(8,128)(2,1)S(1)}, bf16[64,2048]{1,0:T(8,128)(2,1)S(1)}, u32[]{:S(2)}, u32[]{:S(2)}) %collective-permute-start.24) | collective-permute-done | bytes 262176 | tf_op jit(solution)/shard_map/ppermute | solution.py:361
  109.9 1.5 %collective-permute-start.5 = (bf16[128,2048]{1,0:T(8,128)(2,1)S(1)}, bf16[128,2048]{1,0:T(8,128)(2,1)S(1)}, u32[]{:S(2)}, u32[]{:S(2)}) collective-permute-start(bf16[128,2048]{1,0:T(8,128)(2,1)S(1)} %add_convert_fusion), channel_id=1, source_target_pairs={{0,16},{8,24},{16,0},{24,8},{1,17},{9,25},{17,1},{25,9},{2,18},{10... | collective-permute-start | bytes 1572872 | tf_op jit(solution)/shard_map/ppermute | solution.py:331
  111.5 1.4 %collective-permute-done.31 = bf16[64,2048]{1,0:T(8,128)(2,1)S(1)} collective-permute-done((bf16[64,2048]{1,0:T(8,128)(2,1)S(1)}, bf16[64,2048]{1,0:T(8,128)(2,1)S(1)}, u32[]{:S(2)}, u32[]{:S(2)}) %collective-permute-start.31) | collective-permute-done | bytes 262176 | tf_op jit(solution)/shard_map/ppermute | solution.py:361
  112.9 1.1 collective-permute-start.29
  114.1 1.4 %collective-permute-done.21 = bf16[64,2048]{1,0:T(8,128)(2,1)S(1)} collective-permute-done((bf16[64,2048]{1,0:T(8,128)(2,1)S(1)}, bf16[64,2048]{1,0:T(8,128)(2,1)S(1)}, u32[]{:S(2)}, u32[]{:S(2)}) %collective-permute-start.21) | collective-permute-done | bytes 262176 | tf_op jit(solution)/shard_map/ppermute | solution.py:361
  116.6 2.0 %collective-permute-done.25 = bf16[64,2048]{1,0:T(8,128)(2,1)S(1)} collective-permute-done((bf16[64,2048]{1,0:T(8,128)(2,1)S(1)}, bf16[64,2048]{1,0:T(8,128)(2,1)S(1)}, u32[]{:S(2)}, u32[]{:S(2)}) %collective-permute-start.25) | collective-permute-done | bytes 262176 | tf_op jit(solution)/shard_map/ppermute | solution.py:361
  119.8 3.9 %collective-permute-done.32 = bf16[64,2048]{1,0:T(8,128)(2,1)S(1)} collective-permute-done((bf16[64,2048]{1,0:T(8,128)(2,1)S(1)}, bf16[64,2048]{1,0:T(8,128)(2,1)S(1)}, u32[]{:S(2)}, u32[]{:S(2)}) %collective-permute-start.32) | collective-permute-done | bytes 262176 | tf_op jit(solution)/shard_map/ppermute | solution.py:361
  123.7 1.8 %collective-permute-start.26 = (bf16[64,2048]{1,0:T(8,128)(2,1)S(1)}, bf16[64,2048]{1,0:T(8,128)(2,1)S(1)}, u32[]{:S(2)}, u32[]{:S(2)}) collective-permute-start(bf16[64,2048]{1,0:T(8,128)(2,1)S(1)} %add_convert_fusion.7), channel_id=1, source_target_pairs={{2,0},{4,2},{6,4},{7,6},{5,7},{3,5},{1,3},{0,1},{10,8},{12,10},{14... | collective-permute-start | bytes 786440 | tf_op jit(solution)/shard_map/ppermute | solution.py:361
  126.4 1.3 collective-permute-start.33
  128.8 4.1 %collective-permute-done.26 = bf16[64,2048]{1,0:T(8,128)(2,1)S(1)} collective-permute-done((bf16[64,2048]{1,0:T(8,128)(2,1)S(1)}, bf16[64,2048]{1,0:T(8,128)(2,1)S(1)}, u32[]{:S(2)}, u32[]{:S(2)}) %collective-permute-start.26) | collective-permute-done | bytes 262176 | tf_op jit(solution)/shard_map/ppermute | solution.py:361
  133.0 3.6 %collective-permute-done.33 = bf16[64,2048]{1,0:T(8,128)(2,1)S(1)} collective-permute-done((bf16[64,2048]{1,0:T(8,128)(2,1)S(1)}, bf16[64,2048]{1,0:T(8,128)(2,1)S(1)}, u32[]{:S(2)}, u32[]{:S(2)}) %collective-permute-start.33) | collective-permute-done | bytes 262176 | tf_op jit(solution)/shard_map/ppermute | solution.py:361
  (128 shorter events, 18.7 us)
Async XLA Ops:
  1.1 17.5 %collective-permute-start.9 = (bf16[64,2048]{1,0:T(8,128)(2,1)S(1)}, bf16[64,2048]{1,0:T(8,128)(2,1)S(1)}, u32[]{:S(2)}, u32[]{:S(2)}) collective-permute-start(bf16[64,2048]{1,0:T(8,128)(2,1)S(1)} %get-tuple-element.63), channel_id=1, source_target_pairs={{0,2},{2,4},{4,6},{6,7},{7,5},{5,3},{3,1},{1,0},{8,10},{10,12},{12... | collective-permute-start | bytes 786440 | tf_op jit(solution)/shard_map/ppermute | solution.py:299
  4.1 9.2 %collective-permute-start.15 = (bf16[64,2048]{1,0:T(8,128)(2,1)S(1)}, bf16[64,2048]{1,0:T(8,128)(2,1)S(1)}, u32[]{:S(2)}, u32[]{:S(2)}) collective-permute-start(bf16[64,2048]{1,0:T(8,128)(2,1)S(1)} %get-tuple-element.63), channel_id=1, source_target_pairs={{2,0},{4,2},{6,4},{7,6},{5,7},{3,5},{1,3},{0,1},{10,8},{12,10},{14... | collective-permute-start | bytes 786440 | tf_op jit(solution)/shard_map/ppermute | solution.py:302
  4.1 16.1 %collective-permute-start.12 = (bf16[64,2048]{1,0:T(8,128)(2,1)S(1)}, bf16[64,2048]{1,0:T(8,128)(2,1)S(1)}, u32[]{:S(2)}, u32[]{:S(2)}) collective-permute-start(bf16[64,2048]{1,0:T(8,128)(2,1)S(1)} %get-tuple-element.64), channel_id=1, source_target_pairs={{2,0},{4,2},{6,4},{7,6},{5,7},{3,5},{1,3},{0,1},{10,8},{12,10},{14... | collective-permute-start | bytes 786440 | tf_op jit(solution)/shard_map/ppermute | solution.py:302
  6.1 9.9 %collective-permute-start.6 = (bf16[64,2048]{1,0:T(8,128)(2,1)S(1)}, bf16[64,2048]{1,0:T(8,128)(2,1)S(1)}, u32[]{:S(2)}, u32[]{:S(2)}) collective-permute-start(bf16[64,2048]{1,0:T(8,128)(2,1)S(1)} %get-tuple-element.64), channel_id=1, source_target_pairs={{0,2},{2,4},{4,6},{6,7},{7,5},{5,3},{3,1},{1,0},{8,10},{10,12},{12... | collective-permute-start | bytes 786440 | tf_op jit(solution)/shard_map/ppermute | solution.py:299
  6.2 46.8 %collective-permute-start.2 = (bf16[128,2048]{1,0:T(8,128)(2,1)}, bf16[128,2048]{1,0:T(8,128)(2,1)S(1)}, u32[]{:S(2)}, u32[]{:S(2)}) collective-permute-start(bf16[128,2048]{1,0:T(8,128)(2,1)} %refs_4_.1), channel_id=1, source_target_pairs={{0,16},{8,24},{16,0},{24,8},{1,17},{9,25},{17,1},{25,9},{2,18},{10... | collective-permute-start | bytes 1572872 | tf_op jit(solution)/shard_map/ppermute | solution.py:323
  13.4 13.7 %collective-permute-start.16 = (bf16[64,2048]{1,0:T(8,128)(2,1)S(1)}, bf16[64,2048]{1,0:T(8,128)(2,1)S(1)}, u32[]{:S(2)}, u32[]{:S(2)}) collective-permute-start(bf16[64,2048]{1,0:T(8,128)(2,1)S(1)} %collective-permute-done.15.refs_3_), channel_id=1, source_target_pairs={{2,0},{4,2},{6,4},{7,6},{5,7},{3,5},{1,3},{0,1},{10,8},{12,10},{14... | collective-permute-start | bytes 786440 | tf_op jit(solution)/shard_map/ppermute | solution.py:302
  16.0 9.2 %collective-permute-start.7 = (bf16[64,2048]{1,0:T(8,128)(2,1)S(1)}, bf16[64,2048]{1,0:T(8,128)(2,1)S(1)}, u32[]{:S(2)}, u32[]{:S(2)}) collective-permute-start(bf16[64,2048]{1,0:T(8,128)(2,1)S(1)} %collective-permute-done.6.refs_0_), channel_id=1, source_target_pairs={{0,2},{2,4},{4,6},{6,7},{7,5},{5,3},{3,1},{1,0},{8,10},{10,12},{12... | collective-permute-start | bytes 786440 | tf_op jit(solution)/shard_map/ppermute | solution.py:299
  18.6 16.1 %collective-permute-start.10 = (bf16[64,2048]{1,0:T(8,128)(2,1)S(1)}, bf16[64,2048]{1,0:T(8,128)(2,1)S(1)}, u32[]{:S(2)}, u32[]{:S(2)}) collective-permute-start(bf16[64,2048]{1,0:T(8,128)(2,1)S(1)} %collective-permute-done.9.refs_1_), channel_id=1, source_target_pairs={{0,2},{2,4},{4,6},{6,7},{7,5},{5,3},{3,1},{1,0},{8,10},{10,12},{12... | collective-permute-start | bytes 786440 | tf_op jit(solution)/shard_map/ppermute | solution.py:299
  20.3 16.5 %collective-permute-start.13 = (bf16[64,2048]{1,0:T(8,128)(2,1)S(1)}, bf16[64,2048]{1,0:T(8,128)(2,1)S(1)}, u32[]{:S(2)}, u32[]{:S(2)}) collective-permute-start(bf16[64,2048]{1,0:T(8,128)(2,1)S(1)} %collective-permute-done.12.refs_2_), channel_id=1, source_target_pairs={{2,0},{4,2},{6,4},{7,6},{5,7},{3,5},{1,3},{0,1},{10,8},{12,10},{14... | collective-permute-start | bytes 786440 | tf_op jit(solution)/shard_map/ppermute | solution.py:302
  25.2 11.6 %collective-permute-start.8 = (bf16[64,2048]{1,0:T(8,128)(2,1)S(1)}, bf16[64,2048]{1,0:T(8,128)(2,1)S(1)}, u32[]{:S(2)}, u32[]{:S(2)}) collective-permute-start(bf16[64,2048]{1,0:T(8,128)(2,1)S(1)} %collective-permute-done.7.refs_4_), channel_id=1, source_target_pairs={{0,2},{2,4},{4,6},{6,7},{7,5},{5,3},{3,1},{1,0},{8,10},{10,12},{12... | collective-permute-start | bytes 786440 | tf_op jit(solution)/shard_map/ppermute | solution.py:299
  27.1 11.7 %collective-permute-start.17 = (bf16[64,2048]{1,0:T(8,128)(2,1)S(1)}, bf16[64,2048]{1,0:T(8,128)(2,1)S(1)}, u32[]{:S(2)}, u32[]{:S(2)}) collective-permute-start(bf16[64,2048]{1,0:T(8,128)(2,1)S(1)} %collective-permute-done.16.refs_7_), channel_id=1, source_target_pairs={{2,0},{4,2},{6,4},{7,6},{5,7},{3,5},{1,3},{0,1},{10,8},{12,10},{14... | collective-permute-start | bytes 786440 | tf_op jit(solution)/shard_map/ppermute | solution.py:302
  27.9 13.0 %all-to-all-start = ((f32[8,8,128]{2,1,0:T(8,128)}), f32[8,8,128]{2,1,0:T(8,128)S(1)}, u32[]{:S(2)}, u32[]{:S(2)}) async-start(f32[8,8,128]{2,1,0:T(8,128)} %bitcast.20), calls=%async_computation | async-start | bytes 65536 | tf_op jit(solution)/shard_map/all_to_all | solution.py:307
  34.7 35.0 %collective-permute-start.11 = (bf16[64,2048]{1,0:T(8,128)(2,1)S(1)}, bf16[64,2048]{1,0:T(8,128)(2,1)S(1)}, u32[]{:S(2)}, u32[]{:S(2)}) collective-permute-start(bf16[64,2048]{1,0:T(8,128)(2,1)S(1)} %collective-permute-done.10.refs_5_), channel_id=1, source_target_pairs={{0,2},{2,4},{4,6},{6,7},{7,5},{5,3},{3,1},{1,0},{8,10},{10,12},{12... | collective-permute-start | bytes 786440 | tf_op jit(solution)/shard_map/ppermute | solution.py:299
  36.8 33.1 %collective-permute-start.14 = (bf16[64,2048]{1,0:T(8,128)(2,1)S(1)}, bf16[64,2048]{1,0:T(8,128)(2,1)}, u32[]{:S(2)}, u32[]{:S(2)}) collective-permute-start(bf16[64,2048]{1,0:T(8,128)(2,1)S(1)} %collective-permute-done.13.refs_6_), channel_id=1, source_target_pairs={{2,0},{4,2},{6,4},{7,6},{5,7},{3,5},{1,3},{0,1},{10,8},{12,10},{14... | collective-permute-start | bytes 786440 | tf_op jit(solution)/shard_map/ppermute | solution.py:302
  36.8 33.0 %collective-permute-start.18 = (bf16[64,2048]{1,0:T(8,128)(2,1)S(1)}, bf16[64,2048]{1,0:T(8,128)(2,1)}, u32[]{:S(2)}, u32[]{:S(2)}) collective-permute-start(bf16[64,2048]{1,0:T(8,128)(2,1)S(1)} %collective-permute-done.8.refs_0_), channel_id=1, source_target_pairs={{0,2},{2,4},{4,6},{6,7},{7,5},{5,3},{3,1},{1,0},{8,10},{10,12},{12... | collective-permute-start | bytes 786440 | tf_op jit(solution)/shard_map/ppermute | solution.py:299
  38.8 31.1 %collective-permute-start.19 = (bf16[64,2048]{1,0:T(8,128)(2,1)S(1)}, bf16[64,2048]{1,0:T(8,128)(2,1)}, u32[]{:S(2)}, u32[]{:S(2)}) collective-permute-start(bf16[64,2048]{1,0:T(8,128)(2,1)S(1)} %collective-permute-done.17.refs_3_), channel_id=1, source_target_pairs={{2,0},{4,2},{6,4},{7,6},{5,7},{3,5},{1,3},{0,1},{10,8},{12,10},{14... | collective-permute-start | bytes 786440 | tf_op jit(solution)/shard_map/ppermute | solution.py:302
  53.0 35.3 %collective-permute-start = (bf16[128,2048]{1,0:T(8,128)(2,1)S(1)}, bf16[128,2048]{1,0:T(8,128)(2,1)S(1)}, u32[]{:S(2)}, u32[]{:S(2)}) collective-permute-start(bf16[128,2048]{1,0:T(8,128)(2,1)S(1)} %copy-done.3), channel_id=1, source_target_pairs={{0,8},{8,0},{16,24},{24,16},{1,9},{9,1},{17,25},{25,17},{2,10},{10... | collective-permute-start | bytes 1572872 | tf_op jit(solution)/shard_map/ppermute | solution.py:323
  69.8 24.9 %collective-permute-start.3 = (bf16[128,2048]{1,0:T(8,128)(2,1)S(1)}, bf16[128,2048]{1,0:T(8,128)(2,1)S(1)}, u32[]{:S(2)}, u32[]{:S(2)}) collective-permute-start(bf16[128,2048]{1,0:T(8,128)(2,1)S(1)} %collective-permute-done.2.first), channel_id=1, source_target_pairs={{0,8},{8,0},{16,24},{24,16},{1,9},{9,1},{17,25},{25,17},{2,10},{10... | collective-permute-start | bytes 1572872 | tf_op jit(solution)/shard_map/ppermute | solution.py:323
  88.0 12.6 %collective-permute-start.27 = (bf16[64,2048]{1,0:T(8,128)(2,1)}, bf16[64,2048]{1,0:T(8,128)(2,1)S(1)}, u32[]{:S(2)}, u32[]{:S(2)}) collective-permute-start(bf16[64,2048]{1,0:T(8,128)(2,1)} %get-tuple-element.54), channel_id=1, source_target_pairs={{0,2},{2,4},{4,6},{6,7},{7,5},{5,3},{3,1},{1,0},{8,10},{10,12},{12... | collective-permute-start | bytes 786440 | tf_op jit(solution)/shard_map/ppermute | solution.py:361
  92.4 35.4 %collective-permute-start.1 = (bf16[128,2048]{1,0:T(8,128)(2,1)S(1)}, bf16[128,2048]{1,0:T(8,128)(2,1)S(1)}, u32[]{:S(2)}, u32[]{:S(2)}) collective-permute-start(bf16[128,2048]{1,0:T(8,128)(2,1)S(1)} %get-tuple-element.34), channel_id=1, source_target_pairs={{0,8},{8,0},{16,24},{24,16},{1,9},{9,1},{17,25},{25,17},{2,10},{10... | collective-permute-start | bytes 1572872 | tf_op jit(solution)/shard_map/ppermute | solution.py:331
  92.5 9.2 %collective-permute-start.30 = (bf16[64,2048]{1,0:T(8,128)(2,1)S(1)}, bf16[64,2048]{1,0:T(8,128)(2,1)S(1)}, u32[]{:S(2)}, u32[]{:S(2)}) collective-permute-start(bf16[64,2048]{1,0:T(8,128)(2,1)S(1)} %copy-done.30), channel_id=1, source_target_pairs={{2,0},{4,2},{6,4},{7,6},{5,7},{3,5},{1,3},{0,1},{10,8},{12,10},{14... | collective-permute-start | bytes 786440 | tf_op jit(solution)/shard_map/ppermute | solution.py:361
  94.4 8.5 %collective-permute-start.20 = (bf16[64,2048]{1,0:T(8,128)(2,1)S(1)}, bf16[64,2048]{1,0:T(8,128)(2,1)S(1)}, u32[]{:S(2)}, u32[]{:S(2)}) collective-permute-start(bf16[64,2048]{1,0:T(8,128)(2,1)S(1)} %copy-done.29), channel_id=1, source_target_pairs={{0,2},{2,4},{4,6},{6,7},{7,5},{5,3},{3,1},{1,0},{8,10},{10,12},{12... | collective-permute-start | bytes 786440 | tf_op jit(solution)/shard_map/ppermute | solution.py:361
  94.7 12.7 %collective-permute-start.24 = (bf16[64,2048]{1,0:T(8,128)(2,1)S(1)}, bf16[64,2048]{1,0:T(8,128)(2,1)S(1)}, u32[]{:S(2)}, u32[]{:S(2)}) collective-permute-start(bf16[64,2048]{1,0:T(8,128)(2,1)S(1)} %copy-done.28), channel_id=1, source_target_pairs={{2,0},{4,2},{6,4},{7,6},{5,7},{3,5},{1,3},{0,1},{10,8},{12,10},{14... | collective-permute-start | bytes 786440 | tf_op jit(solution)/shard_map/ppermute | solution.py:361
  101.7 8.2 %collective-permute-start.28 = (bf16[64,2048]{1,0:T(8,128)(2,1)S(1)}, bf16[64,2048]{1,0:T(8,128)(2,1)S(1)}, u32[]{:S(2)}, u32[]{:S(2)}) collective-permute-start(bf16[64,2048]{1,0:T(8,128)(2,1)S(1)} %add_convert_fusion.6), channel_id=1, source_target_pairs={{0,2},{2,4},{4,6},{6,7},{7,5},{5,3},{3,1},{1,0},{8,10},{10,12},{12... | collective-permute-start | bytes 786440 | tf_op jit(solution)/shard_map/ppermute | solution.py:361
  102.9 10.0 %collective-permute-start.31 = (bf16[64,2048]{1,0:T(8,128)(2,1)S(1)}, bf16[64,2048]{1,0:T(8,128)(2,1)S(1)}, u32[]{:S(2)}, u32[]{:S(2)}) collective-permute-start(bf16[64,2048]{1,0:T(8,128)(2,1)S(1)} %add_convert_fusion.4), channel_id=1, source_target_pairs={{2,0},{4,2},{6,4},{7,6},{5,7},{3,5},{1,3},{0,1},{10,8},{12,10},{14... | collective-permute-start | bytes 786440 | tf_op jit(solution)/shard_map/ppermute | solution.py:361
  107.3 8.2 %collective-permute-start.21 = (bf16[64,2048]{1,0:T(8,128)(2,1)S(1)}, bf16[64,2048]{1,0:T(8,128)(2,1)S(1)}, u32[]{:S(2)}, u32[]{:S(2)}) collective-permute-start(bf16[64,2048]{1,0:T(8,128)(2,1)S(1)} %add_convert_fusion.11), channel_id=1, source_target_pairs={{0,2},{2,4},{4,6},{6,7},{7,5},{5,3},{3,1},{1,0},{8,10},{10,12},{12... | collective-permute-start | bytes 786440 | tf_op jit(solution)/shard_map/ppermute | solution.py:361
  108.5 10.0 %collective-permute-start.25 = (bf16[64,2048]{1,0:T(8,128)(2,1)S(1)}, bf16[64,2048]{1,0:T(8,128)(2,1)S(1)}, u32[]{:S(2)}, u32[]{:S(2)}) collective-permute-start(bf16[64,2048]{1,0:T(8,128)(2,1)S(1)} %add_convert_fusion.8), channel_id=1, source_target_pairs={{2,0},{4,2},{6,4},{7,6},{5,7},{3,5},{1,3},{0,1},{10,8},{12,10},{14... | collective-permute-start | bytes 786440 | tf_op jit(solution)/shard_map/ppermute | solution.py:361
  109.9 18.7 %collective-permute-start.5 = (bf16[128,2048]{1,0:T(8,128)(2,1)S(1)}, bf16[128,2048]{1,0:T(8,128)(2,1)S(1)}, u32[]{:S(2)}, u32[]{:S(2)}) collective-permute-start(bf16[128,2048]{1,0:T(8,128)(2,1)S(1)} %add_convert_fusion), channel_id=1, source_target_pairs={{0,16},{8,24},{16,0},{24,8},{1,17},{9,25},{17,1},{25,9},{2,18},{10... | collective-permute-start | bytes 1572872 | tf_op jit(solution)/shard_map/ppermute | solution.py:331
  112.9 15.9 %collective-permute-start.29 = (bf16[64,2048]{1,0:T(8,128)(2,1)S(1)}, bf16[64,2048]{1,0:T(8,128)(2,1)S(1)}, u32[]{:S(2)}, u32[]{:S(2)}) collective-permute-start(bf16[64,2048]{1,0:T(8,128)(2,1)S(1)} %add_convert_fusion.5), channel_id=1, source_target_pairs={{0,2},{2,4},{4,6},{6,7},{7,5},{5,3},{3,1},{1,0},{8,10},{10,12},{12... | collective-permute-start | bytes 786440 | tf_op jit(solution)/shard_map/ppermute | solution.py:361
  123.7 9.2 %collective-permute-start.26 = (bf16[64,2048]{1,0:T(8,128)(2,1)S(1)}, bf16[64,2048]{1,0:T(8,128)(2,1)S(1)}, u32[]{:S(2)}, u32[]{:S(2)}) collective-permute-start(bf16[64,2048]{1,0:T(8,128)(2,1)S(1)} %add_convert_fusion.7), channel_id=1, source_target_pairs={{2,0},{4,2},{6,4},{7,6},{5,7},{3,5},{1,3},{0,1},{10,8},{12,10},{14... | collective-permute-start | bytes 786440 | tf_op jit(solution)/shard_map/ppermute | solution.py:361
  126.4 10.2 %collective-permute-start.33 = (bf16[64,2048]{1,0:T(8,128)(2,1)S(1)}, bf16[64,2048]{1,0:T(8,128)(2,1)S(1)}, u32[]{:S(2)}, u32[]{:S(2)}) collective-permute-start(bf16[64,2048]{1,0:T(8,128)(2,1)S(1)} %add_convert_fusion.2), channel_id=1, source_target_pairs={{2,0},{4,2},{6,4},{7,6},{5,7},{3,5},{1,3},{0,1},{10,8},{12,10},{14... | collective-permute-start | bytes 786440 | tf_op jit(solution)/shard_map/ppermute | solution.py:361
  127.8 8.8 %collective-permute-start.23 = (bf16[64,2048]{1,0:T(8,128)(2,1)S(1)}, bf16[64,2048]{1,0:T(8,128)(2,1)S(1)}, u32[]{:S(2)}, u32[]{:S(2)}) collective-permute-start(bf16[64,2048]{1,0:T(8,128)(2,1)S(1)} %add_convert_fusion.9), channel_id=1, source_target_pairs={{0,2},{2,4},{4,6},{6,7},{7,5},{5,3},{3,1},{1,0},{8,10},{10,12},{12... | collective-permute-start | bytes 786440 | tf_op jit(solution)/shard_map/ppermute | solution.py:361
  (34 other events, 527.4 us)

commit v3 on v1

v3 whole, which is shorter than its diff:
```python
import functools

import jax
import jax.numpy as jnp
from jax import lax
from jax.experimental import pallas as pl
from jax.experimental.pallas import tpu as pltpu
from jax.sharding import PartitionSpec as P

HOT_SLOTS = 40
SLOTS = 24
EXTRA = HOT_SLOTS - SLOTS
BF16 = jnp.bfloat16
F32 = jnp.float32
HBM = pl.BlockSpec(memory_space=pltpu.HBM)
VMEM = pl.BlockSpec(memory_space=pltpu.VMEM)
SMEM = pl.BlockSpec(memory_space=pltpu.SMEM)


def ring_of(count):
    return list(range(0, count, 2)) + list(range(count - 1, 0, -2))


def offsets_of(count):
    order = [0, count // 2]
    for hop in range(1, count // 2):
        order += [hop, count - hop]
    return order


def dot(a, b):
    return jnp.dot(a, b, preferred_element_type=F32)


def dot_t(a, b):
    return lax.dot_general(a, b, (((1,), (1,)), ((), ())), preferred_element_type=F32)


def dot_l(a, b):
    return lax.dot_general(a, b, (((0,), (0,)), ((), ())), preferred_element_type=F32)


def routing(expert_ids, gate_weights, capacity, hot_expert, experts):
    tokens, top = expert_ids.shape
    ids, gates = expert_ids.T, gate_weights.T
    labels = jnp.arange(experts, dtype=jnp.int32)[:, None]
    chosen = jnp.zeros((experts, tokens), jnp.bool_)
    weight = jnp.zeros((experts, tokens), F32)
    for k in range(top):
        here = ids[k][None, :] == labels
        chosen = chosen | here
        weight = weight + jnp.where(here, gates[k][None, :], 0.0)
    place = jnp.arange(tokens, dtype=jnp.int32)
    earlier = (place[:, None] < place[None, :]).astype(BF16)
    rank = dot(chosen.astype(BF16), earlier)
    limit = jnp.where(labels == hot_expert[0], HOT_SLOTS, capacity[0][:, None]).astype(F32)
    kept = chosen & (rank < limit)
    return jnp.stack([jnp.where(kept, rank, -1.0), jnp.where(kept, weight, 0.0)], axis=1)


def experts_kernel(offsets, sizes, local, buffers, idx, meta, *refs):
    refs = list(refs)
    units = [[refs.pop(0) for _ in range(size)] for size in sizes]
    source = [refs.pop(0) for _ in range(3)]
    outs = [[refs.pop(0) for _ in range(2)] for _ in offsets]
    held = [refs.pop(0) for _ in range(3)]
    sel, eo, rows, scale, sem = refs
    pairs = len(offsets) // 2
    width = rows.shape[2]
    wide, wide_x = 2 * SLOTS, 2 * EXTRA
    base = pairs * wide
    full = pairs * (wide + wide_x)
    hot = idx[idx.shape[0] - 1]

    def fetching(e, k):
        at = lax.rem(e, buffers)
        return pltpu.make_async_copy(source[k].at[e], held[k].at[at], sem.at[at, k])

    for e in range(min(buffers, local)):
        for k in range(3):
            fetching(e, k).start()

    lane = lax.broadcasted_iota(jnp.int32, (1, 256), 1)
    second = (lane >= 128).astype(F32)
    for p in range(pairs):
        info = [meta[idx[offsets[2 * p + i]]] for i in range(2)]
        blocks = []
        for e in range(local):
            rank = jnp.concatenate([info[0][2 * e : 2 * e + 1], info[1][2 * e : 2 * e + 1]], axis=1)
            gate = jnp.concatenate([info[0][2 * e + 1 : 2 * e + 2], info[1][2 * e + 1 : 2 * e + 2]], axis=1)
            key = jnp.where((rank >= 0) & (rank < SLOTS), rank + SLOTS * second, -1.0).astype(jnp.int32)
            pick = (lax.broadcasted_iota(jnp.int32, (wide, 256), 0) == key).astype(F32)
            blocks.append(pick)
            scale[e, pl.ds(p * wide, wide), :] = jnp.broadcast_to(
                jnp.sum(pick * gate, axis=1, keepdims=True), (wide, 128)
            )
            key_x = jnp.where((rank >= SLOTS) & (hot == e), rank - SLOTS + EXTRA * second, -1.0)
            pick_x = (lax.broadcasted_iota(jnp.int32, (wide_x, 256), 0) == key_x.astype(jnp.int32)).astype(F32)
            scale[e, pl.ds(base + p * wide_x, wide_x), :] = jnp.broadcast_to(
                jnp.sum(pick_x * gate, axis=1, keepdims=True), (wide_x, 128)
            )
            extra = pick_x if e == 0 else extra + pick_x
        blocks.append(extra)
        pick = jnp.concatenate(blocks, axis=0).astype(BF16)
        sel[p] = pick
        pair = jnp.concatenate([unit[...] for mine in units[2 * p : 2 * p + 2] for unit in mine], axis=0)
        got = dot(pick, pair).astype(BF16)
        for e in range(local):
            rows[e, pl.ds(p * wide, wide), :] = got[e * wide : (e + 1) * wide]

            @pl.when(hot == e)
            def _():
                rows[e, pl.ds(base + p * wide_x, wide_x), :] = got[local * wide :]

        eo[p, pl.ds(local * wide, wide_x), :] = jnp.zeros((wide_x, width), BF16)

    def run(e, length):
        at = lax.rem(e, buffers)
        tokens = rows[e, :length]
        gate = dot_t(tokens, held[0][at])
        upper = dot_t(tokens, held[1][at])
        hidden = (gate / (1.0 + jnp.exp(-gate)) * upper * scale[e, :length][:, :1]).astype(BF16)
        fetching(e, 2).wait()
        out = dot(hidden, held[2][at]).astype(BF16)
        for p in range(pairs):
            eo[p, pl.ds(pl.multiple_of(e * wide, wide), wide), :] = out[p * wide : (p + 1) * wide]
            if length > base:
                eo[p, pl.ds(local * wide, wide_x), :] = out[base + p * wide_x : base + (p + 1) * wide_x]

    def body(e, carry):
        fetching(e, 0).wait()
        fetching(e, 1).wait()

        @pl.when(hot == e)
        def _():
            run(e, full)

        @pl.when(hot != e)
        def _():
            run(e, base)

        @pl.when(e + buffers < local)
        def _():
            for k in range(3):
                fetching(e + buffers, k).start()

        return carry

    lax.fori_loop(0, local, body, 0)

    for p in range(pairs):
        total = dot_l(sel[p], eo[p]).astype(BF16)
        for i in range(4):
            outs[2 * p + i // 2][i % 2][...] = total[i * 64 : (i + 1) * 64]


def run_experts(offsets, local, idx, meta, blocks, weights):
    hidden, width = weights[2].shape[1:]
    wide, wide_x = 2 * SLOTS, 2 * EXTRA
    pairs = len(offsets) // 2
    high = local * wide + wide_x
    full = pairs * (wide + wide_x)
    buffers = min(local, 3)
    flat = [unit for o in offsets for unit in blocks[o]]
    sizes = tuple(len(blocks[o]) for o in offsets)
    room = 3 * buffers * hidden * width * 2 + local * full * (2 * width + 512) + pairs * high * (2 * width + 512)
    room += full * (6 * width + 10 * hidden) + (2 << 20)
    flat = [pltpu.with_memory_space_constraint(unit, pltpu.VMEM) for unit in flat]
    weights = [pltpu.with_memory_space_constraint(w, pltpu.HBM) for w in weights]
    flops = 2 * 3 * width * hidden * local * pairs * wide + 4 * len(offsets) * 128 * high * width
    return pl.pallas_call(
        functools.partial(experts_kernel, offsets, sizes, local, buffers),
        out_shape=[pltpu.VMEM((64, width), BF16)] * (2 * len(offsets)),
        in_specs=[SMEM, VMEM] + [VMEM] * len(flat) + [HBM] * 3,
        out_specs=[VMEM] * (2 * len(offsets)),
        scratch_shapes=[
            pltpu.VMEM((buffers, hidden, width), BF16),
            pltpu.VMEM((buffers, hidden, width), BF16),
            pltpu.VMEM((buffers, hidden, width), BF16),
            pltpu.VMEM((pairs, high, 256), BF16),
            pltpu.VMEM((pairs, high, width), BF16),
            pltpu.VMEM((local, full, width), BF16),
            pltpu.VMEM((local, full, 128), F32),
            pltpu.SemaphoreType.DMA((buffers, 3)),
        ],
        cost_estimate=pl.CostEstimate(
            flops=flops,
            transcendentals=local * pairs * wide * hidden,
            bytes_accessed=6 * local * hidden * width,
        ),
        compiler_params=pltpu.CompilerParams(vmem_limit_bytes=room),
        name="routed_experts",
    )(idx, meta, *flat, *weights)


def shared_kernel(first, second, w_gate, w_up, w_down, out_first, out_second):
    tokens = jnp.concatenate([first[...], second[...]], axis=0)
    gate = dot(tokens, w_gate[...])
    upper = dot(tokens, w_up[...])
    hidden = (gate / (1.0 + jnp.exp(-gate)) * upper).astype(BF16)
    out = dot(hidden, w_down[...]).astype(BF16)
    rows = first.shape[0]
    out_first[...] = out[:rows]
    out_second[...] = out[rows:]


def run_shared(first, second, w_gate, w_up, w_down):
    rows, width = first.shape
    hidden = w_gate.shape[1]
    return pl.pallas_call(
        shared_kernel,
        out_shape=[jax.ShapeDtypeStruct((rows, width), BF16)] * 2,
        in_specs=[VMEM] * 5,
        out_specs=[VMEM] * 2,
        cost_estimate=pl.CostEstimate(
            flops=2 * 3 * 2 * rows * width * hidden,
            transcendentals=2 * rows * hidden,
            bytes_accessed=2 * (3 * width * hidden + 4 * rows * width),
        ),
        compiler_params=pltpu.CompilerParams(vmem_limit_bytes=16 << 20),
        name="shared_experts",
    )(first, second, w_gate, w_up, w_down)


def on_device(
    latents,
    expert_ids,
    gate_weights,
    capacity,
    hot_expert,
    w_gate,
    w_up,
    w_down,
    shared_gate,
    shared_up,
    shared_down,
):
    tokens, width = latents.shape
    half = tokens // 2
    experts = capacity.shape[1]
    local = w_gate.shape[0]
    count = lax.axis_size("expert")
    n_dp = lax.axis_size("dp")
    ring = ring_of(count)
    forward = [(ring[i], ring[(i + 1) % count]) for i in range(count)]
    backward = [(b, a) for a, b in forward]
    mid = count // 2

    own = [latents[:half], latents[half:]]
    blocks = {o: [None, None] for o in range(count)}
    for h in range(2):
        up, down = own[h], own[h]
        for hop in range(1, mid + 1):
            if hop < mid or h == 0:
                up = lax.ppermute(up, "expert", forward)
                blocks[hop][h] = up
            if hop < mid or h == 1:
                down = lax.ppermute(down, "expert", backward)
                blocks[count - hop][h] = down
    blocks[0] = [latents]

    info = routing(expert_ids, gate_weights, capacity, hot_expert, experts)
    meta = lax.all_to_all(
        info.reshape(count, 2 * local, tokens), "expert", split_axis=0, concat_axis=0, tiled=True
    )
    me = lax.axis_index("expert")
    table = []
    for e in range(count):
        at = ring.index(e)
        table.append([ring[(at - o) % count] for o in range(count)])
    idx = jnp.array(table, jnp.int32)[me]
    idx = jnp.concatenate([idx, (hot_expert - me * local).astype(jnp.int32)])

    bits = [1 << b for b in range(n_dp.bit_length() - 1)]
    near = {0: latents}
    for bit in reversed(bits):
        swap = [(d, d ^ bit) for d in range(n_dp)]
        for r in list(near):
            near[r ^ bit] = lax.ppermute(near[r], "dp", swap)
    part = {}
    for r in range(0, n_dp, 2):
        part[r], part[r + 1] = run_shared(near[r], near[r + 1], shared_gate, shared_up, shared_down)
    weights = [jnp.swapaxes(w_gate, 1, 2), jnp.swapaxes(w_up, 1, 2), w_down]
    order = offsets_of(count)
    idx, *kept = lax.optimization_barrier((idx, *part.values()))
    part = dict(zip(part, kept))
    done = {}
    for at in range(0, count, 8):
        chunk = tuple(order[at : at + 8])
        flat = run_experts(chunk, local, idx, meta, blocks, weights)
        for i, o in enumerate(chunk):
            done[o] = [flat[2 * i], flat[2 * i + 1]]

    for bit in bits:
        swap = [(d, d ^ bit) for d in range(n_dp)]
        for r in sorted(part):
            if r & bit:
                came = lax.ppermute(part.pop(r), "dp", swap)
                total = part[r ^ bit].astype(F32) + came.astype(F32)
                part[r ^ bit] = total if bit == bits[-1] else total.astype(BF16)
    shared = part[0]

    result = []
    for h in range(2):
        pieces = [done[0][h]]
        for step, perm, long in ((-1, forward, h == 0), (1, backward, h == 1)):
            start = mid if long else mid - 1
            acc = done[(step * start) % count][h]
            for k in range(start, 0, -1):
                came = lax.ppermute(acc, "expert", perm)
                if k > 1:
                    acc = (came.astype(F32) + done[(step * (k - 1)) % count][h].astype(F32)).astype(BF16)
            pieces.append(came)
        total = shared[h * half : (h + 1) * half].astype(F32)
        for piece in pieces:
            total = total + piece.astype(F32)
        result.append(total.astype(BF16))
    return jnp.concatenate(result, axis=0)


def solution(mesh):
    placed = (
        P(("dp", "expert"), None),
        P(("dp", "expert"), None),
        P(("dp", "expert"), None),
        P("dp", None),
        P("dp"),
        P("expert", None, None),
        P("expert", None, None),
        P("expert", None, None),
        P(None, "dp"),
        P(None, "dp"),
        P("dp", None),
    )
    return jax.shard_map(
        on_device, mesh=mesh, in_specs=placed, out_specs=P(("dp", "expert"), None), check_vma=False
    )
```

time: 157 us -> 130 us (0.83)
  local copies, waits for them, and re-layouts: 37.6 us -> 19.7 us
  Pallas kernels: 33.4 us -> 20.4 us
  waiting for transfers between devices: 33.6 us -> 45.2 us
  starting transfers between devices: 46.2 us -> 40.5 us
    unnamed x46 -> x32, local copies, waits for them, and re-layouts: 33.4 us -> 15.5 us
    ppermute x7, starting transfers between devices: 0.04 us -> 9.38 us  [on_device(): down = lax.ppermute(down, 'expert', backward)]
    ppermute x14, waiting for transfers between devices: 19.8 us -> 28.9 us  [on_device(): came = lax.ppermute(acc, 'expert', perm)]
    ppermute x7, starting transfers between devices: 15.8 us -> 7.62 us  [on_device(): up = lax.ppermute(up, 'expert', forward)]
    pallas_call x1, Pallas kernels: 24.8 us -> 16.6 us  [run_experts(): pl.pallas_call(functools.partial(experts_kernel, offsets, sizes, local, b...]
    ppermute x7, waiting for transfers between devices: 0.18 us -> 7.15 us  [on_device(): down = lax.ppermute(down, 'expert', backward)]
    pallas_call x2, Pallas kernels: 8.67 us -> 3.73 us  [run_shared(): pl.pallas_call(shared_kernel, out_shape=[jax.ShapeDtypeStruct((rows, widt...]
    ppermute x14, starting transfers between devices: 20 us -> 15.4 us  [on_device(): came = lax.ppermute(acc, 'expert', perm)]
  transfers between devices with their start and end apart: 35 -> 35, of which waited for: 15 -> 13; matrix products, arithmetic and copies ran while one was open for 25% -> 5% of each run, Pallas kernels for 21% -> 3%
where the time goes in v3:
time: 130 us
  waiting for transfers between devices  45.2 us (35%)
  starting transfers between devices  40.5 us (31%)
  Pallas kernels  20.4 us (16%)
  local copies, waits for them, and re-layouts  19.7 us (15%)
  other arithmetic  2.85 us (2%)
    ppermute x14, waiting for transfers between devices, on_device(): came = lax.ppermute(acc, 'expert', perm)  28.9 us
    pallas_call x1, Pallas kernels, run_experts(): pl.pallas_call(functools.partial(experts_kernel, offsets, sizes, local, b...  16.6 us
    unnamed x32, local copies, waits for them, and re-layouts  15.5 us
    ppermute x14, starting transfers between devices, on_device(): came = lax.ppermute(acc, 'expert', perm)  15.4 us
    ppermute x7, starting transfers between devices, on_device(): down = lax.ppermute(down, 'expert', backward)  9.38 us
    ppermute x7, waiting for transfers between devices, on_device(): up = lax.ppermute(up, 'expert', forward)  9.14 us
    ppermute x7, starting transfers between devices, on_device(): up = lax.ppermute(up, 'expert', forward)  7.62 us
    ppermute x7, waiting for transfers between devices, on_device(): down = lax.ppermute(down, 'expert', backward)  7.15 us
  transfers between devices with their start and end apart: 35, of which 13 were waited for; matrix products, arithmetic and copies ran while one was open for 5% of the time, Pallas kernels for 3%

profile of v3, /device:TPU:0, one launch (start us, length us, event | category | flops | bytes accessed | tf_op | source)
XLA Modules:
  0.0 129.6 jit_solution(3719217791860356191)
XLA Ops:
  0.5 2.6 %collective-permute-start.1 = (bf16[128,2048]{1,0:T(8,128)(2,1)}, bf16[128,2048]{1,0:T(8,128)(2,1)S(1)}, u32[]{:S(2)}, u32[]{:S(2)}) collective-permute-start(bf16[128,2048]{1,0:T(8,128)(2,1)} %refs_0_.1), channel_id=1, source_target_pairs={{0,16},{8,24},{16,0},{24,8},{1,17},{9,25},{17,1},{25,9},{2,18},{10... | collective-permute-start | bytes 1572872 | tf_op jit(solution)/shard_map/ppermute | solution.py:279
  6.2 1.6 %collective-permute-start.6 = (bf16[64,2048]{1,0:T(8,128)(2,1)S(1)}, bf16[64,2048]{1,0:T(8,128)(2,1)S(1)}, u32[]{:S(2)}, u32[]{:S(2)}) collective-permute-start(bf16[64,2048]{1,0:T(8,128)(2,1)S(1)} %get-tuple-element.58), channel_id=1, source_target_pairs={{0,2},{2,4},{4,6},{6,7},{7,5},{5,3},{3,1},{1,0},{8,10},{10,12},{12... | collective-permute-start | bytes 786440 | tf_op jit(solution)/shard_map/ppermute | solution.py:255
  10.2 9.1 %collective-permute-done.6.refs_3_ = bf16[64,2048]{1,0:T(8,128)(2,1)S(1)} collective-permute-done((bf16[64,2048]{1,0:T(8,128)(2,1)S(1)}, bf16[64,2048]{1,0:T(8,128)(2,1)S(1)}, u32[]{:S(2)}, u32[]{:S(2)}) %collective-permute-start.6) | collective-permute-done | bytes 262176 | tf_op jit(solution)/shard_map/ppermute | solution.py:255
  19.4 1.6 %collective-permute-start.15 = (bf16[64,2048]{1,0:T(8,128)(2,1)S(1)}, bf16[64,2048]{1,0:T(8,128)(2,1)S(1)}, u32[]{:S(2)}, u32[]{:S(2)}) collective-permute-start(bf16[64,2048]{1,0:T(8,128)(2,1)S(1)} %get-tuple-element.58), channel_id=1, source_target_pairs={{2,0},{4,2},{6,4},{7,6},{5,7},{3,5},{1,3},{0,1},{10,8},{12,10},{14... | collective-permute-start | bytes 786440 | tf_op jit(solution)/shard_map/ppermute | solution.py:258
  21.4 1.6 %collective-permute-start.11 = (bf16[64,2048]{1,0:T(8,128)(2,1)S(1)}, bf16[64,2048]{1,0:T(8,128)(2,1)}, u32[]{:S(2)}, u32[]{:S(2)}) collective-permute-start(bf16[64,2048]{1,0:T(8,128)(2,1)S(1)} %collective-permute-done.10.refs_6_), channel_id=1, source_target_pairs={{2,0},{4,2},{6,4},{7,6},{5,7},{3,5},{1,3},{0,1},{10,8},{12,10},{14... | collective-permute-start | bytes 786440 | tf_op jit(solution)/shard_map/ppermute | solution.py:258
  23.7 4.9 %collective-permute-done.15.refs_5_ = bf16[64,2048]{1,0:T(8,128)(2,1)S(1)} collective-permute-done((bf16[64,2048]{1,0:T(8,128)(2,1)S(1)}, bf16[64,2048]{1,0:T(8,128)(2,1)S(1)}, u32[]{:S(2)}, u32[]{:S(2)}) %collective-permute-start.15) | collective-permute-done | bytes 262176 | tf_op jit(solution)/shard_map/ppermute | solution.py:258
  32.6 1.8 %collective-permute-done.11.refs_10_ = bf16[64,2048]{1,0:T(8,128)(2,1)} collective-permute-done((bf16[64,2048]{1,0:T(8,128)(2,1)S(1)}, bf16[64,2048]{1,0:T(8,128)(2,1)}, u32[]{:S(2)}, u32[]{:S(2)}) %collective-permute-start.11) | collective-permute-done | bytes 262176 | tf_op jit(solution)/shard_map/ppermute | solution.py:258
  36.5 3.9 %all-to-all-start = ((f32[8,8,128]{2,1,0:T(8,128)}), f32[8,8,128]{2,1,0:T(8,128)S(1)}, u32[]{:S(2)}, u32[]{:S(2)}) async-start(f32[8,8,128]{2,1,0:T(8,128)} %bitcast.20), calls=%async_computation | async-start | bytes 65536 | tf_op jit(solution)/shard_map/all_to_all | solution.py:263
  41.2 2.0 %collective-permute-start.18 = (bf16[64,2048]{1,0:T(8,128)(2,1)}, bf16[64,2048]{1,0:T(8,128)(2,1)}, u32[]{:S(2)}, u32[]{:S(2)}) collective-permute-start(bf16[64,2048]{1,0:T(8,128)(2,1)} %collective-permute-done.16.refs_8_), channel_id=1, source_target_pairs={{0,2},{2,4},{4,6},{6,7},{7,5},{5,3},{3,1},{1,0},{8,10},{10,12},{12... | collective-permute-start | bytes 786440 | tf_op jit(solution)/shard_map/ppermute | solution.py:255
  43.3 2.0 %collective-permute-start.9 = (bf16[64,2048]{1,0:T(8,128)(2,1)}, bf16[64,2048]{1,0:T(8,128)(2,1)}, u32[]{:S(2)}, u32[]{:S(2)}) collective-permute-start(bf16[64,2048]{1,0:T(8,128)(2,1)} %collective-permute-done.8.refs_11_), channel_id=1, source_target_pairs={{0,2},{2,4},{4,6},{6,7},{7,5},{5,3},{3,1},{1,0},{8,10},{10,12},{12... | collective-permute-start | bytes 786440 | tf_op jit(solution)/shard_map/ppermute | solution.py:255
  47.3 1.6 %copy-done = bf16[2048,512]{1,0:T(8,128)(2,1)S(1)} copy-done((bf16[2048,512]{1,0:T(8,128)(2,1)S(1)}, bf16[2048,512]{1,0:T(8,128)(2,1)}, u32[]{:S(2)}) %copy-start) | copy-done | bytes 2097176
  48.9 1.6 %copy-done.2 = bf16[2048,512]{1,0:T(8,128)(2,1)S(1)} copy-done((bf16[2048,512]{1,0:T(8,128)(2,1)S(1)}, bf16[2048,512]{1,0:T(8,128)(2,1)}, u32[]{:S(2)}) %copy-start.2) | copy-done | bytes 2097176
  50.5 1.6 %copy-done.4 = bf16[512,2048]{1,0:T(8,128)(2,1)S(1)} copy-done((bf16[512,2048]{1,0:T(8,128)(2,1)S(1)}, bf16[512,2048]{1,0:T(8,128)(2,1)}, u32[]{:S(2)}) %copy-start.4) | copy-done | bytes 2097176
  53.1 1.9 %shared_experts.2 = (bf16[128,2048]{1,0:T(8,128)(2,1)S(1)}, bf16[128,2048]{1,0:T(8,128)(2,1)S(1)}) custom-call(bf16[128,2048]{1,0:T(8,128)(2,1)S(1)} %copy-done.6, bf16[128,2048]{1,0:T(8,128)(2,1)S(1)} %collective-permute-done.second, bf16[2048,512]{1,0:T(8,128)(2,1)S(1)} %copy-done, bf16[2048,512]{1,0:T(8,128)(2,1)S(1)} %copy-done.2, ...), custom_call_target="tpu_custom_call" | custom-call | flops 1610612736 | bytes 8388608 | tf_op jit(solution)/shard_map/shared_experts/pallas_call | solution.py:210
  55.8 1.6 %copy-done.1 = bf16[2048,512]{1,0:T(8,128)(2,1)S(1)} copy-done((bf16[2048,512]{1,0:T(8,128)(2,1)S(1)}, bf16[2048,512]{1,0:T(8,128)(2,1)}, u32[]{:S(2)}) %copy-start.1) | copy-done | bytes 2097176
  57.4 1.6 %copy-done.3 = bf16[2048,512]{1,0:T(8,128)(2,1)S(1)} copy-done((bf16[2048,512]{1,0:T(8,128)(2,1)S(1)}, bf16[2048,512]{1,0:T(8,128)(2,1)}, u32[]{:S(2)}) %copy-start.3) | copy-done | bytes 2097176
  59.0 1.6 %copy-done.5 = bf16[512,2048]{1,0:T(8,128)(2,1)S(1)} copy-done((bf16[512,2048]{1,0:T(8,128)(2,1)S(1)}, bf16[512,2048]{1,0:T(8,128)(2,1)}, u32[]{:S(2)}) %copy-start.5) | copy-done | bytes 2097176
  60.6 1.9 %shared_experts.3 = (bf16[128,2048]{1,0:T(8,128)(2,1)S(1)}, bf16[128,2048]{1,0:T(8,128)(2,1)S(1)}) custom-call(bf16[128,2048]{1,0:T(8,128)(2,1)S(1)} %collective-permute-done.1.first, bf16[128,2048]{1,0:T(8,128)(2,1)S(1)} %collective-permute-done.2.second, bf16[2048,512]{1,0:T(8,128)(2,1)S(1)} %copy-done.1, bf16[2048,512]{1,0:T(8,128)(2,1)S(1)} %copy-done.3, ...), custom_call_target="tpu_custom_call" | custom-call | flops 1610612736 | bytes 8388608 | tf_op jit(solution)/shard_map/shared_experts/pallas_call | solution.py:210
  65.2 16.6 %routed_experts.1 = (bf16[64,2048]{1,0:T(8,128)(2,1)S(1)}, bf16[64,2048]{1,0:T(8,128)(2,1)S(1)}, bf16[64,2048]{1,0:T(8,128)(2,1)S(1)}, bf16[64,2048]{1,0:T(8,128...) custom-call(s32[9]{0:T(128)S(1)} %pad_add_fusion.idx, ...), custom_call_target="tpu_custom_call" | custom-call | flops 8522825728 | bytes 34603008 | tf_op jit(solution)/shard_map/routed_experts/pallas_call | solution.py:171
  81.9 2.3 %collective-permute-start.24 = (bf16[64,2048]{1,0:T(8,128)(2,1)S(1)}, bf16[64,2048]{1,0:T(8,128)(2,1)S(1)}, u32[]{:S(2)}, u32[]{:S(2)}) collective-permute-start(bf16[64,2048]{1,0:T(8,128)(2,1)S(1)} %get-tuple-element.44), channel_id=1, source_target_pairs={{2,0},{4,2},{6,4},{7,6},{5,7},{3,5},{1,3},{0,1},{10,8},{12,10},{14... | collective-permute-start | bytes 786440 | tf_op jit(solution)/shard_map/ppermute | solution.py:310
  84.7 2.0 %collective-permute-start.30 = (bf16[64,2048]{1,0:T(8,128)(2,1)S(1)}, bf16[64,2048]{1,0:T(8,128)(2,1)S(1)}, u32[]{:S(2)}, u32[]{:S(2)}) collective-permute-start(bf16[64,2048]{1,0:T(8,128)(2,1)S(1)} %get-tuple-element.51), channel_id=1, source_target_pairs={{2,0},{4,2},{6,4},{7,6},{5,7},{3,5},{1,3},{0,1},{10,8},{12,10},{14... | collective-permute-start | bytes 786440 | tf_op jit(solution)/shard_map/ppermute | solution.py:310
  86.7 2.7 %collective-permute-done.24 = bf16[64,2048]{1,0:T(8,128)(2,1)S(1)} collective-permute-done((bf16[64,2048]{1,0:T(8,128)(2,1)S(1)}, bf16[64,2048]{1,0:T(8,128)(2,1)S(1)}, u32[]{:S(2)}, u32[]{:S(2)}) %collective-permute-start.24) | collective-permute-done | bytes 262176 | tf_op jit(solution)/shard_map/ppermute | solution.py:310
  90.2 3.6 %collective-permute-done.20 = bf16[64,2048]{1,0:T(8,128)(2,1)S(1)} collective-permute-done((bf16[64,2048]{1,0:T(8,128)(2,1)S(1)}, bf16[64,2048]{1,0:T(8,128)(2,1)S(1)}, u32[]{:S(2)}, u32[]{:S(2)}) %collective-permute-start.20) | collective-permute-done | bytes 262176 | tf_op jit(solution)/shard_map/ppermute | solution.py:310
  96.1 3.4 %collective-permute-done.27 = bf16[64,2048]{1,0:T(8,128)(2,1)S(1)} collective-permute-done((bf16[64,2048]{1,0:T(8,128)(2,1)S(1)}, bf16[64,2048]{1,0:T(8,128)(2,1)S(1)}, u32[]{:S(2)}, u32[]{:S(2)}) %collective-permute-start.27) | collective-permute-done | bytes 262176 | tf_op jit(solution)/shard_map/ppermute | solution.py:310
  99.5 1.7 %collective-permute-start.31 = (bf16[64,2048]{1,0:T(8,128)(2,1)S(1)}, bf16[64,2048]{1,0:T(8,128)(2,1)S(1)}, u32[]{:S(2)}, u32[]{:S(2)}) collective-permute-start(bf16[64,2048]{1,0:T(8,128)(2,1)S(1)} %add_convert_fusion.4), channel_id=1, source_target_pairs={{2,0},{4,2},{6,4},{7,6},{5,7},{3,5},{1,3},{0,1},{10,8},{12,10},{14... | collective-permute-start | bytes 786440 | tf_op jit(solution)/shard_map/ppermute | solution.py:310
  102.6 2.5 %collective-permute-done.21 = bf16[64,2048]{1,0:T(8,128)(2,1)S(1)} collective-permute-done((bf16[64,2048]{1,0:T(8,128)(2,1)S(1)}, bf16[64,2048]{1,0:T(8,128)(2,1)S(1)}, u32[]{:S(2)}, u32[]{:S(2)}) %collective-permute-start.21) | collective-permute-done | bytes 262176 | tf_op jit(solution)/shard_map/ppermute | solution.py:310
  105.1 1.7 %collective-permute-start.26 = (bf16[64,2048]{1,0:T(8,128)(2,1)S(1)}, bf16[64,2048]{1,0:T(8,128)(2,1)S(1)}, u32[]{:S(2)}, u32[]{:S(2)}) collective-permute-start(bf16[64,2048]{1,0:T(8,128)(2,1)S(1)} %add_convert_fusion.7), channel_id=1, source_target_pairs={{2,0},{4,2},{6,4},{7,6},{5,7},{3,5},{1,3},{0,1},{10,8},{12,10},{14... | collective-permute-start | bytes 786440 | tf_op jit(solution)/shard_map/ppermute | solution.py:310
  107.3 3.4 %collective-permute-done.28 = bf16[64,2048]{1,0:T(8,128)(2,1)S(1)} collective-permute-done((bf16[64,2048]{1,0:T(8,128)(2,1)S(1)}, bf16[64,2048]{1,0:T(8,128)(2,1)S(1)}, u32[]{:S(2)}, u32[]{:S(2)}) %collective-permute-start.28) | collective-permute-done | bytes 262176 | tf_op jit(solution)/shard_map/ppermute | solution.py:310
  110.7 1.7 %collective-permute-start.32 = (bf16[64,2048]{1,0:T(8,128)(2,1)S(1)}, bf16[64,2048]{1,0:T(8,128)(2,1)S(1)}, u32[]{:S(2)}, u32[]{:S(2)}) collective-permute-start(bf16[64,2048]{1,0:T(8,128)(2,1)S(1)} %add_convert_fusion.3), channel_id=1, source_target_pairs={{2,0},{4,2},{6,4},{7,6},{5,7},{3,5},{1,3},{0,1},{10,8},{12,10},{14... | collective-permute-start | bytes 786440 | tf_op jit(solution)/shard_map/ppermute | solution.py:310
  112.5 3.0 %collective-permute-done.22 = bf16[64,2048]{1,0:T(8,128)(2,1)S(1)} collective-permute-done((bf16[64,2048]{1,0:T(8,128)(2,1)S(1)}, bf16[64,2048]{1,0:T(8,128)(2,1)S(1)}, u32[]{:S(2)}, u32[]{:S(2)}) %collective-permute-start.22) | collective-permute-done | bytes 262176 | tf_op jit(solution)/shard_map/ppermute | solution.py:310
  119.6 5.0 %collective-permute-done.29 = bf16[64,2048]{1,0:T(8,128)(2,1)S(1)} collective-permute-done((bf16[64,2048]{1,0:T(8,128)(2,1)S(1)}, bf16[64,2048]{1,0:T(8,128)(2,1)S(1)}, u32[]{:S(2)}, u32[]{:S(2)}) %collective-permute-start.29) | collective-permute-done | bytes 262176 | tf_op jit(solution)/shard_map/ppermute | solution.py:310
  124.7 3.8 %collective-permute-done.23 = bf16[64,2048]{1,0:T(8,128)(2,1)S(1)} collective-permute-done((bf16[64,2048]{1,0:T(8,128)(2,1)S(1)}, bf16[64,2048]{1,0:T(8,128)(2,1)S(1)}, u32[]{:S(2)}, u32[]{:S(2)}) %collective-permute-start.23) | collective-permute-done | bytes 262176 | tf_op jit(solution)/shard_map/ppermute | solution.py:310
  (96 shorter events, 31.1 us)
Async XLA Ops:
  0.0 29.1 %collective-permute-start = (bf16[128,2048]{1,0:T(8,128)(2,1)}, bf16[128,2048]{1,0:T(8,128)(2,1)S(1)}, u32[]{:S(2)}, u32[]{:S(2)}) collective-permute-start(bf16[128,2048]{1,0:T(8,128)(2,1)} %refs_0_.1), channel_id=1, source_target_pairs={{0,8},{8,0},{16,24},{24,16},{1,9},{9,1},{17,25},{25,17},{2,10},{10... | collective-permute-start | bytes 1572872 | tf_op jit(solution)/shard_map/ppermute | solution.py:279
  0.5 23.2 %collective-permute-start.1 = (bf16[128,2048]{1,0:T(8,128)(2,1)}, bf16[128,2048]{1,0:T(8,128)(2,1)S(1)}, u32[]{:S(2)}, u32[]{:S(2)}) collective-permute-start(bf16[128,2048]{1,0:T(8,128)(2,1)} %refs_0_.1), channel_id=1, source_target_pairs={{0,16},{8,24},{16,0},{24,8},{1,17},{9,25},{17,1},{25,9},{2,18},{10... | collective-permute-start | bytes 1572872 | tf_op jit(solution)/shard_map/ppermute | solution.py:279
  4.1 16.8 %collective-permute-start.10 = (bf16[64,2048]{1,0:T(8,128)(2,1)S(1)}, bf16[64,2048]{1,0:T(8,128)(2,1)S(1)}, u32[]{:S(2)}, u32[]{:S(2)}) collective-permute-start(bf16[64,2048]{1,0:T(8,128)(2,1)S(1)} %get-tuple-element.57), channel_id=1, source_target_pairs={{2,0},{4,2},{6,4},{7,6},{5,7},{3,5},{1,3},{0,1},{10,8},{12,10},{14... | collective-permute-start | bytes 786440 | tf_op jit(solution)/shard_map/ppermute | solution.py:258
  5.6 15.7 %collective-permute-start.14 = (bf16[64,2048]{1,0:T(8,128)(2,1)S(1)}, bf16[64,2048]{1,0:T(8,128)(2,1)S(1)}, u32[]{:S(2)}, u32[]{:S(2)}) collective-permute-start(bf16[64,2048]{1,0:T(8,128)(2,1)S(1)} %get-tuple-element.57), channel_id=1, source_target_pairs={{0,2},{2,4},{4,6},{6,7},{7,5},{5,3},{3,1},{1,0},{8,10},{10,12},{12... | collective-permute-start | bytes 786440 | tf_op jit(solution)/shard_map/ppermute | solution.py:255
  6.2 13.2 %collective-permute-start.6 = (bf16[64,2048]{1,0:T(8,128)(2,1)S(1)}, bf16[64,2048]{1,0:T(8,128)(2,1)S(1)}, u32[]{:S(2)}, u32[]{:S(2)}) collective-permute-start(bf16[64,2048]{1,0:T(8,128)(2,1)S(1)} %get-tuple-element.58), channel_id=1, source_target_pairs={{0,2},{2,4},{4,6},{6,7},{7,5},{5,3},{3,1},{1,0},{8,10},{10,12},{12... | collective-permute-start | bytes 786440 | tf_op jit(solution)/shard_map/ppermute | solution.py:255
  19.4 9.2 %collective-permute-start.15 = (bf16[64,2048]{1,0:T(8,128)(2,1)S(1)}, bf16[64,2048]{1,0:T(8,128)(2,1)S(1)}, u32[]{:S(2)}, u32[]{:S(2)}) collective-permute-start(bf16[64,2048]{1,0:T(8,128)(2,1)S(1)} %get-tuple-element.58), channel_id=1, source_target_pairs={{2,0},{4,2},{6,4},{7,6},{5,7},{3,5},{1,3},{0,1},{10,8},{12,10},{14... | collective-permute-start | bytes 786440 | tf_op jit(solution)/shard_map/ppermute | solution.py:258
  20.9 10.4 %collective-permute-start.7 = (bf16[64,2048]{1,0:T(8,128)(2,1)S(1)}, bf16[64,2048]{1,0:T(8,128)(2,1)S(1)}, u32[]{:S(2)}, u32[]{:S(2)}) collective-permute-start(bf16[64,2048]{1,0:T(8,128)(2,1)S(1)} %collective-permute-done.6.refs_3_), channel_id=1, source_target_pairs={{0,2},{2,4},{4,6},{6,7},{7,5},{5,3},{3,1},{1,0},{8,10},{10,12},{12... | collective-permute-start | bytes 786440 | tf_op jit(solution)/shard_map/ppermute | solution.py:255
  21.4 12.9 %collective-permute-start.11 = (bf16[64,2048]{1,0:T(8,128)(2,1)S(1)}, bf16[64,2048]{1,0:T(8,128)(2,1)}, u32[]{:S(2)}, u32[]{:S(2)}) collective-permute-start(bf16[64,2048]{1,0:T(8,128)(2,1)S(1)} %collective-permute-done.10.refs_6_), channel_id=1, source_target_pairs={{2,0},{4,2},{6,4},{7,6},{5,7},{3,5},{1,3},{0,1},{10,8},{12,10},{14... | collective-permute-start | bytes 786440 | tf_op jit(solution)/shard_map/ppermute | solution.py:258
  23.6 32.2 %collective-permute-start.2 = (bf16[128,2048]{1,0:T(8,128)(2,1)S(1)}, bf16[128,2048]{1,0:T(8,128)(2,1)S(1)}, u32[]{:S(2)}, u32[]{:S(2)}) collective-permute-start(bf16[128,2048]{1,0:T(8,128)(2,1)S(1)} %collective-permute-done.1.first), channel_id=1, source_target_pairs={{0,8},{8,0},{16,24},{24,16},{1,9},{9,1},{17,25},{25,17},{2,10},{10... | collective-permute-start | bytes 1572872 | tf_op jit(solution)/shard_map/ppermute | solution.py:279
  28.6 12.6 %collective-permute-start.16 = (bf16[64,2048]{1,0:T(8,128)(2,1)S(1)}, bf16[64,2048]{1,0:T(8,128)(2,1)}, u32[]{:S(2)}, u32[]{:S(2)}) collective-permute-start(bf16[64,2048]{1,0:T(8,128)(2,1)S(1)} %collective-permute-done.14.refs_4_), channel_id=1, source_target_pairs={{0,2},{2,4},{4,6},{6,7},{7,5},{5,3},{3,1},{1,0},{8,10},{10,12},{12... | collective-permute-start | bytes 786440 | tf_op jit(solution)/shard_map/ppermute | solution.py:255
  29.1 14.1 %collective-permute-start.17 = (bf16[64,2048]{1,0:T(8,128)(2,1)S(1)}, bf16[64,2048]{1,0:T(8,128)(2,1)}, u32[]{:S(2)}, u32[]{:S(2)}) collective-permute-start(bf16[64,2048]{1,0:T(8,128)(2,1)S(1)} %collective-permute-done.15.refs_5_), channel_id=1, source_target_pairs={{2,0},{4,2},{6,4},{7,6},{5,7},{3,5},{1,3},{0,1},{10,8},{12,10},{14... | collective-permute-start | bytes 786440 | tf_op jit(solution)/shard_map/ppermute | solution.py:258
  31.3 11.9 %collective-permute-start.8 = (bf16[64,2048]{1,0:T(8,128)(2,1)S(1)}, bf16[64,2048]{1,0:T(8,128)(2,1)}, u32[]{:S(2)}, u32[]{:S(2)}) collective-permute-start(bf16[64,2048]{1,0:T(8,128)(2,1)S(1)} %collective-permute-done.7.refs_7_), channel_id=1, source_target_pairs={{0,2},{2,4},{4,6},{6,7},{7,5},{5,3},{3,1},{1,0},{8,10},{10,12},{12... | collective-permute-start | bytes 786440 | tf_op jit(solution)/shard_map/ppermute | solution.py:255
  34.3 11.4 %collective-permute-start.12 = (bf16[64,2048]{1,0:T(8,128)(2,1)}, bf16[64,2048]{1,0:T(8,128)(2,1)}, u32[]{:S(2)}, u32[]{:S(2)}) collective-permute-start(bf16[64,2048]{1,0:T(8,128)(2,1)} %collective-permute-done.11.refs_10_), channel_id=1, source_target_pairs={{2,0},{4,2},{6,4},{7,6},{5,7},{3,5},{1,3},{0,1},{10,8},{12,10},{14... | collective-permute-start | bytes 786440 | tf_op jit(solution)/shard_map/ppermute | solution.py:258
  36.5 26.7 %all-to-all-start = ((f32[8,8,128]{2,1,0:T(8,128)}), f32[8,8,128]{2,1,0:T(8,128)S(1)}, u32[]{:S(2)}, u32[]{:S(2)}) async-start(f32[8,8,128]{2,1,0:T(8,128)} %bitcast.20), calls=%async_computation | async-start | bytes 65536 | tf_op jit(solution)/shard_map/all_to_all | solution.py:263
  41.2 22.1 %collective-permute-start.18 = (bf16[64,2048]{1,0:T(8,128)(2,1)}, bf16[64,2048]{1,0:T(8,128)(2,1)}, u32[]{:S(2)}, u32[]{:S(2)}) collective-permute-start(bf16[64,2048]{1,0:T(8,128)(2,1)} %collective-permute-done.16.refs_8_), channel_id=1, source_target_pairs={{0,2},{2,4},{4,6},{6,7},{7,5},{5,3},{3,1},{1,0},{8,10},{10,12},{12... | collective-permute-start | bytes 786440 | tf_op jit(solution)/shard_map/ppermute | solution.py:255
  43.2 20.1 %collective-permute-start.19 = (bf16[64,2048]{1,0:T(8,128)(2,1)}, bf16[64,2048]{1,0:T(8,128)(2,1)}, u32[]{:S(2)}, u32[]{:S(2)}) collective-permute-start(bf16[64,2048]{1,0:T(8,128)(2,1)} %collective-permute-done.17.refs_9_), channel_id=1, source_target_pairs={{2,0},{4,2},{6,4},{7,6},{5,7},{3,5},{1,3},{0,1},{10,8},{12,10},{14... | collective-permute-start | bytes 786440 | tf_op jit(solution)/shard_map/ppermute | solution.py:258
  43.3 20.0 %collective-permute-start.9 = (bf16[64,2048]{1,0:T(8,128)(2,1)}, bf16[64,2048]{1,0:T(8,128)(2,1)}, u32[]{:S(2)}, u32[]{:S(2)}) collective-permute-start(bf16[64,2048]{1,0:T(8,128)(2,1)} %collective-permute-done.8.refs_11_), channel_id=1, source_target_pairs={{0,2},{2,4},{4,6},{6,7},{7,5},{5,3},{3,1},{1,0},{8,10},{10,12},{12... | collective-permute-start | bytes 786440 | tf_op jit(solution)/shard_map/ppermute | solution.py:255
  45.8 17.5 %collective-permute-start.13 = (bf16[64,2048]{1,0:T(8,128)(2,1)}, bf16[64,2048]{1,0:T(8,128)(2,1)}, u32[]{:S(2)}, u32[]{:S(2)}) collective-permute-start(bf16[64,2048]{1,0:T(8,128)(2,1)} %collective-permute-done.12.refs_14_), channel_id=1, source_target_pairs={{2,0},{4,2},{6,4},{7,6},{5,7},{3,5},{1,3},{0,1},{10,8},{12,10},{14... | collective-permute-start | bytes 786440 | tf_op jit(solution)/shard_map/ppermute | solution.py:258
  84.2 17.1 %collective-permute-start.4 = (bf16[128,2048]{1,0:T(8,128)(2,1)S(1)}, bf16[128,2048]{1,0:T(8,128)(2,1)S(1)}, u32[]{:S(2)}, u32[]{:S(2)}) collective-permute-start(bf16[128,2048]{1,0:T(8,128)(2,1)S(1)} %copy-done.15), channel_id=1, source_target_pairs={{0,8},{8,0},{16,24},{24,16},{1,9},{9,1},{17,25},{25,17},{2,10},{10... | collective-permute-start | bytes 1572872 | tf_op jit(solution)/shard_map/ppermute | solution.py:298
  84.2 33.8 %collective-permute-start.3 = (bf16[128,2048]{1,0:T(8,128)(2,1)S(1)}, bf16[128,2048]{1,0:T(8,128)(2,1)S(1)}, u32[]{:S(2)}, u32[]{:S(2)}) collective-permute-start(bf16[128,2048]{1,0:T(8,128)(2,1)S(1)} %copy-done.13), channel_id=1, source_target_pairs={{0,8},{8,0},{16,24},{24,16},{1,9},{9,1},{17,25},{25,17},{2,10},{10... | collective-permute-start | bytes 1572872 | tf_op jit(solution)/shard_map/ppermute | solution.py:298
  84.7 9.2 %collective-permute-start.20 = (bf16[64,2048]{1,0:T(8,128)(2,1)S(1)}, bf16[64,2048]{1,0:T(8,128)(2,1)S(1)}, u32[]{:S(2)}, u32[]{:S(2)}) collective-permute-start(bf16[64,2048]{1,0:T(8,128)(2,1)S(1)} %get-tuple-element.40), channel_id=1, source_target_pairs={{0,2},{2,4},{4,6},{6,7},{7,5},{5,3},{3,1},{1,0},{8,10},{10,12},{12... | collective-permute-start | bytes 786440 | tf_op jit(solution)/shard_map/ppermute | solution.py:310
  84.7 10.3 %collective-permute-start.30 = (bf16[64,2048]{1,0:T(8,128)(2,1)S(1)}, bf16[64,2048]{1,0:T(8,128)(2,1)S(1)}, u32[]{:S(2)}, u32[]{:S(2)}) collective-permute-start(bf16[64,2048]{1,0:T(8,128)(2,1)S(1)} %get-tuple-element.51), channel_id=1, source_target_pairs={{2,0},{4,2},{6,4},{7,6},{5,7},{3,5},{1,3},{0,1},{10,8},{12,10},{14... | collective-permute-start | bytes 786440 | tf_op jit(solution)/shard_map/ppermute | solution.py:310
  89.4 10.0 %collective-permute-start.27 = (bf16[64,2048]{1,0:T(8,128)(2,1)S(1)}, bf16[64,2048]{1,0:T(8,128)(2,1)S(1)}, u32[]{:S(2)}, u32[]{:S(2)}) collective-permute-start(bf16[64,2048]{1,0:T(8,128)(2,1)S(1)} %get-tuple-element.48), channel_id=1, source_target_pairs={{0,2},{2,4},{4,6},{6,7},{7,5},{5,3},{3,1},{1,0},{8,10},{10,12},{12... | collective-permute-start | bytes 786440 | tf_op jit(solution)/shard_map/ppermute | solution.py:310
  93.8 7.9 %collective-permute-start.25 = (bf16[64,2048]{1,0:T(8,128)(2,1)S(1)}, bf16[64,2048]{1,0:T(8,128)(2,1)S(1)}, u32[]{:S(2)}, u32[]{:S(2)}) collective-permute-start(bf16[64,2048]{1,0:T(8,128)(2,1)S(1)} %add_convert_fusion.8), channel_id=1, source_target_pairs={{2,0},{4,2},{6,4},{7,6},{5,7},{3,5},{1,3},{0,1},{10,8},{12,10},{14... | collective-permute-start | bytes 786440 | tf_op jit(solution)/shard_map/ppermute | solution.py:310
  95.0 10.1 %collective-permute-start.21 = (bf16[64,2048]{1,0:T(8,128)(2,1)S(1)}, bf16[64,2048]{1,0:T(8,128)(2,1)S(1)}, u32[]{:S(2)}, u32[]{:S(2)}) collective-permute-start(bf16[64,2048]{1,0:T(8,128)(2,1)S(1)} %add_convert_fusion.11), channel_id=1, source_target_pairs={{0,2},{2,4},{4,6},{6,7},{7,5},{5,3},{3,1},{1,0},{8,10},{10,12},{12... | collective-permute-start | bytes 786440 | tf_op jit(solution)/shard_map/ppermute | solution.py:310
  101.3 9.4 %collective-permute-start.28 = (bf16[64,2048]{1,0:T(8,128)(2,1)S(1)}, bf16[64,2048]{1,0:T(8,128)(2,1)S(1)}, u32[]{:S(2)}, u32[]{:S(2)}) collective-permute-start(bf16[64,2048]{1,0:T(8,128)(2,1)S(1)} %add_convert_fusion.6), channel_id=1, source_target_pairs={{0,2},{2,4},{4,6},{6,7},{7,5},{5,3},{3,1},{1,0},{8,10},{10,12},{12... | collective-permute-start | bytes 786440 | tf_op jit(solution)/shard_map/ppermute | solution.py:310
  101.8 17.7 %collective-permute-start.5 = (bf16[128,2048]{1,0:T(8,128)(2,1)S(1)}, bf16[128,2048]{1,0:T(8,128)(2,1)S(1)}, u32[]{:S(2)}, u32[]{:S(2)}) collective-permute-start(bf16[128,2048]{1,0:T(8,128)(2,1)S(1)} %add_convert_fusion), channel_id=1, source_target_pairs={{0,16},{8,24},{16,0},{24,8},{1,17},{9,25},{17,1},{25,9},{2,18},{10... | collective-permute-start | bytes 1572872 | tf_op jit(solution)/shard_map/ppermute | solution.py:298
  105.1 14.6 %collective-permute-start.26 = (bf16[64,2048]{1,0:T(8,128)(2,1)S(1)}, bf16[64,2048]{1,0:T(8,128)(2,1)S(1)}, u32[]{:S(2)}, u32[]{:S(2)}) collective-permute-start(bf16[64,2048]{1,0:T(8,128)(2,1)S(1)} %add_convert_fusion.7), channel_id=1, source_target_pairs={{2,0},{4,2},{6,4},{7,6},{5,7},{3,5},{1,3},{0,1},{10,8},{12,10},{14... | collective-permute-start | bytes 786440 | tf_op jit(solution)/shard_map/ppermute | solution.py:310
  106.9 8.6 %collective-permute-start.22 = (bf16[64,2048]{1,0:T(8,128)(2,1)S(1)}, bf16[64,2048]{1,0:T(8,128)(2,1)S(1)}, u32[]{:S(2)}, u32[]{:S(2)}) collective-permute-start(bf16[64,2048]{1,0:T(8,128)(2,1)S(1)} %add_convert_fusion.10), channel_id=1, source_target_pairs={{0,2},{2,4},{4,6},{6,7},{7,5},{5,3},{3,1},{1,0},{8,10},{10,12},{12... | collective-permute-start | bytes 786440 | tf_op jit(solution)/shard_map/ppermute | solution.py:310
  115.4 9.2 %collective-permute-start.29 = (bf16[64,2048]{1,0:T(8,128)(2,1)S(1)}, bf16[64,2048]{1,0:T(8,128)(2,1)S(1)}, u32[]{:S(2)}, u32[]{:S(2)}) collective-permute-start(bf16[64,2048]{1,0:T(8,128)(2,1)S(1)} %add_convert_fusion.5), channel_id=1, source_target_pairs={{0,2},{2,4},{4,6},{6,7},{7,5},{5,3},{3,1},{1,0},{8,10},{10,12},{12... | collective-permute-start | bytes 786440 | tf_op jit(solution)/shard_map/ppermute | solution.py:310
  117.3 11.2 %collective-permute-start.23 = (bf16[64,2048]{1,0:T(8,128)(2,1)S(1)}, bf16[64,2048]{1,0:T(8,128)(2,1)S(1)}, u32[]{:S(2)}, u32[]{:S(2)}) collective-permute-start(bf16[64,2048]{1,0:T(8,128)(2,1)S(1)} %add_convert_fusion.9), channel_id=1, source_target_pairs={{0,2},{2,4},{4,6},{6,7},{7,5},{5,3},{3,1},{1,0},{8,10},{10,12},{12... | collective-permute-start | bytes 786440 | tf_op jit(solution)/shard_map/ppermute | solution.py:310
  117.9 10.6 %collective-permute-start.33 = (bf16[64,2048]{1,0:T(8,128)(2,1)S(1)}, bf16[64,2048]{1,0:T(8,128)(2,1)S(1)}, u32[]{:S(2)}, u32[]{:S(2)}) collective-permute-start(bf16[64,2048]{1,0:T(8,128)(2,1)S(1)} %add_convert_fusion.2), channel_id=1, source_target_pairs={{2,0},{4,2},{6,4},{7,6},{5,7},{3,5},{1,3},{0,1},{10,8},{12,10},{14... | collective-permute-start | bytes 786440 | tf_op jit(solution)/shard_map/ppermute | solution.py:310
  (19 other events, 138.3 us)

commit v4 on v3

--- a/solution.py
+++ b/solution.py
@@ -9,6 +9,7 @@
 
 HOT_SLOTS = 40
 SLOTS = 24
+SHARED_COST = 1000
 EXTRA = HOT_SLOTS - SLOTS
 BF16 = jnp.bfloat16
 F32 = jnp.float32
@@ -193,33 +194,65 @@
     )(idx, meta, *flat, *weights)
 
 
-def shared_kernel(first, second, w_gate, w_up, w_down, out_first, out_second):
-    tokens = jnp.concatenate([first[...], second[...]], axis=0)
-    gate = dot(tokens, w_gate[...])
-    upper = dot(tokens, w_up[...])
+def shared_kernel(count, *refs):
+    blocks, weights, outs = refs[:count], refs[count : count + 3], refs[count + 3 : count + 5]
+    x, wg, wu, wd, out, sem = refs[count + 5 :]
+    rows = blocks[0].shape[0]
+    loads = [
+        pltpu.make_async_copy(block, x.at[pl.ds(i * rows, rows)], sem.at[i]) for i, block in enumerate(blocks)
+    ]
+    loads += [
+        pltpu.make_async_copy(source, target, sem.at[count + k])
+        for k, (source, target) in enumerate(zip(weights, (wg, wu, wd)))
+    ]
+    for copy in loads:
+        copy.start()
+    for copy in loads[:-2]:
+        copy.wait()
+    gate = dot(x[...], wg[...])
+    loads[-2].wait()
+    upper = dot(x[...], wu[...])
     hidden = (gate / (1.0 + jnp.exp(-gate)) * upper).astype(BF16)
-    out = dot(hidden, w_down[...]).astype(BF16)
-    rows = first.shape[0]
-    out_first[...] = out[:rows]
-    out_second[...] = out[rows:]
-
-
-def run_shared(first, second, w_gate, w_up, w_down):
-    rows, width = first.shape
-    hidden = w_gate.shape[1]
+    loads[-1].wait()
+    half = count * rows // 2
+    stores = []
+    for i in (1, 0):
+        out[i] = dot(hidden[i * half : (i + 1) * half], wd[...]).astype(BF16)
+        stores.append(pltpu.make_async_copy(out.at[i], outs[i], sem.at[count + 3 + i]))
+        stores[-1].start()
+    for copy in stores:
+        copy.wait()
+
+
+def run_shared(blocks, weights):
+    count = len(blocks)
+    rows, width = blocks[0].shape
+    hidden = weights[0].shape[1]
+    blocks = [pltpu.with_memory_space_constraint(block, pltpu.HBM) for block in blocks]
+    weights = [pltpu.with_memory_space_constraint(w, pltpu.HBM) for w in weights]
     return pl.pallas_call(
-        shared_kernel,
-        out_shape=[jax.ShapeDtypeStruct((rows, width), BF16)] * 2,
-        in_specs=[VMEM] * 5,
-        out_specs=[VMEM] * 2,
+        functools.partial(shared_kernel, count),
+        out_shape=[pltpu.HBM((count * rows // 2, width), BF16)] * 2,
+        in_specs=[HBM] * (count + 3),
+        out_specs=[HBM] * 2,
+        scratch_shapes=[
+            pltpu.VMEM((count * rows, width), BF16),
+            pltpu.VMEM((width, hidden), BF16),
+            pltpu.VMEM((width, hidden), BF16),
+            pltpu.VMEM((hidden, width), BF16),
+            pltpu.VMEM((2, count * rows // 2, width), BF16),
+            pltpu.SemaphoreType.DMA((count + 5,)),
+        ],
         cost_estimate=pl.CostEstimate(
-            flops=2 * 3 * 2 * rows * width * hidden,
-            transcendentals=2 * rows * hidden,
-            bytes_accessed=2 * (3 * width * hidden + 4 * rows * width),
+            flops=SHARED_COST, transcendentals=0, bytes_accessed=SHARED_COST,
         ),
-        compiler_params=pltpu.CompilerParams(vmem_limit_bytes=16 << 20),
+        compiler_params=pltpu.CompilerParams(vmem_limit_bytes=26 << 20),
         name="shared_experts",
-    )(first, second, w_gate, w_up, w_down)
+    )(*blocks, *weights)
+
+
+def tied(values, anchors):
+    return lax.optimization_barrier((tuple(values), tuple(anchors)))[0]
 
 
 def on_device(
@@ -246,19 +279,6 @@
     backward = [(b, a) for a, b in forward]
     mid = count // 2
 
-    own = [latents[:half], latents[half:]]
-    blocks = {o: [None, None] for o in range(count)}
-    for h in range(2):
-        up, down = own[h], own[h]
-        for hop in range(1, mid + 1):
-            if hop < mid or h == 0:
-                up = lax.ppermute(up, "expert", forward)
-                blocks[hop][h] = up
-            if hop < mid or h == 1:
-                down = lax.ppermute(down, "expert", backward)
-                blocks[count - hop][h] = down
-    blocks[0] = [latents]
-
     info = routing(expert_ids, gate_weights, capacity, hot_expert, experts)
     meta = lax.all_to_all(
         info.reshape(count, 2 * local, tokens), "expert", split_axis=0, concat_axis=0, tiled=True
@@ -272,33 +292,46 @@
     idx = jnp.concatenate([idx, (hot_expert - me * local).astype(jnp.int32)])
 
     bits = [1 << b for b in range(n_dp.bit_length() - 1)]
-    near = {0: latents}
-    for bit in reversed(bits):
+    blocks = {o: [None, None] for o in range(count)}
+    up, down = [latents[:half], latents[half:]], [latents[:half], latents[half:]]
+    for hop in range(1, mid + 1):
+        for h in range(2):
+            if hop < mid or h == 0:
+                up[h] = lax.ppermute(up[h], "expert", forward)
+                blocks[hop][h] = up[h]
+            if hop < mid or h == 1:
+                down[h] = lax.ppermute(down[h], "expert", backward)
+                blocks[count - hop][h] = down[h]
+    blocks[0] = [latents]
+    mine = [latents]
+    for bit in reversed(bits[1:]):
         swap = [(d, d ^ bit) for d in range(n_dp)]
-        for r in list(near):
-            near[r ^ bit] = lax.ppermute(near[r], "dp", swap)
-    part = {}
-    for r in range(0, n_dp, 2):
-        part[r], part[r + 1] = run_shared(near[r], near[r + 1], shared_gate, shared_up, shared_down)
+        mine += [lax.ppermute(block, "dp", swap) for block in mine]
+    mine = jnp.concatenate(mine, axis=0)
+    swap = [(d, d ^ 1) for d in range(n_dp)]
+    keep, give = run_shared([mine, lax.ppermute(mine, "dp", swap)], (shared_gate, shared_up, shared_down))
+    (idx,), (keep, give) = lax.optimization_barrier(((idx,), (keep, give)))
+    shared = keep.astype(F32) + lax.ppermute(give, "dp", swap).astype(F32)
+    where = [0]
+    for bit in reversed(bits[1:]):
+        where += [r ^ bit for r in where]
+    part = {r: shared[i * tokens : (i + 1) * tokens] for i, r in enumerate(where)}
+    for bit in bits[1:]:
+        swap = [(d, d ^ bit) for d in range(n_dp)]
+        for r in sorted(part):
+            if r & bit:
+                came = lax.ppermute(part.pop(r).astype(BF16), "dp", swap)
+                part[r ^ bit] = part[r ^ bit] + came.astype(F32)
+    shared = part[0]
+
     weights = [jnp.swapaxes(w_gate, 1, 2), jnp.swapaxes(w_up, 1, 2), w_down]
     order = offsets_of(count)
-    idx, *kept = lax.optimization_barrier((idx, *part.values()))
-    part = dict(zip(part, kept))
     done = {}
     for at in range(0, count, 8):
         chunk = tuple(order[at : at + 8])
         flat = run_experts(chunk, local, idx, meta, blocks, weights)
         for i, o in enumerate(chunk):
             done[o] = [flat[2 * i], flat[2 * i + 1]]
-
-    for bit in bits:
-        swap = [(d, d ^ bit) for d in range(n_dp)]
-        for r in sorted(part):
-            if r & bit:
-                came = lax.ppermute(part.pop(r), "dp", swap)
-                total = part[r ^ bit].astype(F32) + came.astype(F32)
-                part[r ^ bit] = total if bit == bits[-1] else total.astype(BF16)
-    shared = part[0]
 
     result = []
     for h in range(2):

time: 130 us -> 115 us (0.88)
  local copies, waits for them, and re-layouts: 19.7 us -> 5.21 us
  Pallas kernels: 20.4 us -> 24.2 us
  starting transfers between devices: 40.5 us -> 37.9 us
  waiting for transfers between devices: 45.2 us -> 43.6 us
    unnamed x32 -> x13, local copies, waits for them, and re-layouts: 15.5 us -> 1.9 us
    ppermute x14, waiting for transfers between devices: 28.9 us -> 21.8 us  [on_device(): came = lax.ppermute(acc, 'expert', perm)]
    ppermute x20 -> x18, waiting for transfers between devices: 16.3 us -> 21.8 us  [the longest x7 16 us: on_device(): up[h] = lax.ppermute(up[h], 'expert', forward)]
    ppermute x20 -> x18, starting transfers between devices: 21.3 us -> 17.3 us  [the longest x7 11.1 us: on_device(): up[h] = lax.ppermute(up[h], 'expert', forward)]
    pallas_call x2 -> x1, Pallas kernels: 3.73 us -> 7.13 us  [run_shared(): pl.pallas_call(functools.partial(shared_kernel, count), out_shape=[pltpu....]
    all_to_all x1, starting transfers between devices: 3.87 us -> 5.81 us  [on_device(): lax.all_to_all(info.reshape(count, 2 * local, tokens), 'expert', split_ax...]
  transfers between devices with their start and end apart: 35 -> 33, of which waited for: 13 -> 17; matrix products, arithmetic and copies ran while one was open for 5% -> 6% of each run, Pallas kernels for 3% -> 6%
where the time goes in v4:
time: 115 us; the launch traced here: 114 us
  waiting for transfers between devices  43.6 us (38%)
  starting transfers between devices  37.9 us (33%)
  Pallas kernels  24.2 us (21%)
  local copies, waits for them, and re-layouts  5.21 us (5%)
  other arithmetic  2.35 us (2%)
    ppermute x14, waiting for transfers between devices, on_device(): came = lax.ppermute(acc, 'expert', perm)  21.8 us
    pallas_call x1, Pallas kernels, run_experts(): pl.pallas_call(functools.partial(experts_kernel, offsets, sizes, local, b...  17.1 us
    ppermute x7, waiting for transfers between devices, on_device(): up[h] = lax.ppermute(up[h], 'expert', forward)  16 us
    ppermute x14, starting transfers between devices, on_device(): came = lax.ppermute(acc, 'expert', perm)  14.8 us
    ppermute x7, starting transfers between devices, on_device(): up[h] = lax.ppermute(up[h], 'expert', forward)  11.1 us
    pallas_call x1, Pallas kernels, run_shared(): pl.pallas_call(functools.partial(shared_kernel, count), out_shape=[pltpu....  7.13 us
    all_to_all x1, starting transfers between devices, on_device(): lax.all_to_all(info.reshape(count, 2 * local, tokens), 'expert', split_ax...  5.81 us
    ppermute x1, waiting for transfers between devices, on_device(): came = lax.ppermute(part.pop(r).astype(BF16), 'dp', swap)  5.73 us
  transfers between devices with their start and end apart: 33, of which 17 were waited for; matrix products, arithmetic and copies ran while one was open for 6% of the time, Pallas kernels for 6%

profile of v4, /device:TPU:0, one launch (start us, length us, event | category | flops | bytes accessed | tf_op | source)
XLA Modules:
  0.0 114.2 jit_solution(1684610564136744018)
XLA Ops:
  0.0 3.0 %collective-permute-start = (bf16[128,2048]{1,0:T(8,128)(2,1)}, bf16[128,2048]{1,0:T(8,128)(2,1)S(1)}, u32[]{:S(2)}, u32[]{:S(2)}) collective-permute-start(bf16[128,2048]{1,0:T(8,128)(2,1)} %refs_0_.1), channel_id=1, source_target_pairs={{0,16},{8,24},{16,0},{24,8},{1,17},{9,25},{17,1},{25,9},{2,18},{10... | collective-permute-start | bytes 1572872 | tf_op jit(solution)/shard_map/ppermute | solution.py:309
  4.1 1.6 %collective-permute-start.4 = (bf16[64,2048]{1,0:T(8,128)(2,1)S(1)}, bf16[64,2048]{1,0:T(8,128)(2,1)S(1)}, u32[]{:S(2)}, u32[]{:S(2)}) collective-permute-start(bf16[64,2048]{1,0:T(8,128)(2,1)S(1)} %get-tuple-element.50), channel_id=1, source_target_pairs={{0,2},{2,4},{4,6},{6,7},{7,5},{5,3},{3,1},{1,0},{8,10},{10,12},{12... | collective-permute-start | bytes 786440 | tf_op jit(solution)/shard_map/ppermute | solution.py:300
  6.2 1.6 %collective-permute-start.12 = (bf16[64,2048]{1,0:T(8,128)(2,1)S(1)}, bf16[64,2048]{1,0:T(8,128)(2,1)S(1)}, u32[]{:S(2)}, u32[]{:S(2)}) collective-permute-start(bf16[64,2048]{1,0:T(8,128)(2,1)S(1)} %get-tuple-element.49), channel_id=1, source_target_pairs={{0,2},{2,4},{4,6},{6,7},{7,5},{5,3},{3,1},{1,0},{8,10},{10,12},{12... | collective-permute-start | bytes 786440 | tf_op jit(solution)/shard_map/ppermute | solution.py:300
  8.2 1.9 %constant_dynamic-update-slice_fusion.1 = bf16[256,2048]{1,0:T(8,128)(2,1)} fusion(bf16[128,2048]{1,0:T(8,128)(2,1)} %refs_0_.1), kind=kLoop, calls=%fused_computation.40 | loop fusion | bytes 1048576
  10.1 3.3 %collective-permute-done.4.refs_3_ = bf16[64,2048]{1,0:T(8,128)(2,1)S(1)} collective-permute-done((bf16[64,2048]{1,0:T(8,128)(2,1)S(1)}, bf16[64,2048]{1,0:T(8,128)(2,1)S(1)}, u32[]{:S(2)}, u32[]{:S(2)}) %collective-permute-start.4) | collective-permute-done | bytes 262176 | tf_op jit(solution)/shard_map/ppermute | solution.py:300
  13.4 1.6 %collective-permute-start.5 = (bf16[64,2048]{1,0:T(8,128)(2,1)S(1)}, bf16[64,2048]{1,0:T(8,128)(2,1)S(1)}, u32[]{:S(2)}, u32[]{:S(2)}) collective-permute-start(bf16[64,2048]{1,0:T(8,128)(2,1)S(1)} %collective-permute-done.4.refs_3_), channel_id=1, source_target_pairs={{0,2},{2,4},{4,6},{6,7},{7,5},{5,3},{3,1},{1,0},{8,10},{10,12},{12... | collective-permute-start | bytes 786440 | tf_op jit(solution)/shard_map/ppermute | solution.py:300
  17.0 2.0 %collective-permute-done.12.refs_4_ = bf16[64,2048]{1,0:T(8,128)(2,1)S(1)} collective-permute-done((bf16[64,2048]{1,0:T(8,128)(2,1)S(1)}, bf16[64,2048]{1,0:T(8,128)(2,1)S(1)}, u32[]{:S(2)}, u32[]{:S(2)}) %collective-permute-start.12) | collective-permute-done | bytes 262176 | tf_op jit(solution)/shard_map/ppermute | solution.py:300
  19.0 1.6 %collective-permute-start.14 = (bf16[64,2048]{1,0:T(8,128)(2,1)S(1)}, bf16[64,2048]{1,0:T(8,128)(2,1)S(1)}, u32[]{:S(2)}, u32[]{:S(2)}) collective-permute-start(bf16[64,2048]{1,0:T(8,128)(2,1)S(1)} %collective-permute-done.12.refs_4_), channel_id=1, source_target_pairs={{0,2},{2,4},{4,6},{6,7},{7,5},{5,3},{3,1},{1,0},{8,10},{10,12},{12... | collective-permute-start | bytes 786440 | tf_op jit(solution)/shard_map/ppermute | solution.py:300
  21.1 3.6 %collective-permute-done.5.refs_7_ = bf16[64,2048]{1,0:T(8,128)(2,1)S(1)} collective-permute-done((bf16[64,2048]{1,0:T(8,128)(2,1)S(1)}, bf16[64,2048]{1,0:T(8,128)(2,1)S(1)}, u32[]{:S(2)}, u32[]{:S(2)}) %collective-permute-start.5) | collective-permute-done | bytes 262176 | tf_op jit(solution)/shard_map/ppermute | solution.py:300
  24.6 1.6 %collective-permute-start.6 = (bf16[64,2048]{1,0:T(8,128)(2,1)S(1)}, bf16[64,2048]{1,0:T(8,128)(2,1)S(1)}, u32[]{:S(2)}, u32[]{:S(2)}) collective-permute-start(bf16[64,2048]{1,0:T(8,128)(2,1)S(1)} %collective-permute-done.5.refs_7_), channel_id=1, source_target_pairs={{0,2},{2,4},{4,6},{6,7},{7,5},{5,3},{3,1},{1,0},{8,10},{10,12},{12... | collective-permute-start | bytes 786440 | tf_op jit(solution)/shard_map/ppermute | solution.py:300
  26.8 3.5 %collective-permute-done.14.refs_8_ = bf16[64,2048]{1,0:T(8,128)(2,1)S(1)} collective-permute-done((bf16[64,2048]{1,0:T(8,128)(2,1)S(1)}, bf16[64,2048]{1,0:T(8,128)(2,1)S(1)}, u32[]{:S(2)}, u32[]{:S(2)}) %collective-permute-start.14) | collective-permute-done | bytes 262176 | tf_op jit(solution)/shard_map/ppermute | solution.py:300
  30.2 1.6 %collective-permute-start.16 = (bf16[64,2048]{1,0:T(8,128)(2,1)S(1)}, bf16[64,2048]{1,0:T(8,128)(2,1)S(1)}, u32[]{:S(2)}, u32[]{:S(2)}) collective-permute-start(bf16[64,2048]{1,0:T(8,128)(2,1)S(1)} %collective-permute-done.14.refs_8_), channel_id=1, source_target_pairs={{0,2},{2,4},{4,6},{6,7},{7,5},{5,3},{3,1},{1,0},{8,10},{10,12},{12... | collective-permute-start | bytes 786440 | tf_op jit(solution)/shard_map/ppermute | solution.py:300
  32.3 3.6 %collective-permute-done.6.refs_11_ = bf16[64,2048]{1,0:T(8,128)(2,1)S(1)} collective-permute-done((bf16[64,2048]{1,0:T(8,128)(2,1)S(1)}, bf16[64,2048]{1,0:T(8,128)(2,1)S(1)}, u32[]{:S(2)}, u32[]{:S(2)}) %collective-permute-start.6) | collective-permute-done | bytes 262176 | tf_op jit(solution)/shard_map/ppermute | solution.py:300
  35.9 1.6 %collective-permute-start.7 = (bf16[64,2048]{1,0:T(8,128)(2,1)S(1)}, bf16[64,2048]{1,0:T(8,128)(2,1)}, u32[]{:S(2)}, u32[]{:S(2)}) collective-permute-start(bf16[64,2048]{1,0:T(8,128)(2,1)S(1)} %collective-permute-done.6.refs_11_), channel_id=1, source_target_pairs={{0,2},{2,4},{4,6},{6,7},{7,5},{5,3},{3,1},{1,0},{8,10},{10,12},{12... | collective-permute-start | bytes 786440 | tf_op jit(solution)/shard_map/ppermute | solution.py:300
  38.6 5.8 %all-to-all-start = ((f32[8,8,128]{2,1,0:T(8,128)}), f32[8,8,128]{2,1,0:T(8,128)S(1)}, u32[]{:S(2)}, u32[]{:S(2)}) async-start(f32[8,8,128]{2,1,0:T(8,128)} %bitcast.20), calls=%async_computation | async-start | bytes 65536 | tf_op jit(solution)/shard_map/all_to_all | solution.py:283
  45.1 7.1 %shared_experts.1 = (bf16[256,2048]{1,0:T(8,128)(2,1)}, bf16[256,2048]{1,0:T(8,128)(2,1)}) custom-call(bf16[256,2048]{1,0:T(8,128)(2,1)} %constant_dynamic-update-slice_fusion.refs_0_, bf16[256,2048]{1,0:T(8,128)(2,1)} %collective-permute-done.1.refs_1_, bf16[2048,512]{1,0:T(8,128)(2,1)} %refs_2_.1, bf16[2048,512]{1,0:T(8,128)(2,1)} %refs_3_.1, ...), custom_call_target="tpu_custom_call" | custom-call | flops 1000 | bytes 1000 | tf_op jit(solution)/shard_map/shared_experts/pallas_call | solution.py:233
  52.3 17.1 %routed_experts.1 = (bf16[64,2048]{1,0:T(8,128)(2,1)S(1)}, bf16[64,2048]{1,0:T(8,128)(2,1)S(1)}, bf16[64,2048]{1,0:T(8,128)(2,1)S(1)}, bf16[64,2048]{1,0:T(8,128...) custom-call(s32[9]{0:T(128)S(1)} %pad_add_fusion.idx, ...), custom_call_target="tpu_custom_call" | custom-call | flops 8522825728 | bytes 34603008 | tf_op jit(solution)/shard_map/routed_experts/pallas_call | solution.py:172
  69.4 1.2 %collective-permute-start.22 = (bf16[64,2048]{1,0:T(8,128)(2,1)S(1)}, bf16[64,2048]{1,0:T(8,128)(2,1)S(1)}, u32[]{:S(2)}, u32[]{:S(2)}) collective-permute-start(bf16[64,2048]{1,0:T(8,128)(2,1)S(1)} %get-tuple-element.36), channel_id=1, source_target_pairs={{2,0},{4,2},{6,4},{7,6},{5,7},{3,5},{1,3},{0,1},{10,8},{12,10},{14... | collective-permute-start | bytes 786440 | tf_op jit(solution)/shard_map/ppermute | solution.py:343
  71.5 1.2 %collective-permute-start.28 = (bf16[64,2048]{1,0:T(8,128)(2,1)S(1)}, bf16[64,2048]{1,0:T(8,128)(2,1)S(1)}, u32[]{:S(2)}, u32[]{:S(2)}) collective-permute-start(bf16[64,2048]{1,0:T(8,128)(2,1)S(1)} %get-tuple-element.43), channel_id=1, source_target_pairs={{2,0},{4,2},{6,4},{7,6},{5,7},{3,5},{1,3},{0,1},{10,8},{12,10},{14... | collective-permute-start | bytes 786440 | tf_op jit(solution)/shard_map/ppermute | solution.py:343
  73.5 3.8 %collective-permute-done.22 = bf16[64,2048]{1,0:T(8,128)(2,1)S(1)} collective-permute-done((bf16[64,2048]{1,0:T(8,128)(2,1)S(1)}, bf16[64,2048]{1,0:T(8,128)(2,1)S(1)}, u32[]{:S(2)}, u32[]{:S(2)}) %collective-permute-start.22) | collective-permute-done | bytes 262176 | tf_op jit(solution)/shard_map/ppermute | solution.py:343
  77.4 1.2 %collective-permute-start.23 = (bf16[64,2048]{1,0:T(8,128)(2,1)S(1)}, bf16[64,2048]{1,0:T(8,128)(2,1)S(1)}, u32[]{:S(2)}, u32[]{:S(2)}) collective-permute-start(bf16[64,2048]{1,0:T(8,128)(2,1)S(1)} %add_convert_fusion.6), channel_id=1, source_target_pairs={{2,0},{4,2},{6,4},{7,6},{5,7},{3,5},{1,3},{0,1},{10,8},{12,10},{14... | collective-permute-start | bytes 786440 | tf_op jit(solution)/shard_map/ppermute | solution.py:343
  80.7 2.2 %collective-permute-done.28 = bf16[64,2048]{1,0:T(8,128)(2,1)S(1)} collective-permute-done((bf16[64,2048]{1,0:T(8,128)(2,1)S(1)}, bf16[64,2048]{1,0:T(8,128)(2,1)S(1)}, u32[]{:S(2)}, u32[]{:S(2)}) %collective-permute-start.28) | collective-permute-done | bytes 262176 | tf_op jit(solution)/shard_map/ppermute | solution.py:343
  83.0 1.2 %collective-permute-start.29 = (bf16[64,2048]{1,0:T(8,128)(2,1)S(1)}, bf16[64,2048]{1,0:T(8,128)(2,1)S(1)}, u32[]{:S(2)}, u32[]{:S(2)}) collective-permute-start(bf16[64,2048]{1,0:T(8,128)(2,1)S(1)} %add_convert_fusion.2), channel_id=1, source_target_pairs={{2,0},{4,2},{6,4},{7,6},{5,7},{3,5},{1,3},{0,1},{10,8},{12,10},{14... | collective-permute-start | bytes 786440 | tf_op jit(solution)/shard_map/ppermute | solution.py:343
  86.3 2.2 %collective-permute-done.23 = bf16[64,2048]{1,0:T(8,128)(2,1)S(1)} collective-permute-done((bf16[64,2048]{1,0:T(8,128)(2,1)S(1)}, bf16[64,2048]{1,0:T(8,128)(2,1)S(1)}, u32[]{:S(2)}, u32[]{:S(2)}) %collective-permute-start.23) | collective-permute-done | bytes 262176 | tf_op jit(solution)/shard_map/ppermute | solution.py:343
  88.6 1.2 %collective-permute-start.24 = (bf16[64,2048]{1,0:T(8,128)(2,1)S(1)}, bf16[64,2048]{1,0:T(8,128)(2,1)S(1)}, u32[]{:S(2)}, u32[]{:S(2)}) collective-permute-start(bf16[64,2048]{1,0:T(8,128)(2,1)S(1)} %add_convert_fusion.5), channel_id=1, source_target_pairs={{2,0},{4,2},{6,4},{7,6},{5,7},{3,5},{1,3},{0,1},{10,8},{12,10},{14... | collective-permute-start | bytes 786440 | tf_op jit(solution)/shard_map/ppermute | solution.py:343
  92.0 2.2 %collective-permute-done.29 = bf16[64,2048]{1,0:T(8,128)(2,1)S(1)} collective-permute-done((bf16[64,2048]{1,0:T(8,128)(2,1)S(1)}, bf16[64,2048]{1,0:T(8,128)(2,1)S(1)}, u32[]{:S(2)}, u32[]{:S(2)}) %collective-permute-start.29) | collective-permute-done | bytes 262176 | tf_op jit(solution)/shard_map/ppermute | solution.py:343
  94.2 1.2 %collective-permute-start.30 = (bf16[64,2048]{1,0:T(8,128)(2,1)S(1)}, bf16[64,2048]{1,0:T(8,128)(2,1)S(1)}, u32[]{:S(2)}, u32[]{:S(2)}) collective-permute-start(bf16[64,2048]{1,0:T(8,128)(2,1)S(1)} %add_convert_fusion.1), channel_id=1, source_target_pairs={{2,0},{4,2},{6,4},{7,6},{5,7},{3,5},{1,3},{0,1},{10,8},{12,10},{14... | collective-permute-start | bytes 786440 | tf_op jit(solution)/shard_map/ppermute | solution.py:343
  95.5 1.1 collective-permute-done.26
  98.1 4.1 %collective-permute-done.20 = bf16[64,2048]{1,0:T(8,128)(2,1)S(1)} collective-permute-done((bf16[64,2048]{1,0:T(8,128)(2,1)S(1)}, bf16[64,2048]{1,0:T(8,128)(2,1)S(1)}, u32[]{:S(2)}, u32[]{:S(2)}) %collective-permute-start.20) | collective-permute-done | bytes 262176 | tf_op jit(solution)/shard_map/ppermute | solution.py:343
  104.0 1.2 %collective-permute-start.31 = (bf16[64,2048]{1,0:T(8,128)(2,1)S(1)}, bf16[64,2048]{1,0:T(8,128)(2,1)S(1)}, u32[]{:S(2)}, u32[]{:S(2)}) collective-permute-start(bf16[64,2048]{1,0:T(8,128)(2,1)S(1)} %add_convert_fusion), channel_id=1, source_target_pairs={{2,0},{4,2},{6,4},{7,6},{5,7},{3,5},{1,3},{0,1},{10,8},{12,10},{14... | collective-permute-start | bytes 786440 | tf_op jit(solution)/shard_map/ppermute | solution.py:343
  105.2 5.7 %collective-permute-done.3 = bf16[128,2048]{1,0:T(8,128)(2,1)S(1)} collective-permute-done((bf16[128,2048]{1,0:T(8,128)(2,1)S(1)}, bf16[128,2048]{1,0:T(8,128)(2,1)S(1)}, u32[]{:S(2)}, u32[]{:S(2)}) %collective-permute-start.3) | collective-permute-done | bytes 524320 | tf_op jit(solution)/shard_map/ppermute | solution.py:323
  111.1 2.0 %collective-permute-done.21 = bf16[64,2048]{1,0:T(8,128)(2,1)S(1)} collective-permute-done((bf16[64,2048]{1,0:T(8,128)(2,1)S(1)}, bf16[64,2048]{1,0:T(8,128)(2,1)S(1)}, u32[]{:S(2)}, u32[]{:S(2)}) %collective-permute-start.21) | collective-permute-done | bytes 262176 | tf_op jit(solution)/shard_map/ppermute | solution.py:343
  (74 shorter events, 19.3 us)
Async XLA Ops:
  0.0 15.4 %collective-permute-start = (bf16[128,2048]{1,0:T(8,128)(2,1)}, bf16[128,2048]{1,0:T(8,128)(2,1)S(1)}, u32[]{:S(2)}, u32[]{:S(2)}) collective-permute-start(bf16[128,2048]{1,0:T(8,128)(2,1)} %refs_0_.1), channel_id=1, source_target_pairs={{0,16},{8,24},{16,0},{24,8},{1,17},{9,25},{17,1},{25,9},{2,18},{10... | collective-permute-start | bytes 1572872 | tf_op jit(solution)/shard_map/ppermute | solution.py:309
  4.1 9.3 %collective-permute-start.4 = (bf16[64,2048]{1,0:T(8,128)(2,1)S(1)}, bf16[64,2048]{1,0:T(8,128)(2,1)S(1)}, u32[]{:S(2)}, u32[]{:S(2)}) collective-permute-start(bf16[64,2048]{1,0:T(8,128)(2,1)S(1)} %get-tuple-element.50), channel_id=1, source_target_pairs={{0,2},{2,4},{4,6},{6,7},{7,5},{5,3},{3,1},{1,0},{8,10},{10,12},{12... | collective-permute-start | bytes 786440 | tf_op jit(solution)/shard_map/ppermute | solution.py:300
  5.7 9.2 %collective-permute-start.8 = (bf16[64,2048]{1,0:T(8,128)(2,1)S(1)}, bf16[64,2048]{1,0:T(8,128)(2,1)S(1)}, u32[]{:S(2)}, u32[]{:S(2)}) collective-permute-start(bf16[64,2048]{1,0:T(8,128)(2,1)S(1)} %get-tuple-element.49), channel_id=1, source_target_pairs={{2,0},{4,2},{6,4},{7,6},{5,7},{3,5},{1,3},{0,1},{10,8},{12,10},{14... | collective-permute-start | bytes 786440 | tf_op jit(solution)/shard_map/ppermute | solution.py:303
  6.2 12.8 %collective-permute-start.12 = (bf16[64,2048]{1,0:T(8,128)(2,1)S(1)}, bf16[64,2048]{1,0:T(8,128)(2,1)S(1)}, u32[]{:S(2)}, u32[]{:S(2)}) collective-permute-start(bf16[64,2048]{1,0:T(8,128)(2,1)S(1)} %get-tuple-element.49), channel_id=1, source_target_pairs={{0,2},{2,4},{4,6},{6,7},{7,5},{5,3},{3,1},{1,0},{8,10},{10,12},{12... | collective-permute-start | bytes 786440 | tf_op jit(solution)/shard_map/ppermute | solution.py:300
  7.8 12.8 %collective-permute-start.13 = (bf16[64,2048]{1,0:T(8,128)(2,1)S(1)}, bf16[64,2048]{1,0:T(8,128)(2,1)S(1)}, u32[]{:S(2)}, u32[]{:S(2)}) collective-permute-start(bf16[64,2048]{1,0:T(8,128)(2,1)S(1)} %get-tuple-element.50), channel_id=1, source_target_pairs={{2,0},{4,2},{6,4},{7,6},{5,7},{3,5},{1,3},{0,1},{10,8},{12,10},{14... | collective-permute-start | bytes 786440 | tf_op jit(solution)/shard_map/ppermute | solution.py:303
  13.4 11.2 %collective-permute-start.5 = (bf16[64,2048]{1,0:T(8,128)(2,1)S(1)}, bf16[64,2048]{1,0:T(8,128)(2,1)S(1)}, u32[]{:S(2)}, u32[]{:S(2)}) collective-permute-start(bf16[64,2048]{1,0:T(8,128)(2,1)S(1)} %collective-permute-done.4.refs_3_), channel_id=1, source_target_pairs={{0,2},{2,4},{4,6},{6,7},{7,5},{5,3},{3,1},{1,0},{8,10},{10,12},{12... | collective-permute-start | bytes 786440 | tf_op jit(solution)/shard_map/ppermute | solution.py:300
  15.0 11.2 %collective-permute-start.9 = (bf16[64,2048]{1,0:T(8,128)(2,1)S(1)}, bf16[64,2048]{1,0:T(8,128)(2,1)S(1)}, u32[]{:S(2)}, u32[]{:S(2)}) collective-permute-start(bf16[64,2048]{1,0:T(8,128)(2,1)S(1)} %collective-permute-done.8.refs_6_), channel_id=1, source_target_pairs={{2,0},{4,2},{6,4},{7,6},{5,7},{3,5},{1,3},{0,1},{10,8},{12,10},{14... | collective-permute-start | bytes 786440 | tf_op jit(solution)/shard_map/ppermute | solution.py:303
  16.3 28.9 %collective-permute-start.1 = (bf16[256,2048]{1,0:T(8,128)(2,1)}, bf16[256,2048]{1,0:T(8,128)(2,1)}, u32[]{:S(2)}, u32[]{:S(2)}) collective-permute-start(bf16[256,2048]{1,0:T(8,128)(2,1)} %constant_dynamic-update-slice_fusion.refs_0_), channel_id=1, source_target_pairs={{0,8},{8,0},{16,24},{24,16},{1,9},{9,1},{17,25},{25,17},{2,10},{10... | collective-permute-start | bytes 3145736 | tf_op jit(solution)/shard_map/ppermute | solution.py:312
  19.0 11.2 %collective-permute-start.14 = (bf16[64,2048]{1,0:T(8,128)(2,1)S(1)}, bf16[64,2048]{1,0:T(8,128)(2,1)S(1)}, u32[]{:S(2)}, u32[]{:S(2)}) collective-permute-start(bf16[64,2048]{1,0:T(8,128)(2,1)S(1)} %collective-permute-done.12.refs_4_), channel_id=1, source_target_pairs={{0,2},{2,4},{4,6},{6,7},{7,5},{5,3},{3,1},{1,0},{8,10},{10,12},{12... | collective-permute-start | bytes 786440 | tf_op jit(solution)/shard_map/ppermute | solution.py:300
  20.6 11.2 %collective-permute-start.15 = (bf16[64,2048]{1,0:T(8,128)(2,1)S(1)}, bf16[64,2048]{1,0:T(8,128)(2,1)S(1)}, u32[]{:S(2)}, u32[]{:S(2)}) collective-permute-start(bf16[64,2048]{1,0:T(8,128)(2,1)S(1)} %collective-permute-done.13.refs_5_), channel_id=1, source_target_pairs={{2,0},{4,2},{6,4},{7,6},{5,7},{3,5},{1,3},{0,1},{10,8},{12,10},{14... | collective-permute-start | bytes 786440 | tf_op jit(solution)/shard_map/ppermute | solution.py:303
  24.6 11.2 %collective-permute-start.6 = (bf16[64,2048]{1,0:T(8,128)(2,1)S(1)}, bf16[64,2048]{1,0:T(8,128)(2,1)S(1)}, u32[]{:S(2)}, u32[]{:S(2)}) collective-permute-start(bf16[64,2048]{1,0:T(8,128)(2,1)S(1)} %collective-permute-done.5.refs_7_), channel_id=1, source_target_pairs={{0,2},{2,4},{4,6},{6,7},{7,5},{5,3},{3,1},{1,0},{8,10},{10,12},{12... | collective-permute-start | bytes 786440 | tf_op jit(solution)/shard_map/ppermute | solution.py:300
  26.2 11.2 %collective-permute-start.10 = (bf16[64,2048]{1,0:T(8,128)(2,1)S(1)}, bf16[64,2048]{1,0:T(8,128)(2,1)S(1)}, u32[]{:S(2)}, u32[]{:S(2)}) collective-permute-start(bf16[64,2048]{1,0:T(8,128)(2,1)S(1)} %collective-permute-done.9.refs_10_), channel_id=1, source_target_pairs={{2,0},{4,2},{6,4},{7,6},{5,7},{3,5},{1,3},{0,1},{10,8},{12,10},{14... | collective-permute-start | bytes 786440 | tf_op jit(solution)/shard_map/ppermute | solution.py:303
  30.2 22.0 %collective-permute-start.16 = (bf16[64,2048]{1,0:T(8,128)(2,1)S(1)}, bf16[64,2048]{1,0:T(8,128)(2,1)S(1)}, u32[]{:S(2)}, u32[]{:S(2)}) collective-permute-start(bf16[64,2048]{1,0:T(8,128)(2,1)S(1)} %collective-permute-done.14.refs_8_), channel_id=1, source_target_pairs={{0,2},{2,4},{4,6},{6,7},{7,5},{5,3},{3,1},{1,0},{8,10},{10,12},{12... | collective-permute-start | bytes 786440 | tf_op jit(solution)/shard_map/ppermute | solution.py:300
  31.8 20.5 %collective-permute-start.17 = (bf16[64,2048]{1,0:T(8,128)(2,1)S(1)}, bf16[64,2048]{1,0:T(8,128)(2,1)}, u32[]{:S(2)}, u32[]{:S(2)}) collective-permute-start(bf16[64,2048]{1,0:T(8,128)(2,1)S(1)} %collective-permute-done.15.refs_9_), channel_id=1, source_target_pairs={{2,0},{4,2},{6,4},{7,6},{5,7},{3,5},{1,3},{0,1},{10,8},{12,10},{14... | collective-permute-start | bytes 786440 | tf_op jit(solution)/shard_map/ppermute | solution.py:303
  35.9 16.4 %collective-permute-start.7 = (bf16[64,2048]{1,0:T(8,128)(2,1)S(1)}, bf16[64,2048]{1,0:T(8,128)(2,1)}, u32[]{:S(2)}, u32[]{:S(2)}) collective-permute-start(bf16[64,2048]{1,0:T(8,128)(2,1)S(1)} %collective-permute-done.6.refs_11_), channel_id=1, source_target_pairs={{0,2},{2,4},{4,6},{6,7},{7,5},{5,3},{3,1},{1,0},{8,10},{10,12},{12... | collective-permute-start | bytes 786440 | tf_op jit(solution)/shard_map/ppermute | solution.py:300
  37.5 14.9 %collective-permute-start.11 = (bf16[64,2048]{1,0:T(8,128)(2,1)S(1)}, bf16[64,2048]{1,0:T(8,128)(2,1)}, u32[]{:S(2)}, u32[]{:S(2)}) collective-permute-start(bf16[64,2048]{1,0:T(8,128)(2,1)S(1)} %collective-permute-done.10.refs_14_), channel_id=1, source_target_pairs={{2,0},{4,2},{6,4},{7,6},{5,7},{3,5},{1,3},{0,1},{10,8},{12,10},{14... | collective-permute-start | bytes 786440 | tf_op jit(solution)/shard_map/ppermute | solution.py:303
  38.6 13.7 %all-to-all-start = ((f32[8,8,128]{2,1,0:T(8,128)}), f32[8,8,128]{2,1,0:T(8,128)S(1)}, u32[]{:S(2)}, u32[]{:S(2)}) async-start(f32[8,8,128]{2,1,0:T(8,128)} %bitcast.20), calls=%async_computation | async-start | bytes 65536 | tf_op jit(solution)/shard_map/all_to_all | solution.py:283
  70.7 26.9 %collective-permute-start.2 = (bf16[256,2048]{1,0:T(8,128)(2,1)S(1)}, bf16[256,2048]{1,0:T(8,128)(2,1)S(1)}, u32[]{:S(2)}, u32[]{:S(2)}) collective-permute-start(bf16[256,2048]{1,0:T(8,128)(2,1)S(1)} %copy-done.4), channel_id=1, source_target_pairs={{0,8},{8,0},{16,24},{24,16},{1,9},{9,1},{17,25},{25,17},{2,10},{10... | collective-permute-start | bytes 3145736 | tf_op jit(solution)/shard_map/ppermute | solution.py:314
  70.7 9.1 %collective-permute-start.18 = (bf16[64,2048]{1,0:T(8,128)(2,1)S(1)}, bf16[64,2048]{1,0:T(8,128)(2,1)S(1)}, u32[]{:S(2)}, u32[]{:S(2)}) collective-permute-start(bf16[64,2048]{1,0:T(8,128)(2,1)S(1)} %get-tuple-element.32), channel_id=1, source_target_pairs={{0,2},{2,4},{4,6},{6,7},{7,5},{5,3},{3,1},{1,0},{8,10},{10,12},{12... | collective-permute-start | bytes 786440 | tf_op jit(solution)/shard_map/ppermute | solution.py:343
  71.5 11.4 %collective-permute-start.28 = (bf16[64,2048]{1,0:T(8,128)(2,1)S(1)}, bf16[64,2048]{1,0:T(8,128)(2,1)S(1)}, u32[]{:S(2)}, u32[]{:S(2)}) collective-permute-start(bf16[64,2048]{1,0:T(8,128)(2,1)S(1)} %get-tuple-element.43), channel_id=1, source_target_pairs={{2,0},{4,2},{6,4},{7,6},{5,7},{3,5},{1,3},{0,1},{10,8},{12,10},{14... | collective-permute-start | bytes 786440 | tf_op jit(solution)/shard_map/ppermute | solution.py:343
  72.7 12.7 %collective-permute-start.25 = (bf16[64,2048]{1,0:T(8,128)(2,1)S(1)}, bf16[64,2048]{1,0:T(8,128)(2,1)S(1)}, u32[]{:S(2)}, u32[]{:S(2)}) collective-permute-start(bf16[64,2048]{1,0:T(8,128)(2,1)S(1)} %get-tuple-element.40), channel_id=1, source_target_pairs={{0,2},{2,4},{4,6},{6,7},{7,5},{5,3},{3,1},{1,0},{8,10},{10,12},{12... | collective-permute-start | bytes 786440 | tf_op jit(solution)/shard_map/ppermute | solution.py:343
  77.4 11.2 %collective-permute-start.23 = (bf16[64,2048]{1,0:T(8,128)(2,1)S(1)}, bf16[64,2048]{1,0:T(8,128)(2,1)S(1)}, u32[]{:S(2)}, u32[]{:S(2)}) collective-permute-start(bf16[64,2048]{1,0:T(8,128)(2,1)S(1)} %add_convert_fusion.6), channel_id=1, source_target_pairs={{2,0},{4,2},{6,4},{7,6},{5,7},{3,5},{1,3},{0,1},{10,8},{12,10},{14... | collective-permute-start | bytes 786440 | tf_op jit(solution)/shard_map/ppermute | solution.py:343
  79.8 11.2 %collective-permute-start.19 = (bf16[64,2048]{1,0:T(8,128)(2,1)S(1)}, bf16[64,2048]{1,0:T(8,128)(2,1)S(1)}, u32[]{:S(2)}, u32[]{:S(2)}) collective-permute-start(bf16[64,2048]{1,0:T(8,128)(2,1)S(1)} %add_convert_fusion.9), channel_id=1, source_target_pairs={{0,2},{2,4},{4,6},{6,7},{7,5},{5,3},{3,1},{1,0},{8,10},{10,12},{12... | collective-permute-start | bytes 786440 | tf_op jit(solution)/shard_map/ppermute | solution.py:343
  83.0 11.2 %collective-permute-start.29 = (bf16[64,2048]{1,0:T(8,128)(2,1)S(1)}, bf16[64,2048]{1,0:T(8,128)(2,1)S(1)}, u32[]{:S(2)}, u32[]{:S(2)}) collective-permute-start(bf16[64,2048]{1,0:T(8,128)(2,1)S(1)} %add_convert_fusion.2), channel_id=1, source_target_pairs={{2,0},{4,2},{6,4},{7,6},{5,7},{3,5},{1,3},{0,1},{10,8},{12,10},{14... | collective-permute-start | bytes 786440 | tf_op jit(solution)/shard_map/ppermute | solution.py:343
  85.5 11.2 %collective-permute-start.26 = (bf16[64,2048]{1,0:T(8,128)(2,1)S(1)}, bf16[64,2048]{1,0:T(8,128)(2,1)S(1)}, u32[]{:S(2)}, u32[]{:S(2)}) collective-permute-start(bf16[64,2048]{1,0:T(8,128)(2,1)S(1)} %add_convert_fusion.4), channel_id=1, source_target_pairs={{0,2},{2,4},{4,6},{6,7},{7,5},{5,3},{3,1},{1,0},{8,10},{10,12},{12... | collective-permute-start | bytes 786440 | tf_op jit(solution)/shard_map/ppermute | solution.py:343
  88.6 22.5 %collective-permute-start.24 = (bf16[64,2048]{1,0:T(8,128)(2,1)S(1)}, bf16[64,2048]{1,0:T(8,128)(2,1)S(1)}, u32[]{:S(2)}, u32[]{:S(2)}) collective-permute-start(bf16[64,2048]{1,0:T(8,128)(2,1)S(1)} %add_convert_fusion.5), channel_id=1, source_target_pairs={{2,0},{4,2},{6,4},{7,6},{5,7},{3,5},{1,3},{0,1},{10,8},{12,10},{14... | collective-permute-start | bytes 786440 | tf_op jit(solution)/shard_map/ppermute | solution.py:343
  91.1 11.2 %collective-permute-start.20 = (bf16[64,2048]{1,0:T(8,128)(2,1)S(1)}, bf16[64,2048]{1,0:T(8,128)(2,1)S(1)}, u32[]{:S(2)}, u32[]{:S(2)}) collective-permute-start(bf16[64,2048]{1,0:T(8,128)(2,1)S(1)} %add_convert_fusion.8), channel_id=1, source_target_pairs={{0,2},{2,4},{4,6},{6,7},{7,5},{5,3},{3,1},{1,0},{8,10},{10,12},{12... | collective-permute-start | bytes 786440 | tf_op jit(solution)/shard_map/ppermute | solution.py:343
  94.2 9.7 %collective-permute-start.30 = (bf16[64,2048]{1,0:T(8,128)(2,1)S(1)}, bf16[64,2048]{1,0:T(8,128)(2,1)S(1)}, u32[]{:S(2)}, u32[]{:S(2)}) collective-permute-start(bf16[64,2048]{1,0:T(8,128)(2,1)S(1)} %add_convert_fusion.1), channel_id=1, source_target_pairs={{2,0},{4,2},{6,4},{7,6},{5,7},{3,5},{1,3},{0,1},{10,8},{12,10},{14... | collective-permute-start | bytes 786440 | tf_op jit(solution)/shard_map/ppermute | solution.py:343
  96.7 14.4 %collective-permute-start.27 = (bf16[64,2048]{1,0:T(8,128)(2,1)S(1)}, bf16[64,2048]{1,0:T(8,128)(2,1)S(1)}, u32[]{:S(2)}, u32[]{:S(2)}) collective-permute-start(bf16[64,2048]{1,0:T(8,128)(2,1)S(1)} %add_convert_fusion.3), channel_id=1, source_target_pairs={{0,2},{2,4},{4,6},{6,7},{7,5},{5,3},{3,1},{1,0},{8,10},{10,12},{12... | collective-permute-start | bytes 786440 | tf_op jit(solution)/shard_map/ppermute | solution.py:343
  98.0 13.0 %collective-permute-start.3 = (bf16[128,2048]{1,0:T(8,128)(2,1)S(1)}, bf16[128,2048]{1,0:T(8,128)(2,1)S(1)}, u32[]{:S(2)}, u32[]{:S(2)}) collective-permute-start(bf16[128,2048]{1,0:T(8,128)(2,1)S(1)} %slice.107), channel_id=1, source_target_pairs={{0,16},{8,24},{16,0},{24,8},{1,17},{9,25},{17,1},{25,9},{2,18},{10... | collective-permute-start | bytes 1572872 | tf_op jit(solution)/shard_map/ppermute | solution.py:323
  102.3 10.8 %collective-permute-start.21 = (bf16[64,2048]{1,0:T(8,128)(2,1)S(1)}, bf16[64,2048]{1,0:T(8,128)(2,1)S(1)}, u32[]{:S(2)}, u32[]{:S(2)}) collective-permute-start(bf16[64,2048]{1,0:T(8,128)(2,1)S(1)} %add_convert_fusion.7), channel_id=1, source_target_pairs={{0,2},{2,4},{4,6},{6,7},{7,5},{5,3},{3,1},{1,0},{8,10},{10,12},{12... | collective-permute-start | bytes 786440 | tf_op jit(solution)/shard_map/ppermute | solution.py:343
  104.0 9.1 %collective-permute-start.31 = (bf16[64,2048]{1,0:T(8,128)(2,1)S(1)}, bf16[64,2048]{1,0:T(8,128)(2,1)S(1)}, u32[]{:S(2)}, u32[]{:S(2)}) collective-permute-start(bf16[64,2048]{1,0:T(8,128)(2,1)S(1)} %add_convert_fusion), channel_id=1, source_target_pairs={{2,0},{4,2},{6,4},{7,6},{5,7},{3,5},{1,3},{0,1},{10,8},{12,10},{14... | collective-permute-start | bytes 786440 | tf_op jit(solution)/shard_map/ppermute | solution.py:343
  (7 other events, 107.9 us)

commit v5 on v4

v5 whole, which is shorter than its diff:
```python
import functools

import jax
import jax.numpy as jnp
from jax import lax
from jax.experimental import pallas as pl
from jax.experimental.pallas import tpu as pltpu
from jax.sharding import PartitionSpec as P

HOT_SLOTS = 40
SLOTS = 24
SMALL = 1000
EXTRA = HOT_SLOTS - SLOTS
BF16 = jnp.bfloat16
F32 = jnp.float32
HBM = pl.BlockSpec(memory_space=pltpu.HBM)
VMEM = pl.BlockSpec(memory_space=pltpu.VMEM)
SMEM = pl.BlockSpec(memory_space=pltpu.SMEM)


def ring_of(count):
    return list(range(0, count, 2)) + list(range(count - 1, 0, -2))


def offsets_of(count):
    order = [0, count // 2]
    for hop in range(1, count // 2):
        order += [hop, count - hop]
    return order


def dot(a, b):
    return jnp.dot(a, b, preferred_element_type=F32)


def dot_t(a, b):
    return lax.dot_general(a, b, (((1,), (1,)), ((), ())), preferred_element_type=F32)


def dot_l(a, b):
    return lax.dot_general(a, b, (((0,), (0,)), ((), ())), preferred_element_type=F32)


def routing(expert_ids, gate_weights, capacity, hot_expert, experts):
    tokens, top = expert_ids.shape
    ids, gates = expert_ids.T, gate_weights.T
    labels = jnp.arange(experts, dtype=jnp.int32)[:, None]
    chosen = jnp.zeros((experts, tokens), jnp.bool_)
    weight = jnp.zeros((experts, tokens), F32)
    for k in range(top):
        here = ids[k][None, :] == labels
        chosen = chosen | here
        weight = weight + jnp.where(here, gates[k][None, :], 0.0)
    place = jnp.arange(tokens, dtype=jnp.int32)
    earlier = (place[:, None] < place[None, :]).astype(BF16)
    rank = dot(chosen.astype(BF16), earlier)
    limit = jnp.where(labels == hot_expert[0], HOT_SLOTS, capacity[0][:, None]).astype(F32)
    kept = chosen & (rank < limit)
    return jnp.stack([jnp.where(kept, rank, -1.0), jnp.where(kept, weight, 0.0)], axis=1)


def source_of(place, offset, count):
    at = jnp.where(place % 2 == 0, place // 2, count // 2 + (count - 1 - place) // 2)
    at = lax.rem(at - offset + count, count)
    return jnp.where(at < count // 2, 2 * at, 2 * count - 1 - 2 * at)


def pick_kernel(offsets, early, sizes, count, local, where, meta, *refs):
    refs = list(refs)
    units = [[refs.pop(0) for _ in range(size)] for size in sizes]
    sel, scale, rows = refs
    pairs = len(offsets) // 2
    wide, wide_x = 2 * SLOTS, 2 * EXTRA
    base, base_e = pairs * wide, early * wide
    hot = where[1]
    lane = lax.broadcasted_iota(jnp.int32, (1, 256), 1)
    second = (lane >= 128).astype(F32)
    for p in range(pairs):
        info = [meta[source_of(where[0], offsets[2 * p + i], count)] for i in range(2)]
        blocks = []
        for e in range(local):
            rank = jnp.concatenate([part[2 * e : 2 * e + 1] for part in info], axis=1)
            gate = jnp.concatenate([part[2 * e + 1 : 2 * e + 2] for part in info], axis=1)
            key = jnp.where((rank >= 0) & (rank < SLOTS), rank + SLOTS * second, -1.0).astype(jnp.int32)
            pick = (lax.broadcasted_iota(jnp.int32, (wide, 256), 0) == key).astype(F32)
            blocks.append(pick)
            scale[e, pl.ds(p * wide, wide), :] = jnp.broadcast_to(
                jnp.sum(pick * gate, axis=1, keepdims=True), (wide, 128)
            )
            key_x = jnp.where((rank >= SLOTS) & (hot == e), rank - SLOTS + EXTRA * second, -1.0)
            pick_x = (lax.broadcasted_iota(jnp.int32, (wide_x, 256), 0) == key_x.astype(jnp.int32)).astype(F32)
            scale[e, pl.ds(base + p * wide_x, wide_x), :] = jnp.broadcast_to(
                jnp.sum(pick_x * gate, axis=1, keepdims=True), (wide_x, 128)
            )
            extra = pick_x if e == 0 else extra + pick_x
        blocks.append(extra)
        sel[p] = jnp.concatenate(blocks, axis=0).astype(BF16)
        if p < early:
            gather_pair(sel[p], units[2 * p] + units[2 * p + 1], rows, p, base_e, local, hot)


def gather_pair(pick, units, rows, p, base, local, hot):
    wide, wide_x = 2 * SLOTS, 2 * EXTRA
    pair = jnp.concatenate([unit[...] for unit in units], axis=0)
    got = dot(pick, pair).astype(BF16)
    for e in range(local):
        rows[e, pl.ds(p * wide, wide), :] = got[e * wide : (e + 1) * wide]

        @pl.when(hot == e)
        def _():
            rows[e, pl.ds(base + p * wide_x, wide_x), :] = got[local * wide :]


def run_pick(offsets, early, count, local, where, meta, blocks):
    flat = [unit for o in offsets[: 2 * early] for unit in blocks[o]]
    sizes = tuple(len(blocks[o]) for o in offsets[: 2 * early])
    width = flat[0].shape[1]
    pairs = len(offsets) // 2
    wide, wide_x = 2 * SLOTS, 2 * EXTRA
    flat = [pltpu.with_memory_space_constraint(unit, pltpu.VMEM) for unit in flat]
    return pl.pallas_call(
        functools.partial(pick_kernel, offsets, early, sizes, count, local),
        out_shape=[
            pltpu.VMEM((pairs, local * wide + wide_x, 256), BF16),
            pltpu.VMEM((local, pairs * (wide + wide_x), 128), F32),
            pltpu.VMEM((local, early * (wide + wide_x), width), BF16),
        ],
        in_specs=[SMEM, VMEM] + [VMEM] * len(flat),
        out_specs=[VMEM] * 3,
        cost_estimate=pl.CostEstimate(flops=SMALL, transcendentals=0, bytes_accessed=SMALL),
        compiler_params=pltpu.CompilerParams(vmem_limit_bytes=6 << 20),
        name="pick",
    )(where, meta, *flat)


def experts_kernel(offsets, early, sizes, local, buffers, where, sel, scale, rows_e, *refs):
    refs = list(refs)
    units = [[refs.pop(0) for _ in range(size)] for size in sizes]
    ready = [refs.pop(0) for _ in range(3)]
    source = [refs.pop(0) for _ in range(3)]
    outs = [[refs.pop(0) for _ in range(2)] for _ in offsets]
    held = [refs.pop(0) for _ in range(3)]
    eo, rows, sem = refs
    pairs = len(offsets) // 2
    late = pairs - early
    width = rows.shape[2]
    wide, wide_x = 2 * SLOTS, 2 * EXTRA
    base, base_e, base_l = pairs * wide, early * wide, late * wide
    hot = where[1]

    def fetching(e, k):
        at = lax.rem(e - 1, buffers)
        return pltpu.make_async_copy(source[k].at[e], held[k].at[at], sem.at[at, k])

    for e in range(1, min(buffers + 1, local)):
        for k in range(3):
            fetching(e, k).start()

    for p in range(late):
        gather_pair(sel[early + p], units[2 * p] + units[2 * p + 1], rows, p, base_l, local, hot)
    for p in range(pairs):
        eo[p, pl.ds(local * wide, wide_x), :] = jnp.zeros((wide_x, width), BF16)

    def run(e, gates, uppers, downs, before_down, whole):
        tokens = [rows_e[e, :base_e], rows[e, :base_l]]
        if whole:
            tokens += [rows_e[e, base_e:], rows[e, base_l:]]
        tokens = jnp.concatenate(tokens, axis=0)
        gate = dot_t(tokens, gates[...])
        upper = dot_t(tokens, uppers[...])
        weight = scale[e, : tokens.shape[0]][:, :1]
        hidden = (gate / (1.0 + jnp.exp(-gate)) * upper * weight).astype(BF16)
        before_down()
        out = dot(hidden, downs[...]).astype(BF16)
        for p in range(pairs):
            at = e * wide if isinstance(e, int) else pl.multiple_of(e * wide, wide)
            eo[p, pl.ds(at, wide), :] = out[p * wide : (p + 1) * wide]
            if whole:
                eo[p, pl.ds(local * wide, wide_x), :] = out[base + p * wide_x : base + (p + 1) * wide_x]

    def either(e, *rest):
        @pl.when(hot == e)
        def _():
            run(e, *rest, True)

        @pl.when(hot != e)
        def _():
            run(e, *rest, False)

    either(0, *ready, lambda: None)

    def body(e, carry):
        at = lax.rem(e - 1, buffers)
        fetching(e, 0).wait()
        fetching(e, 1).wait()
        either(e, *(w.at[at] for w in held), lambda: fetching(e, 2).wait())

        @pl.when(e + buffers < local)
        def _():
            for k in range(3):
                fetching(e + buffers, k).start()

        return carry

    lax.fori_loop(1, local, body, 0)

    for p in range(pairs):
        total = dot_l(sel[p], eo[p]).astype(BF16)
        for i in range(4):
            outs[2 * p + i // 2][i % 2][...] = total[i * 64 : (i + 1) * 64]


def run_experts(offsets, early, local, where, picked, blocks, ready, weights):
    hidden, width = weights[2].shape[1:]
    wide, wide_x = 2 * SLOTS, 2 * EXTRA
    pairs = len(offsets) // 2
    late = pairs - early
    high = local * wide + wide_x
    full, full_l = pairs * (wide + wide_x), late * (wide + wide_x)
    buffers = max(1, min(local - 1, 2))
    flat = [unit for o in offsets[2 * early :] for unit in blocks[o]]
    sizes = tuple(len(blocks[o]) for o in offsets[2 * early :])
    room = 2 * width * (3 * buffers * hidden + local * full_l + pairs * high)
    room += full * (6 * width + 10 * hidden) + (2 << 20)
    inside = [pltpu.with_memory_space_constraint(v, pltpu.VMEM) for v in [*picked, *flat, *ready]]
    weights = [pltpu.with_memory_space_constraint(w, pltpu.HBM) for w in weights]
    return pl.pallas_call(
        functools.partial(experts_kernel, offsets, early, sizes, local, buffers),
        out_shape=[pltpu.VMEM((64, width), BF16)] * (2 * len(offsets)),
        in_specs=[SMEM] + [VMEM] * len(inside) + [HBM] * 3,
        out_specs=[VMEM] * (2 * len(offsets)),
        scratch_shapes=[
            pltpu.VMEM((buffers, hidden, width), BF16),
            pltpu.VMEM((buffers, hidden, width), BF16),
            pltpu.VMEM((buffers, hidden, width), BF16),
            pltpu.VMEM((pairs, high, width), BF16),
            pltpu.VMEM((local, full_l, width), BF16),
            pltpu.SemaphoreType.DMA((buffers, 3)),
        ],
        cost_estimate=pl.CostEstimate(
            flops=2 * 3 * width * hidden * local * pairs * wide + 4 * len(offsets) * 128 * high * width,
            transcendentals=local * pairs * wide * hidden,
            bytes_accessed=6 * local * hidden * width,
        ),
        compiler_params=pltpu.CompilerParams(vmem_limit_bytes=room),
        name="routed_experts",
    )(where, *inside, *weights)


def shared_kernel(count, *refs):
    blocks, weights, ahead = refs[:count], refs[count : count + 3], refs[count + 3 : count + 6]
    outs, ready = refs[count + 6 : count + 8], refs[count + 8 : count + 11]
    x, wg, wu, wd, out, sem, sem_r = refs[count + 11 :]
    rows = blocks[0].shape[0]
    loads = [
        pltpu.make_async_copy(block, x.at[pl.ds(i * rows, rows)], sem.at[i]) for i, block in enumerate(blocks)
    ]
    loads += [
        pltpu.make_async_copy(source, target, sem.at[count + k])
        for k, (source, target) in enumerate(zip(weights, (wg, wu, wd)))
    ]
    fetches = [
        pltpu.make_async_copy(source.at[0], target, sem_r.at[k])
        for k, (source, target) in enumerate(zip(ahead, ready))
    ]
    for copy in loads + fetches:
        copy.start()
    for copy in loads[:-2]:
        copy.wait()
    gate = dot(x[...], wg[...])
    loads[-2].wait()
    upper = dot(x[...], wu[...])
    hidden = (gate / (1.0 + jnp.exp(-gate)) * upper).astype(BF16)
    loads[-1].wait()
    half = count * rows // 2
    stores = []
    for i in (1, 0):
        out[i] = dot(hidden[i * half : (i + 1) * half], wd[...]).astype(BF16)
        stores.append(pltpu.make_async_copy(out.at[i], outs[i], sem.at[count + 3 + i]))
        stores[-1].start()
    for copy in fetches + stores:
        copy.wait()


def run_shared(blocks, weights, ahead):
    count = len(blocks)
    rows, width = blocks[0].shape
    hidden = weights[0].shape[1]
    blocks = [pltpu.with_memory_space_constraint(block, pltpu.HBM) for block in blocks]
    weights = [pltpu.with_memory_space_constraint(w, pltpu.HBM) for w in [*weights, *ahead]]
    return pl.pallas_call(
        functools.partial(shared_kernel, count),
        out_shape=[pltpu.HBM((count * rows // 2, width), BF16)] * 2
        + [pltpu.VMEM(w.shape[1:], BF16) for w in ahead],
        in_specs=[HBM] * (count + 6),
        out_specs=[HBM] * 2 + [VMEM] * 3,
        scratch_shapes=[
            pltpu.VMEM((count * rows, width), BF16),
            pltpu.VMEM((width, hidden), BF16),
            pltpu.VMEM((width, hidden), BF16),
            pltpu.VMEM((hidden, width), BF16),
            pltpu.VMEM((2, count * rows // 2, width), BF16),
            pltpu.SemaphoreType.DMA((count + 5,)),
            pltpu.SemaphoreType.DMA((3,)),
        ],
        cost_estimate=pl.CostEstimate(
            flops=SMALL, transcendentals=0, bytes_accessed=SMALL,
        ),
        compiler_params=pltpu.CompilerParams(vmem_limit_bytes=20 << 20),
        name="shared_experts",
    )(*blocks, *weights)


def tied(values, anchors):
    return lax.optimization_barrier((tuple(values), tuple(anchors)))[0]


def on_device(
    latents,
    expert_ids,
    gate_weights,
    capacity,
    hot_expert,
    w_gate,
    w_up,
    w_down,
    shared_gate,
    shared_up,
    shared_down,
):
    tokens, width = latents.shape
    half = tokens // 2
    local = w_gate.shape[0]
    count = lax.axis_size("expert")
    n_dp = lax.axis_size("dp")
    ring = ring_of(count)
    forward = [(ring[i], ring[(i + 1) % count]) for i in range(count)]
    backward = [(b, a) for a, b in forward]
    mid = count // 2

    info = routing(expert_ids, gate_weights, capacity, hot_expert, capacity.shape[1])
    info = info.reshape(count, 2 * local, tokens)
    meta = lax.all_to_all(info, "expert", split_axis=0, concat_axis=0, tiled=True)
    me = lax.axis_index("expert")
    where = jnp.stack([me, hot_expert[0] - me * local]).astype(jnp.int32)
    weights = [jnp.swapaxes(w_gate, 1, 2), jnp.swapaxes(w_up, 1, 2), w_down]

    bits = [1 << b for b in range(n_dp.bit_length() - 1)]
    blocks = {o: [None, None] for o in range(count)}
    up, down = [latents[:half], latents[half:]], [latents[:half], latents[half:]]
    for hop in range(1, mid + 1):
        if hop == mid:
            blocks[0] = [latents]
            order = offsets_of(count)
            order = order[2:-2] + order[-2:] + order[:2]
            picked = run_pick(tuple(order[:8]), 2, count, local, where, meta, blocks)
            up[0], down[1] = tied([up[0], down[1]], [picked[1]])
        for h in range(2):
            if hop < mid or h == 0:
                up[h] = lax.ppermute(up[h], "expert", forward)
                blocks[hop][h] = up[h]
            if hop < mid or h == 1:
                down[h] = lax.ppermute(down[h], "expert", backward)
                blocks[count - hop][h] = down[h]
    mine = [latents]
    for bit in reversed(bits[1:]):
        swap = [(d, d ^ bit) for d in range(n_dp)]
        mine += [lax.ppermute(block, "dp", swap) for block in mine]
    mine = jnp.concatenate(mine, axis=0)
    swap = [(d, d ^ 1) for d in range(n_dp)]
    keep, give, *ready = run_shared(
        [mine, lax.ppermute(mine, "dp", swap)], (shared_gate, shared_up, shared_down), weights
    )
    shared = keep.astype(F32) + lax.ppermute(give, "dp", swap).astype(F32)
    turns = [0]
    for bit in reversed(bits[1:]):
        turns += [r ^ bit for r in turns]
    part = {r: shared[i * tokens : (i + 1) * tokens] for i, r in enumerate(turns)}
    for bit in bits[1:]:
        swap = [(d, d ^ bit) for d in range(n_dp)]
        for r in sorted(part):
            if r & bit:
                came = lax.ppermute(part.pop(r).astype(BF16), "dp", swap)
                part[r ^ bit] = part[r ^ bit] + came.astype(F32)
    shared = part[0]

    done = {}
    for at in range(0, count, 8):
        chunk = tuple(order[at : at + 8])
        if at > 0:
            picked = run_pick(chunk, 2, count, local, where, meta, blocks)
        flat = run_experts(chunk, 2, local, where, picked, blocks, ready, weights)
        for i, o in enumerate(chunk):
            done[o] = [flat[2 * i], flat[2 * i + 1]]

    result = []
    for h in range(2):
        pieces = [done[0][h]]
        for step, perm, long in ((-1, forward, h == 0), (1, backward, h == 1)):
            start = mid if long else mid - 1
            acc = done[(step * start) % count][h]
            for k in range(start, 0, -1):
                came = lax.ppermute(acc, "expert", perm)
                if k > 1:
                    acc = (came.astype(F32) + done[(step * (k - 1)) % count][h].astype(F32)).astype(BF16)
            pieces.append(came)
        total = shared[h * half : (h + 1) * half].astype(F32)
        for piece in pieces:
            total = total + piece.astype(F32)
        result.append(total.astype(BF16))
    return jnp.concatenate(result, axis=0)


def solution(mesh):
    placed = (
        P(("dp", "expert"), None),
        P(("dp", "expert"), None),
        P(("dp", "expert"), None),
        P("dp", None),
        P("dp"),
        P("expert", None, None),
        P("expert", None, None),
        P("expert", None, None),
        P(None, "dp"),
        P(None, "dp"),
        P("dp", None),
    )
    return jax.shard_map(
        on_device, mesh=mesh, in_specs=placed, out_specs=P(("dp", "expert"), None), check_vma=False
    )
```

time: 115 us -> 110 us (0.957)
  waiting for transfers between devices: 43.6 us -> 40.4 us
  Pallas kernels: 24.2 us -> 22.9 us
    ppermute x7, waiting for transfers between devices: 16 us -> 2.65 us  [on_device(): up[h] = lax.ppermute(up[h], 'expert', forward)]
    ppermute x7, waiting for transfers between devices: 0.08 us -> 5.25 us  [on_device(): down[h] = lax.ppermute(down[h], 'expert', backward)]
    all_to_all x1, waiting for transfers between devices: 0.01 us -> 4.81 us  [on_device(): lax.all_to_all(info, 'expert', split_axis=0, concat_axis=0, tiled=True)]
    pallas_call x1 -> x2, Pallas kernels: 17.1 us -> 15.4 us  [the longest x1 13.7 us: run_experts(): pl.pallas_call(functools.partial(experts_kernel, offsets, early, sizes, l...]
  transfers between devices with their start and end apart: 33 -> 33, of which waited for: 17 -> 17; matrix products, arithmetic and copies ran while one was open for 6% -> 6% of each run, Pallas kernels for 6% -> 8%
where the time goes in v5:
time: 110 us
  waiting for transfers between devices  40.4 us (37%)
  starting transfers between devices  37.6 us (34%)
  Pallas kernels  22.9 us (21%)
  local copies, waits for them, and re-layouts  5.42 us (5%)
  other arithmetic  2.37 us (2%)
    ppermute x14, waiting for transfers between devices, on_device(): came = lax.ppermute(acc, 'expert', perm)  21.6 us
    ppermute x14, starting transfers between devices, on_device(): came = lax.ppermute(acc, 'expert', perm)  13.8 us
    pallas_call x1, Pallas kernels, run_experts(): pl.pallas_call(functools.partial(experts_kernel, offsets, early, sizes, l...  13.7 us
    ppermute x7, starting transfers between devices, on_device(): up[h] = lax.ppermute(up[h], 'expert', forward)  10.4 us
    pallas_call x1, Pallas kernels, run_shared(): pl.pallas_call(functools.partial(shared_kernel, count), out_shape=[pltpu....  7.48 us
    ppermute x1, waiting for transfers between devices, on_device(): came = lax.ppermute(part.pop(r).astype(BF16), 'dp', swap)  6.04 us
    all_to_all x1, starting transfers between devices, on_device(): lax.all_to_all(info, 'expert', split_axis=0, concat_axis=0, tiled=True)  5.81 us
    ppermute x7, waiting for transfers between devices, on_device(): down[h] = lax.ppermute(down[h], 'expert', backward)  5.25 us
  transfers between devices with their start and end apart: 33, of which 17 were waited for; matrix products, arithmetic and copies ran while one was open for 6% of the time, Pallas kernels for 8%

profile of v5, /device:TPU:0, one launch (start us, length us, event | category | flops | bytes accessed | tf_op | source)
XLA Modules:
  0.0 109.6 jit_solution(13143206304422599602)
XLA Ops:
  0.0 3.0 %collective-permute-start = (bf16[128,2048]{1,0:T(8,128)(2,1)}, bf16[128,2048]{1,0:T(8,128)(2,1)S(1)}, u32[]{:S(2)}, u32[]{:S(2)}) collective-permute-start(bf16[128,2048]{1,0:T(8,128)(2,1)} %refs_4_.3), channel_id=1, source_target_pairs={{0,16},{8,24},{16,0},{24,8},{1,17},{9,25},{17,1},{25,9},{2,18},{10... | collective-permute-start | bytes 1572872 | tf_op jit(solution)/shard_map/ppermute | solution.py:368
  4.0 1.6 %collective-permute-start.4 = (bf16[64,2048]{1,0:T(8,128)(2,1)S(1)}, bf16[64,2048]{1,0:T(8,128)(2,1)S(1)}, u32[]{:S(2)}, u32[]{:S(2)}) collective-permute-start(bf16[64,2048]{1,0:T(8,128)(2,1)S(1)} %get-tuple-element.60), channel_id=1, source_target_pairs={{0,2},{2,4},{4,6},{6,7},{7,5},{5,3},{3,1},{1,0},{8,10},{10,12},{12... | collective-permute-start | bytes 786440 | tf_op jit(solution)/shard_map/ppermute | solution.py:360
  6.1 1.6 %collective-permute-start.5 = (bf16[64,2048]{1,0:T(8,128)(2,1)S(1)}, bf16[64,2048]{1,0:T(8,128)(2,1)S(1)}, u32[]{:S(2)}, u32[]{:S(2)}) collective-permute-start(bf16[64,2048]{1,0:T(8,128)(2,1)S(1)} %get-tuple-element.59), channel_id=1, source_target_pairs={{0,2},{2,4},{4,6},{6,7},{7,5},{5,3},{3,1},{1,0},{8,10},{10,12},{12... | collective-permute-start | bytes 786440 | tf_op jit(solution)/shard_map/ppermute | solution.py:360
  9.7 1.9 %constant_dynamic-update-slice_fusion.1 = bf16[256,2048]{1,0:T(8,128)(2,1)} fusion(bf16[128,2048]{1,0:T(8,128)(2,1)} %refs_4_.3), kind=kLoop, calls=%fused_computation.40 | loop fusion | bytes 1048576
  11.6 1.7 %collective-permute-done.4.refs_0_ = bf16[64,2048]{1,0:T(8,128)(2,1)S(1)} collective-permute-done((bf16[64,2048]{1,0:T(8,128)(2,1)S(1)}, bf16[64,2048]{1,0:T(8,128)(2,1)S(1)}, u32[]{:S(2)}, u32[]{:S(2)}) %collective-permute-start.4) | collective-permute-done | bytes 262176 | tf_op jit(solution)/shard_map/ppermute | solution.py:360
  13.3 1.6 %collective-permute-start.8 = (bf16[64,2048]{1,0:T(8,128)(2,1)S(1)}, bf16[64,2048]{1,0:T(8,128)(2,1)S(1)}, u32[]{:S(2)}, u32[]{:S(2)}) collective-permute-start(bf16[64,2048]{1,0:T(8,128)(2,1)S(1)} %collective-permute-done.4.refs_0_), channel_id=1, source_target_pairs={{0,2},{2,4},{4,6},{6,7},{7,5},{5,3},{3,1},{1,0},{8,10},{10,12},{12... | collective-permute-start | bytes 786440 | tf_op jit(solution)/shard_map/ppermute | solution.py:360
  14.9 3.9 %collective-permute-done.7.refs_3_ = bf16[64,2048]{1,0:T(8,128)(2,1)S(1)} collective-permute-done((bf16[64,2048]{1,0:T(8,128)(2,1)S(1)}, bf16[64,2048]{1,0:T(8,128)(2,1)S(1)}, u32[]{:S(2)}, u32[]{:S(2)}) %collective-permute-start.7) | collective-permute-done | bytes 262176 | tf_op jit(solution)/shard_map/ppermute | solution.py:363
  20.1 1.6 %collective-permute-start.9 = (bf16[64,2048]{1,0:T(8,128)(2,1)S(1)}, bf16[64,2048]{1,0:T(8,128)(2,1)S(1)}, u32[]{:S(2)}, u32[]{:S(2)}) collective-permute-start(bf16[64,2048]{1,0:T(8,128)(2,1)S(1)} %collective-permute-done.5.refs_1_), channel_id=1, source_target_pairs={{0,2},{2,4},{4,6},{6,7},{7,5},{5,3},{3,1},{1,0},{8,10},{10,12},{12... | collective-permute-start | bytes 786440 | tf_op jit(solution)/shard_map/ppermute | solution.py:360
  23.1 1.6 %collective-permute-start.12 = (bf16[64,2048]{1,0:T(8,128)(2,1)S(1)}, bf16[64,2048]{1,0:T(8,128)(2,1)S(1)}, u32[]{:S(2)}, u32[]{:S(2)}) collective-permute-start(bf16[64,2048]{1,0:T(8,128)(2,1)S(1)} %collective-permute-done.8.refs_4_), channel_id=1, source_target_pairs={{0,2},{2,4},{4,6},{6,7},{7,5},{5,3},{3,1},{1,0},{8,10},{10,12},{12... | collective-permute-start | bytes 786440 | tf_op jit(solution)/shard_map/ppermute | solution.py:360
  24.7 1.4 %collective-permute-done.11.refs_7_ = bf16[64,2048]{1,0:T(8,128)(2,1)S(1)} collective-permute-done((bf16[64,2048]{1,0:T(8,128)(2,1)S(1)}, bf16[64,2048]{1,0:T(8,128)(2,1)S(1)}, u32[]{:S(2)}, u32[]{:S(2)}) %collective-permute-start.11) | collective-permute-done | bytes 262176 | tf_op jit(solution)/shard_map/ppermute | solution.py:363
  27.3 5.8 %all-to-all-start = ((f32[8,8,128]{2,1,0:T(8,128)}), f32[8,8,128]{2,1,0:T(8,128)S(1)}, u32[]{:S(2)}, u32[]{:S(2)}) async-start(f32[8,8,128]{2,1,0:T(8,128)} %bitcast.22), calls=%async_computation | async-start | bytes 65536 | tf_op jit(solution)/shard_map/all_to_all | solution.py:343
  33.2 2.0 %collective-permute-start.13 = (bf16[64,2048]{1,0:T(8,128)(2,1)S(1)}, bf16[64,2048]{1,0:T(8,128)(2,1)S(1)}, u32[]{:S(2)}, u32[]{:S(2)}) collective-permute-start(bf16[64,2048]{1,0:T(8,128)(2,1)S(1)} %collective-permute-done.9.refs_5_), channel_id=1, source_target_pairs={{0,2},{2,4},{4,6},{6,7},{7,5},{5,3},{3,1},{1,0},{8,10},{10,12},{12... | collective-permute-start | bytes 786440 | tf_op jit(solution)/shard_map/ppermute | solution.py:360
  35.3 4.8 %all-to-all-done.meta = f32[8,8,128]{2,1,0:T(8,128)S(1)} async-done(((f32[8,8,128]{2,1,0:T(8,128)}), f32[8,8,128]{2,1,0:T(8,128)S(1)}, u32[]{:S(2)}, u32[]{:S(2)}) %all-to-all-start) | async-done | bytes 32800 | tf_op jit(solution)/shard_map/all_to_all | solution.py:343
  40.1 1.7 %pick.1 = (bf16[4,224,256]{2,1,0:T(8,128)(2,1)S(1)}, f32[4,320,128]{2,1,0:T(8,128)S(1)}, bf16[4,160,2048]{2,1,0:T(8,128)(2,1)S(1)}) custom-call(s32[2]{0:T(128)S(1)} %pad_add_fusion.where, f32[8,8,128]{2,1,0:T(8,128)S(1)} %all-to-all-done.meta, bf16[64,2048]{1,0:T(8,128)(2,1)S(1)} %collective-permute-done.4.refs_0_, ...), custom_call_target="tpu_custom_call" | custom-call | flops 1000 | bytes 1000 | tf_op jit(solution)/shard_map/pick/pallas_call | solution.py:121
  42.2 1.7 %collective-permute-start.17 = (bf16[64,2048]{1,0:T(8,128)(2,1)S(1)}, bf16[64,2048]{1,0:T(8,128)(2,1)S(1)}, u32[]{:S(2)}, u32[]{:S(2)}) collective-permute-start(bf16[64,2048]{1,0:T(8,128)(2,1)S(1)} %collective-permute-done.15.refs_3_), channel_id=1, source_target_pairs={{2,0},{4,2},{6,4},{7,6},{5,7},{3,5},{1,3},{0,1},{10,8},{12,10},{14... | collective-permute-start | bytes 786440 | tf_op jit(solution)/shard_map/ppermute | solution.py:363
  43.9 7.5 %shared_experts.1 = (bf16[256,2048]{1,0:T(8,128)(2,1)}, bf16[256,2048]{1,0:T(8,128)(2,1)}, bf16[704,2048]{1,0:T(8,128)(2,1)S(1)}, bf16[704,2048]{1,0:T(8,128)(2,1)S(1)}, bf16[704,2048]{1,0:T(8,128)(2,1)S(1)}) custom-call(bf16[256,2048]{1,0:T(8,128)(2,1)} %constant_dynamic-update-slice_fusion.refs_0_, bf16[256,2048]{1,0:T(8,128)(2,1)} %collective-permute-done.1.refs_1_, ...), custom_call_target="tpu_custom_call" | custom-call | flops 1000 | bytes 1000 | tf_op jit(solution)/shard_map/shared_experts/pallas_call | solution.py:291
  51.4 13.7 %routed_experts.1 = (bf16[64,2048]{1,0:T(8,128)(2,1)S(1)}, bf16[64,2048]{1,0:T(8,128)(2,1)S(1)}, bf16[64,2048]{1,0:T(8,128)(2,1)S(1)}, bf16[64,2048]{1,0:T(8,128...) custom-call(s32[2]{0:T(128)S(1)} %pad_add_fusion.where, ...), custom_call_target="tpu_custom_call" | custom-call | flops 8522825728 | bytes 34603008 | tf_op jit(solution)/shard_map/routed_experts/pallas_call | solution.py:227
  66.0 1.2 %collective-permute-start.18 = (bf16[64,2048]{1,0:T(8,128)(2,1)S(1)}, bf16[64,2048]{1,0:T(8,128)(2,1)S(1)}, u32[]{:S(2)}, u32[]{:S(2)}) collective-permute-start(bf16[64,2048]{1,0:T(8,128)(2,1)S(1)} %get-tuple-element.42), channel_id=1, source_target_pairs={{0,2},{2,4},{4,6},{6,7},{7,5},{5,3},{3,1},{1,0},{8,10},{10,12},{12... | collective-permute-start | bytes 786440 | tf_op jit(solution)/shard_map/ppermute | solution.py:403
  68.1 1.2 %collective-permute-start.25 = (bf16[64,2048]{1,0:T(8,128)(2,1)S(1)}, bf16[64,2048]{1,0:T(8,128)(2,1)S(1)}, u32[]{:S(2)}, u32[]{:S(2)}) collective-permute-start(bf16[64,2048]{1,0:T(8,128)(2,1)S(1)} %get-tuple-element.50), channel_id=1, source_target_pairs={{0,2},{2,4},{4,6},{6,7},{7,5},{5,3},{3,1},{1,0},{8,10},{10,12},{12... | collective-permute-start | bytes 786440 | tf_op jit(solution)/shard_map/ppermute | solution.py:403
  69.2 4.0 %collective-permute-done.22 = bf16[64,2048]{1,0:T(8,128)(2,1)S(1)} collective-permute-done((bf16[64,2048]{1,0:T(8,128)(2,1)S(1)}, bf16[64,2048]{1,0:T(8,128)(2,1)S(1)}, u32[]{:S(2)}, u32[]{:S(2)}) %collective-permute-start.22) | collective-permute-done | bytes 262176 | tf_op jit(solution)/shard_map/ppermute | solution.py:403
  75.2 1.2 %collective-permute-start.19 = (bf16[64,2048]{1,0:T(8,128)(2,1)S(1)}, bf16[64,2048]{1,0:T(8,128)(2,1)S(1)}, u32[]{:S(2)}, u32[]{:S(2)}) collective-permute-start(bf16[64,2048]{1,0:T(8,128)(2,1)S(1)} %add_convert_fusion.9), channel_id=1, source_target_pairs={{0,2},{2,4},{4,6},{6,7},{7,5},{5,3},{3,1},{1,0},{8,10},{10,12},{12... | collective-permute-start | bytes 786440 | tf_op jit(solution)/shard_map/ppermute | solution.py:403
  76.4 2.4 %collective-permute-done.28 = bf16[64,2048]{1,0:T(8,128)(2,1)S(1)} collective-permute-done((bf16[64,2048]{1,0:T(8,128)(2,1)S(1)}, bf16[64,2048]{1,0:T(8,128)(2,1)S(1)}, u32[]{:S(2)}, u32[]{:S(2)}) %collective-permute-start.28) | collective-permute-done | bytes 262176 | tf_op jit(solution)/shard_map/ppermute | solution.py:403
  80.8 1.2 %collective-permute-start.26 = (bf16[64,2048]{1,0:T(8,128)(2,1)S(1)}, bf16[64,2048]{1,0:T(8,128)(2,1)S(1)}, u32[]{:S(2)}, u32[]{:S(2)}) collective-permute-start(bf16[64,2048]{1,0:T(8,128)(2,1)S(1)} %add_convert_fusion.4), channel_id=1, source_target_pairs={{0,2},{2,4},{4,6},{6,7},{7,5},{5,3},{3,1},{1,0},{8,10},{10,12},{12... | collective-permute-start | bytes 786440 | tf_op jit(solution)/shard_map/ppermute | solution.py:403
  82.0 2.4 %collective-permute-done.23 = bf16[64,2048]{1,0:T(8,128)(2,1)S(1)} collective-permute-done((bf16[64,2048]{1,0:T(8,128)(2,1)S(1)}, bf16[64,2048]{1,0:T(8,128)(2,1)S(1)}, u32[]{:S(2)}, u32[]{:S(2)}) %collective-permute-start.23) | collective-permute-done | bytes 262176 | tf_op jit(solution)/shard_map/ppermute | solution.py:403
  85.2 1.1 %collective-permute-done.19 = bf16[64,2048]{1,0:T(8,128)(2,1)S(1)} collective-permute-done((bf16[64,2048]{1,0:T(8,128)(2,1)S(1)}, bf16[64,2048]{1,0:T(8,128)(2,1)S(1)}, u32[]{:S(2)}, u32[]{:S(2)}) %collective-permute-start.19) | collective-permute-done | bytes 262176 | tf_op jit(solution)/shard_map/ppermute | solution.py:403
  86.4 1.2 %collective-permute-start.20 = (bf16[64,2048]{1,0:T(8,128)(2,1)S(1)}, bf16[64,2048]{1,0:T(8,128)(2,1)S(1)}, u32[]{:S(2)}, u32[]{:S(2)}) collective-permute-start(bf16[64,2048]{1,0:T(8,128)(2,1)S(1)} %add_convert_fusion.8), channel_id=1, source_target_pairs={{0,2},{2,4},{4,6},{6,7},{7,5},{5,3},{3,1},{1,0},{8,10},{10,12},{12... | collective-permute-start | bytes 786440 | tf_op jit(solution)/shard_map/ppermute | solution.py:403
  87.7 2.4 %collective-permute-done.29 = bf16[64,2048]{1,0:T(8,128)(2,1)S(1)} collective-permute-done((bf16[64,2048]{1,0:T(8,128)(2,1)S(1)}, bf16[64,2048]{1,0:T(8,128)(2,1)S(1)}, u32[]{:S(2)}, u32[]{:S(2)}) %collective-permute-start.29) | collective-permute-done | bytes 262176 | tf_op jit(solution)/shard_map/ppermute | solution.py:403
  92.1 1.2 %collective-permute-start.27 = (bf16[64,2048]{1,0:T(8,128)(2,1)S(1)}, bf16[64,2048]{1,0:T(8,128)(2,1)S(1)}, u32[]{:S(2)}, u32[]{:S(2)}) collective-permute-start(bf16[64,2048]{1,0:T(8,128)(2,1)S(1)} %add_convert_fusion.3), channel_id=1, source_target_pairs={{0,2},{2,4},{4,6},{6,7},{7,5},{5,3},{3,1},{1,0},{8,10},{10,12},{12... | collective-permute-start | bytes 786440 | tf_op jit(solution)/shard_map/ppermute | solution.py:403
  94.3 3.4 %collective-permute-done.20 = bf16[64,2048]{1,0:T(8,128)(2,1)S(1)} collective-permute-done((bf16[64,2048]{1,0:T(8,128)(2,1)S(1)}, bf16[64,2048]{1,0:T(8,128)(2,1)S(1)}, u32[]{:S(2)}, u32[]{:S(2)}) %collective-permute-start.20) | collective-permute-done | bytes 262176 | tf_op jit(solution)/shard_map/ppermute | solution.py:403
  97.7 1.2 %collective-permute-start.21 = (bf16[64,2048]{1,0:T(8,128)(2,1)S(1)}, bf16[64,2048]{1,0:T(8,128)(2,1)S(1)}, u32[]{:S(2)}, u32[]{:S(2)}) collective-permute-start(bf16[64,2048]{1,0:T(8,128)(2,1)S(1)} %add_convert_fusion.7), channel_id=1, source_target_pairs={{0,2},{2,4},{4,6},{6,7},{7,5},{5,3},{3,1},{1,0},{8,10},{10,12},{12... | collective-permute-start | bytes 786440 | tf_op jit(solution)/shard_map/ppermute | solution.py:403
  100.6 6.0 %collective-permute-done.3 = bf16[128,2048]{1,0:T(8,128)(2,1)S(1)} collective-permute-done((bf16[128,2048]{1,0:T(8,128)(2,1)S(1)}, bf16[128,2048]{1,0:T(8,128)(2,1)S(1)}, u32[]{:S(2)}, u32[]{:S(2)}) %collective-permute-start.3) | collective-permute-done | bytes 524320 | tf_op jit(solution)/shard_map/ppermute | solution.py:383
  106.8 1.7 %collective-permute-done.21 = bf16[64,2048]{1,0:T(8,128)(2,1)S(1)} collective-permute-done((bf16[64,2048]{1,0:T(8,128)(2,1)S(1)}, bf16[64,2048]{1,0:T(8,128)(2,1)S(1)}, u32[]{:S(2)}, u32[]{:S(2)}) %collective-permute-start.21) | collective-permute-done | bytes 262176 | tf_op jit(solution)/shard_map/ppermute | solution.py:403
  (72 shorter events, 20.0 us)
Async XLA Ops:
  0.0 19.2 %collective-permute-start = (bf16[128,2048]{1,0:T(8,128)(2,1)}, bf16[128,2048]{1,0:T(8,128)(2,1)S(1)}, u32[]{:S(2)}, u32[]{:S(2)}) collective-permute-start(bf16[128,2048]{1,0:T(8,128)(2,1)} %refs_4_.3), channel_id=1, source_target_pairs={{0,16},{8,24},{16,0},{24,8},{1,17},{9,25},{17,1},{25,9},{2,18},{10... | collective-permute-start | bytes 1572872 | tf_op jit(solution)/shard_map/ppermute | solution.py:368
  4.0 9.3 %collective-permute-start.4 = (bf16[64,2048]{1,0:T(8,128)(2,1)S(1)}, bf16[64,2048]{1,0:T(8,128)(2,1)S(1)}, u32[]{:S(2)}, u32[]{:S(2)}) collective-permute-start(bf16[64,2048]{1,0:T(8,128)(2,1)S(1)} %get-tuple-element.60), channel_id=1, source_target_pairs={{0,2},{2,4},{4,6},{6,7},{7,5},{5,3},{3,1},{1,0},{8,10},{10,12},{12... | collective-permute-start | bytes 786440 | tf_op jit(solution)/shard_map/ppermute | solution.py:360
  5.7 16.1 %collective-permute-start.6 = (bf16[64,2048]{1,0:T(8,128)(2,1)S(1)}, bf16[64,2048]{1,0:T(8,128)(2,1)S(1)}, u32[]{:S(2)}, u32[]{:S(2)}) collective-permute-start(bf16[64,2048]{1,0:T(8,128)(2,1)S(1)} %get-tuple-element.60), channel_id=1, source_target_pairs={{2,0},{4,2},{6,4},{7,6},{5,7},{3,5},{1,3},{0,1},{10,8},{12,10},{14... | collective-permute-start | bytes 786440 | tf_op jit(solution)/shard_map/ppermute | solution.py:363
  6.1 14.0 %collective-permute-start.5 = (bf16[64,2048]{1,0:T(8,128)(2,1)S(1)}, bf16[64,2048]{1,0:T(8,128)(2,1)S(1)}, u32[]{:S(2)}, u32[]{:S(2)}) collective-permute-start(bf16[64,2048]{1,0:T(8,128)(2,1)S(1)} %get-tuple-element.59), channel_id=1, source_target_pairs={{0,2},{2,4},{4,6},{6,7},{7,5},{5,3},{3,1},{1,0},{8,10},{10,12},{12... | collective-permute-start | bytes 786440 | tf_op jit(solution)/shard_map/ppermute | solution.py:360
  7.7 11.1 %collective-permute-start.7 = (bf16[64,2048]{1,0:T(8,128)(2,1)S(1)}, bf16[64,2048]{1,0:T(8,128)(2,1)S(1)}, u32[]{:S(2)}, u32[]{:S(2)}) collective-permute-start(bf16[64,2048]{1,0:T(8,128)(2,1)S(1)} %get-tuple-element.59), channel_id=1, source_target_pairs={{2,0},{4,2},{6,4},{7,6},{5,7},{3,5},{1,3},{0,1},{10,8},{12,10},{14... | collective-permute-start | bytes 786440 | tf_op jit(solution)/shard_map/ppermute | solution.py:363
  13.3 9.8 %collective-permute-start.8 = (bf16[64,2048]{1,0:T(8,128)(2,1)S(1)}, bf16[64,2048]{1,0:T(8,128)(2,1)S(1)}, u32[]{:S(2)}, u32[]{:S(2)}) collective-permute-start(bf16[64,2048]{1,0:T(8,128)(2,1)S(1)} %collective-permute-done.4.refs_0_), channel_id=1, source_target_pairs={{0,2},{2,4},{4,6},{6,7},{7,5},{5,3},{3,1},{1,0},{8,10},{10,12},{12... | collective-permute-start | bytes 786440 | tf_op jit(solution)/shard_map/ppermute | solution.py:360
  20.1 23.8 %collective-permute-start.1 = (bf16[256,2048]{1,0:T(8,128)(2,1)}, bf16[256,2048]{1,0:T(8,128)(2,1)}, u32[]{:S(2)}, u32[]{:S(2)}) collective-permute-start(bf16[256,2048]{1,0:T(8,128)(2,1)} %constant_dynamic-update-slice_fusion.refs_0_), channel_id=1, source_target_pairs={{0,8},{8,0},{16,24},{24,16},{1,9},{9,1},{17,25},{25,17},{2,10},{10... | collective-permute-start | bytes 3145736 | tf_op jit(solution)/shard_map/ppermute | solution.py:372
  20.1 13.0 %collective-permute-start.9 = (bf16[64,2048]{1,0:T(8,128)(2,1)S(1)}, bf16[64,2048]{1,0:T(8,128)(2,1)S(1)}, u32[]{:S(2)}, u32[]{:S(2)}) collective-permute-start(bf16[64,2048]{1,0:T(8,128)(2,1)S(1)} %collective-permute-done.5.refs_1_), channel_id=1, source_target_pairs={{0,2},{2,4},{4,6},{6,7},{7,5},{5,3},{3,1},{1,0},{8,10},{10,12},{12... | collective-permute-start | bytes 786440 | tf_op jit(solution)/shard_map/ppermute | solution.py:360
  21.7 13.4 %collective-permute-start.10 = (bf16[64,2048]{1,0:T(8,128)(2,1)S(1)}, bf16[64,2048]{1,0:T(8,128)(2,1)S(1)}, u32[]{:S(2)}, u32[]{:S(2)}) collective-permute-start(bf16[64,2048]{1,0:T(8,128)(2,1)S(1)} %collective-permute-done.6.refs_2_), channel_id=1, source_target_pairs={{2,0},{4,2},{6,4},{7,6},{5,7},{3,5},{1,3},{0,1},{10,8},{12,10},{14... | collective-permute-start | bytes 786440 | tf_op jit(solution)/shard_map/ppermute | solution.py:363
  23.1 18.7 %collective-permute-start.12 = (bf16[64,2048]{1,0:T(8,128)(2,1)S(1)}, bf16[64,2048]{1,0:T(8,128)(2,1)S(1)}, u32[]{:S(2)}, u32[]{:S(2)}) collective-permute-start(bf16[64,2048]{1,0:T(8,128)(2,1)S(1)} %collective-permute-done.8.refs_4_), channel_id=1, source_target_pairs={{0,2},{2,4},{4,6},{6,7},{7,5},{5,3},{3,1},{1,0},{8,10},{10,12},{12... | collective-permute-start | bytes 786440 | tf_op jit(solution)/shard_map/ppermute | solution.py:360
  26.0 15.8 %collective-permute-start.15 = (bf16[64,2048]{1,0:T(8,128)(2,1)S(1)}, bf16[64,2048]{1,0:T(8,128)(2,1)S(1)}, u32[]{:S(2)}, u32[]{:S(2)}) collective-permute-start(bf16[64,2048]{1,0:T(8,128)(2,1)S(1)} %collective-permute-done.11.refs_7_), channel_id=1, source_target_pairs={{2,0},{4,2},{6,4},{7,6},{5,7},{3,5},{1,3},{0,1},{10,8},{12,10},{14... | collective-permute-start | bytes 786440 | tf_op jit(solution)/shard_map/ppermute | solution.py:363
  27.3 12.8 %all-to-all-start = ((f32[8,8,128]{2,1,0:T(8,128)}), f32[8,8,128]{2,1,0:T(8,128)S(1)}, u32[]{:S(2)}, u32[]{:S(2)}) async-start(f32[8,8,128]{2,1,0:T(8,128)} %bitcast.22), calls=%async_computation | async-start | bytes 65536 | tf_op jit(solution)/shard_map/all_to_all | solution.py:343
  33.2 18.2 %collective-permute-start.13 = (bf16[64,2048]{1,0:T(8,128)(2,1)S(1)}, bf16[64,2048]{1,0:T(8,128)(2,1)S(1)}, u32[]{:S(2)}, u32[]{:S(2)}) collective-permute-start(bf16[64,2048]{1,0:T(8,128)(2,1)S(1)} %collective-permute-done.9.refs_5_), channel_id=1, source_target_pairs={{0,2},{2,4},{4,6},{6,7},{7,5},{5,3},{3,1},{1,0},{8,10},{10,12},{12... | collective-permute-start | bytes 786440 | tf_op jit(solution)/shard_map/ppermute | solution.py:360
  35.2 16.2 %collective-permute-start.14 = (bf16[64,2048]{1,0:T(8,128)(2,1)S(1)}, bf16[64,2048]{1,0:T(8,128)(2,1)S(1)}, u32[]{:S(2)}, u32[]{:S(2)}) collective-permute-start(bf16[64,2048]{1,0:T(8,128)(2,1)S(1)} %collective-permute-done.10.refs_6_), channel_id=1, source_target_pairs={{2,0},{4,2},{6,4},{7,6},{5,7},{3,5},{1,3},{0,1},{10,8},{12,10},{14... | collective-permute-start | bytes 786440 | tf_op jit(solution)/shard_map/ppermute | solution.py:363
  41.8 9.6 %collective-permute-start.16 = (bf16[64,2048]{1,0:T(8,128)(2,1)S(1)}, bf16[64,2048]{1,0:T(8,128)(2,1)S(1)}, u32[]{:S(2)}, u32[]{:S(2)}) collective-permute-start(bf16[64,2048]{1,0:T(8,128)(2,1)S(1)} %collective-permute-done.12.refs_0_), channel_id=1, source_target_pairs={{0,2},{2,4},{4,6},{6,7},{7,5},{5,3},{3,1},{1,0},{8,10},{10,12},{12... | collective-permute-start | bytes 786440 | tf_op jit(solution)/shard_map/ppermute | solution.py:360
  42.2 9.2 %collective-permute-start.17 = (bf16[64,2048]{1,0:T(8,128)(2,1)S(1)}, bf16[64,2048]{1,0:T(8,128)(2,1)S(1)}, u32[]{:S(2)}, u32[]{:S(2)}) collective-permute-start(bf16[64,2048]{1,0:T(8,128)(2,1)S(1)} %collective-permute-done.15.refs_3_), channel_id=1, source_target_pairs={{2,0},{4,2},{6,4},{7,6},{5,7},{3,5},{1,3},{0,1},{10,8},{12,10},{14... | collective-permute-start | bytes 786440 | tf_op jit(solution)/shard_map/ppermute | solution.py:363
  65.1 8.1 %collective-permute-start.22 = (bf16[64,2048]{1,0:T(8,128)(2,1)S(1)}, bf16[64,2048]{1,0:T(8,128)(2,1)S(1)}, u32[]{:S(2)}, u32[]{:S(2)}) collective-permute-start(bf16[64,2048]{1,0:T(8,128)(2,1)S(1)} %get-tuple-element.46), channel_id=1, source_target_pairs={{2,0},{4,2},{6,4},{7,6},{5,7},{3,5},{1,3},{0,1},{10,8},{12,10},{14... | collective-permute-start | bytes 786440 | tf_op jit(solution)/shard_map/ppermute | solution.py:403
  66.0 27.2 %collective-permute-start.2 = (bf16[256,2048]{1,0:T(8,128)(2,1)S(1)}, bf16[256,2048]{1,0:T(8,128)(2,1)S(1)}, u32[]{:S(2)}, u32[]{:S(2)}) collective-permute-start(bf16[256,2048]{1,0:T(8,128)(2,1)S(1)} %copy-done.3), channel_id=1, source_target_pairs={{0,8},{8,0},{16,24},{24,16},{1,9},{9,1},{17,25},{25,17},{2,10},{10... | collective-permute-start | bytes 3145736 | tf_op jit(solution)/shard_map/ppermute | solution.py:374
  66.0 9.1 %collective-permute-start.18 = (bf16[64,2048]{1,0:T(8,128)(2,1)S(1)}, bf16[64,2048]{1,0:T(8,128)(2,1)S(1)}, u32[]{:S(2)}, u32[]{:S(2)}) collective-permute-start(bf16[64,2048]{1,0:T(8,128)(2,1)S(1)} %get-tuple-element.42), channel_id=1, source_target_pairs={{0,2},{2,4},{4,6},{6,7},{7,5},{5,3},{3,1},{1,0},{8,10},{10,12},{12... | collective-permute-start | bytes 786440 | tf_op jit(solution)/shard_map/ppermute | solution.py:403
  67.2 11.6 %collective-permute-start.28 = (bf16[64,2048]{1,0:T(8,128)(2,1)S(1)}, bf16[64,2048]{1,0:T(8,128)(2,1)S(1)}, u32[]{:S(2)}, u32[]{:S(2)}) collective-permute-start(bf16[64,2048]{1,0:T(8,128)(2,1)S(1)} %get-tuple-element.53), channel_id=1, source_target_pairs={{2,0},{4,2},{6,4},{7,6},{5,7},{3,5},{1,3},{0,1},{10,8},{12,10},{14... | collective-permute-start | bytes 786440 | tf_op jit(solution)/shard_map/ppermute | solution.py:403
  68.1 12.7 %collective-permute-start.25 = (bf16[64,2048]{1,0:T(8,128)(2,1)S(1)}, bf16[64,2048]{1,0:T(8,128)(2,1)S(1)}, u32[]{:S(2)}, u32[]{:S(2)}) collective-permute-start(bf16[64,2048]{1,0:T(8,128)(2,1)S(1)} %get-tuple-element.50), channel_id=1, source_target_pairs={{0,2},{2,4},{4,6},{6,7},{7,5},{5,3},{3,1},{1,0},{8,10},{10,12},{12... | collective-permute-start | bytes 786440 | tf_op jit(solution)/shard_map/ppermute | solution.py:403
  73.3 11.2 %collective-permute-start.23 = (bf16[64,2048]{1,0:T(8,128)(2,1)S(1)}, bf16[64,2048]{1,0:T(8,128)(2,1)S(1)}, u32[]{:S(2)}, u32[]{:S(2)}) collective-permute-start(bf16[64,2048]{1,0:T(8,128)(2,1)S(1)} %add_convert_fusion.6), channel_id=1, source_target_pairs={{2,0},{4,2},{6,4},{7,6},{5,7},{3,5},{1,3},{0,1},{10,8},{12,10},{14... | collective-permute-start | bytes 786440 | tf_op jit(solution)/shard_map/ppermute | solution.py:403
  75.2 11.2 %collective-permute-start.19 = (bf16[64,2048]{1,0:T(8,128)(2,1)S(1)}, bf16[64,2048]{1,0:T(8,128)(2,1)S(1)}, u32[]{:S(2)}, u32[]{:S(2)}) collective-permute-start(bf16[64,2048]{1,0:T(8,128)(2,1)S(1)} %add_convert_fusion.9), channel_id=1, source_target_pairs={{0,2},{2,4},{4,6},{6,7},{7,5},{5,3},{3,1},{1,0},{8,10},{10,12},{12... | collective-permute-start | bytes 786440 | tf_op jit(solution)/shard_map/ppermute | solution.py:403
  78.9 11.2 %collective-permute-start.29 = (bf16[64,2048]{1,0:T(8,128)(2,1)S(1)}, bf16[64,2048]{1,0:T(8,128)(2,1)S(1)}, u32[]{:S(2)}, u32[]{:S(2)}) collective-permute-start(bf16[64,2048]{1,0:T(8,128)(2,1)S(1)} %add_convert_fusion.2), channel_id=1, source_target_pairs={{2,0},{4,2},{6,4},{7,6},{5,7},{3,5},{1,3},{0,1},{10,8},{12,10},{14... | collective-permute-start | bytes 786440 | tf_op jit(solution)/shard_map/ppermute | solution.py:403
  80.8 11.2 %collective-permute-start.26 = (bf16[64,2048]{1,0:T(8,128)(2,1)S(1)}, bf16[64,2048]{1,0:T(8,128)(2,1)S(1)}, u32[]{:S(2)}, u32[]{:S(2)}) collective-permute-start(bf16[64,2048]{1,0:T(8,128)(2,1)S(1)} %add_convert_fusion.4), channel_id=1, source_target_pairs={{0,2},{2,4},{4,6},{6,7},{7,5},{5,3},{3,1},{1,0},{8,10},{10,12},{12... | collective-permute-start | bytes 786440 | tf_op jit(solution)/shard_map/ppermute | solution.py:403
  84.5 22.3 %collective-permute-start.24 = (bf16[64,2048]{1,0:T(8,128)(2,1)S(1)}, bf16[64,2048]{1,0:T(8,128)(2,1)S(1)}, u32[]{:S(2)}, u32[]{:S(2)}) collective-permute-start(bf16[64,2048]{1,0:T(8,128)(2,1)S(1)} %add_convert_fusion.5), channel_id=1, source_target_pairs={{2,0},{4,2},{6,4},{7,6},{5,7},{3,5},{1,3},{0,1},{10,8},{12,10},{14... | collective-permute-start | bytes 786440 | tf_op jit(solution)/shard_map/ppermute | solution.py:403
  86.4 11.2 %collective-permute-start.20 = (bf16[64,2048]{1,0:T(8,128)(2,1)S(1)}, bf16[64,2048]{1,0:T(8,128)(2,1)S(1)}, u32[]{:S(2)}, u32[]{:S(2)}) collective-permute-start(bf16[64,2048]{1,0:T(8,128)(2,1)S(1)} %add_convert_fusion.8), channel_id=1, source_target_pairs={{0,2},{2,4},{4,6},{6,7},{7,5},{5,3},{3,1},{1,0},{8,10},{10,12},{12... | collective-permute-start | bytes 786440 | tf_op jit(solution)/shard_map/ppermute | solution.py:403
  90.1 9.6 %collective-permute-start.30 = (bf16[64,2048]{1,0:T(8,128)(2,1)S(1)}, bf16[64,2048]{1,0:T(8,128)(2,1)S(1)}, u32[]{:S(2)}, u32[]{:S(2)}) collective-permute-start(bf16[64,2048]{1,0:T(8,128)(2,1)S(1)} %add_convert_fusion.1), channel_id=1, source_target_pairs={{2,0},{4,2},{6,4},{7,6},{5,7},{3,5},{1,3},{0,1},{10,8},{12,10},{14... | collective-permute-start | bytes 786440 | tf_op jit(solution)/shard_map/ppermute | solution.py:403
  92.1 14.7 %collective-permute-start.27 = (bf16[64,2048]{1,0:T(8,128)(2,1)S(1)}, bf16[64,2048]{1,0:T(8,128)(2,1)S(1)}, u32[]{:S(2)}, u32[]{:S(2)}) collective-permute-start(bf16[64,2048]{1,0:T(8,128)(2,1)S(1)} %add_convert_fusion.3), channel_id=1, source_target_pairs={{0,2},{2,4},{4,6},{6,7},{7,5},{5,3},{3,1},{1,0},{8,10},{10,12},{12... | collective-permute-start | bytes 786440 | tf_op jit(solution)/shard_map/ppermute | solution.py:403
  93.7 13.0 %collective-permute-start.3 = (bf16[128,2048]{1,0:T(8,128)(2,1)S(1)}, bf16[128,2048]{1,0:T(8,128)(2,1)S(1)}, u32[]{:S(2)}, u32[]{:S(2)}) collective-permute-start(bf16[128,2048]{1,0:T(8,128)(2,1)S(1)} %slice.107), channel_id=1, source_target_pairs={{0,16},{8,24},{16,0},{24,8},{1,17},{9,25},{17,1},{25,9},{2,18},{10... | collective-permute-start | bytes 1572872 | tf_op jit(solution)/shard_map/ppermute | solution.py:383
  97.7 10.8 %collective-permute-start.21 = (bf16[64,2048]{1,0:T(8,128)(2,1)S(1)}, bf16[64,2048]{1,0:T(8,128)(2,1)S(1)}, u32[]{:S(2)}, u32[]{:S(2)}) collective-permute-start(bf16[64,2048]{1,0:T(8,128)(2,1)S(1)} %add_convert_fusion.7), channel_id=1, source_target_pairs={{0,2},{2,4},{4,6},{6,7},{7,5},{5,3},{3,1},{1,0},{8,10},{10,12},{12... | collective-permute-start | bytes 786440 | tf_op jit(solution)/shard_map/ppermute | solution.py:403
  99.8 8.7 %collective-permute-start.31 = (bf16[64,2048]{1,0:T(8,128)(2,1)S(1)}, bf16[64,2048]{1,0:T(8,128)(2,1)S(1)}, u32[]{:S(2)}, u32[]{:S(2)}) collective-permute-start(bf16[64,2048]{1,0:T(8,128)(2,1)S(1)} %add_convert_fusion), channel_id=1, source_target_pairs={{2,0},{4,2},{6,4},{7,6},{5,7},{3,5},{1,3},{0,1},{10,8},{12,10},{14... | collective-permute-start | bytes 786440 | tf_op jit(solution)/shard_map/ppermute | solution.py:403
  (6 other events, 83.9 us)

commit v6 on v5

--- a/solution.py
+++ b/solution.py
@@ -263,10 +263,12 @@
         pltpu.make_async_copy(source.at[0], target, sem_r.at[k])
         for k, (source, target) in enumerate(zip(ahead, ready))
     ]
-    for copy in loads + fetches:
+    for copy in loads:
         copy.start()
     for copy in loads[:-2]:
         copy.wait()
+    for copy in fetches:
+        copy.start()
     gate = dot(x[...], wg[...])
     loads[-2].wait()
     upper = dot(x[...], wu[...])

time: 110 us -> 110 us (level)
  waiting for transfers between devices: 40.4 us -> 38.6 us
  starting transfers between devices: 37.6 us -> 39.3 us
    ppermute x14, waiting for transfers between devices: 21.6 us -> 19.9 us  [on_device(): came = lax.ppermute(acc, 'expert', perm)]
where the time goes in v6:
time: 110 us; the launch traced here: 109 us
  starting transfers between devices  39.3 us (36%)
  waiting for transfers between devices  38.6 us (35%)
  Pallas kernels  22.6 us (21%)
  local copies, waits for them, and re-layouts  5.42 us (5%)
  other arithmetic  2.37 us (2%)
    ppermute x14, waiting for transfers between devices, on_device(): came = lax.ppermute(acc, 'expert', perm)  19.9 us
    ppermute x14, starting transfers between devices, on_device(): came = lax.ppermute(acc, 'expert', perm)  14.8 us
    pallas_call x1, Pallas kernels, run_experts(): pl.pallas_call(functools.partial(experts_kernel, offsets, early, sizes, l...  13.7 us
    ppermute x7, starting transfers between devices, on_device(): up[h] = lax.ppermute(up[h], 'expert', forward)  10.4 us
    pallas_call x1, Pallas kernels, run_shared(): pl.pallas_call(functools.partial(shared_kernel, count), out_shape=[pltpu....  7.17 us
    ppermute x1, waiting for transfers between devices, on_device(): came = lax.ppermute(part.pop(r).astype(BF16), 'dp', swap)  6.04 us
    all_to_all x1, starting transfers between devices, on_device(): lax.all_to_all(info, 'expert', split_axis=0, concat_axis=0, tiled=True)  5.81 us
    ppermute x7, waiting for transfers between devices, on_device(): down[h] = lax.ppermute(down[h], 'expert', backward)  5.25 us
  transfers between devices with their start and end apart: 33, of which 17 were waited for; matrix products, arithmetic and copies ran while one was open for 6% of the time, Pallas kernels for 8%

profile of v6, /device:TPU:0, one launch (start us, length us, event | category | flops | bytes accessed | tf_op | source)
XLA Modules:
  0.0 109.3 jit_solution(6358781246126368396)
XLA Ops:
  0.0 3.0 %collective-permute-start = (bf16[128,2048]{1,0:T(8,128)(2,1)}, bf16[128,2048]{1,0:T(8,128)(2,1)S(1)}, u32[]{:S(2)}, u32[]{:S(2)}) collective-permute-start(bf16[128,2048]{1,0:T(8,128)(2,1)} %refs_4_.3), channel_id=1, source_target_pairs={{0,16},{8,24},{16,0},{24,8},{1,17},{9,25},{17,1},{25,9},{2,18},{10... | collective-permute-start | bytes 1572872 | tf_op jit(solution)/shard_map/ppermute | solution.py:370
  4.0 1.6 %collective-permute-start.4 = (bf16[64,2048]{1,0:T(8,128)(2,1)S(1)}, bf16[64,2048]{1,0:T(8,128)(2,1)S(1)}, u32[]{:S(2)}, u32[]{:S(2)}) collective-permute-start(bf16[64,2048]{1,0:T(8,128)(2,1)S(1)} %get-tuple-element.60), channel_id=1, source_target_pairs={{0,2},{2,4},{4,6},{6,7},{7,5},{5,3},{3,1},{1,0},{8,10},{10,12},{12... | collective-permute-start | bytes 786440 | tf_op jit(solution)/shard_map/ppermute | solution.py:362
  6.1 1.6 %collective-permute-start.5 = (bf16[64,2048]{1,0:T(8,128)(2,1)S(1)}, bf16[64,2048]{1,0:T(8,128)(2,1)S(1)}, u32[]{:S(2)}, u32[]{:S(2)}) collective-permute-start(bf16[64,2048]{1,0:T(8,128)(2,1)S(1)} %get-tuple-element.59), channel_id=1, source_target_pairs={{0,2},{2,4},{4,6},{6,7},{7,5},{5,3},{3,1},{1,0},{8,10},{10,12},{12... | collective-permute-start | bytes 786440 | tf_op jit(solution)/shard_map/ppermute | solution.py:362
  9.7 1.9 %constant_dynamic-update-slice_fusion.1 = bf16[256,2048]{1,0:T(8,128)(2,1)} fusion(bf16[128,2048]{1,0:T(8,128)(2,1)} %refs_4_.3), kind=kLoop, calls=%fused_computation.40 | loop fusion | bytes 1048576
  11.6 1.7 %collective-permute-done.4.refs_0_ = bf16[64,2048]{1,0:T(8,128)(2,1)S(1)} collective-permute-done((bf16[64,2048]{1,0:T(8,128)(2,1)S(1)}, bf16[64,2048]{1,0:T(8,128)(2,1)S(1)}, u32[]{:S(2)}, u32[]{:S(2)}) %collective-permute-start.4) | collective-permute-done | bytes 262176 | tf_op jit(solution)/shard_map/ppermute | solution.py:362
  13.3 1.6 %collective-permute-start.8 = (bf16[64,2048]{1,0:T(8,128)(2,1)S(1)}, bf16[64,2048]{1,0:T(8,128)(2,1)S(1)}, u32[]{:S(2)}, u32[]{:S(2)}) collective-permute-start(bf16[64,2048]{1,0:T(8,128)(2,1)S(1)} %collective-permute-done.4.refs_0_), channel_id=1, source_target_pairs={{0,2},{2,4},{4,6},{6,7},{7,5},{5,3},{3,1},{1,0},{8,10},{10,12},{12... | collective-permute-start | bytes 786440 | tf_op jit(solution)/shard_map/ppermute | solution.py:362
  14.9 3.9 %collective-permute-done.7.refs_3_ = bf16[64,2048]{1,0:T(8,128)(2,1)S(1)} collective-permute-done((bf16[64,2048]{1,0:T(8,128)(2,1)S(1)}, bf16[64,2048]{1,0:T(8,128)(2,1)S(1)}, u32[]{:S(2)}, u32[]{:S(2)}) %collective-permute-start.7) | collective-permute-done | bytes 262176 | tf_op jit(solution)/shard_map/ppermute | solution.py:365
  20.1 1.6 %collective-permute-start.9 = (bf16[64,2048]{1,0:T(8,128)(2,1)S(1)}, bf16[64,2048]{1,0:T(8,128)(2,1)S(1)}, u32[]{:S(2)}, u32[]{:S(2)}) collective-permute-start(bf16[64,2048]{1,0:T(8,128)(2,1)S(1)} %collective-permute-done.5.refs_1_), channel_id=1, source_target_pairs={{0,2},{2,4},{4,6},{6,7},{7,5},{5,3},{3,1},{1,0},{8,10},{10,12},{12... | collective-permute-start | bytes 786440 | tf_op jit(solution)/shard_map/ppermute | solution.py:362
  23.1 1.6 %collective-permute-start.12 = (bf16[64,2048]{1,0:T(8,128)(2,1)S(1)}, bf16[64,2048]{1,0:T(8,128)(2,1)S(1)}, u32[]{:S(2)}, u32[]{:S(2)}) collective-permute-start(bf16[64,2048]{1,0:T(8,128)(2,1)S(1)} %collective-permute-done.8.refs_4_), channel_id=1, source_target_pairs={{0,2},{2,4},{4,6},{6,7},{7,5},{5,3},{3,1},{1,0},{8,10},{10,12},{12... | collective-permute-start | bytes 786440 | tf_op jit(solution)/shard_map/ppermute | solution.py:362
  24.7 1.4 %collective-permute-done.11.refs_7_ = bf16[64,2048]{1,0:T(8,128)(2,1)S(1)} collective-permute-done((bf16[64,2048]{1,0:T(8,128)(2,1)S(1)}, bf16[64,2048]{1,0:T(8,128)(2,1)S(1)}, u32[]{:S(2)}, u32[]{:S(2)}) %collective-permute-start.11) | collective-permute-done | bytes 262176 | tf_op jit(solution)/shard_map/ppermute | solution.py:365
  27.3 5.8 %all-to-all-start = ((f32[8,8,128]{2,1,0:T(8,128)}), f32[8,8,128]{2,1,0:T(8,128)S(1)}, u32[]{:S(2)}, u32[]{:S(2)}) async-start(f32[8,8,128]{2,1,0:T(8,128)} %bitcast.22), calls=%async_computation | async-start | bytes 65536 | tf_op jit(solution)/shard_map/all_to_all | solution.py:345
  33.2 2.0 %collective-permute-start.13 = (bf16[64,2048]{1,0:T(8,128)(2,1)S(1)}, bf16[64,2048]{1,0:T(8,128)(2,1)S(1)}, u32[]{:S(2)}, u32[]{:S(2)}) collective-permute-start(bf16[64,2048]{1,0:T(8,128)(2,1)S(1)} %collective-permute-done.9.refs_5_), channel_id=1, source_target_pairs={{0,2},{2,4},{4,6},{6,7},{7,5},{5,3},{3,1},{1,0},{8,10},{10,12},{12... | collective-permute-start | bytes 786440 | tf_op jit(solution)/shard_map/ppermute | solution.py:362
  35.3 4.8 %all-to-all-done.meta = f32[8,8,128]{2,1,0:T(8,128)S(1)} async-done(((f32[8,8,128]{2,1,0:T(8,128)}), f32[8,8,128]{2,1,0:T(8,128)S(1)}, u32[]{:S(2)}, u32[]{:S(2)}) %all-to-all-start) | async-done | bytes 32800 | tf_op jit(solution)/shard_map/all_to_all | solution.py:345
  40.1 1.7 %pick.1 = (bf16[4,224,256]{2,1,0:T(8,128)(2,1)S(1)}, f32[4,320,128]{2,1,0:T(8,128)S(1)}, bf16[4,160,2048]{2,1,0:T(8,128)(2,1)S(1)}) custom-call(s32[2]{0:T(128)S(1)} %pad_add_fusion.where, f32[8,8,128]{2,1,0:T(8,128)S(1)} %all-to-all-done.meta, bf16[64,2048]{1,0:T(8,128)(2,1)S(1)} %collective-permute-done.4.refs_0_, ...), custom_call_target="tpu_custom_call" | custom-call | flops 1000 | bytes 1000 | tf_op jit(solution)/shard_map/pick/pallas_call | solution.py:121
  42.2 1.7 %collective-permute-start.17 = (bf16[64,2048]{1,0:T(8,128)(2,1)S(1)}, bf16[64,2048]{1,0:T(8,128)(2,1)S(1)}, u32[]{:S(2)}, u32[]{:S(2)}) collective-permute-start(bf16[64,2048]{1,0:T(8,128)(2,1)S(1)} %collective-permute-done.15.refs_3_), channel_id=1, source_target_pairs={{2,0},{4,2},{6,4},{7,6},{5,7},{3,5},{1,3},{0,1},{10,8},{12,10},{14... | collective-permute-start | bytes 786440 | tf_op jit(solution)/shard_map/ppermute | solution.py:365
  43.9 7.2 %shared_experts.1 = (bf16[256,2048]{1,0:T(8,128)(2,1)}, bf16[256,2048]{1,0:T(8,128)(2,1)}, bf16[704,2048]{1,0:T(8,128)(2,1)S(1)}, bf16[704,2048]{1,0:T(8,128)(2,1)S(1)}, bf16[704,2048]{1,0:T(8,128)(2,1)S(1)}) custom-call(bf16[256,2048]{1,0:T(8,128)(2,1)} %constant_dynamic-update-slice_fusion.refs_0_, bf16[256,2048]{1,0:T(8,128)(2,1)} %collective-permute-done.1.refs_1_, ...), custom_call_target="tpu_custom_call" | custom-call | flops 1000 | bytes 1000 | tf_op jit(solution)/shard_map/shared_experts/pallas_call | solution.py:293
  51.1 13.7 %routed_experts.1 = (bf16[64,2048]{1,0:T(8,128)(2,1)S(1)}, bf16[64,2048]{1,0:T(8,128)(2,1)S(1)}, bf16[64,2048]{1,0:T(8,128)(2,1)S(1)}, bf16[64,2048]{1,0:T(8,128...) custom-call(s32[2]{0:T(128)S(1)} %pad_add_fusion.where, ...), custom_call_target="tpu_custom_call" | custom-call | flops 8522825728 | bytes 34603008 | tf_op jit(solution)/shard_map/routed_experts/pallas_call | solution.py:227
  65.7 1.2 %collective-permute-start.18 = (bf16[64,2048]{1,0:T(8,128)(2,1)S(1)}, bf16[64,2048]{1,0:T(8,128)(2,1)S(1)}, u32[]{:S(2)}, u32[]{:S(2)}) collective-permute-start(bf16[64,2048]{1,0:T(8,128)(2,1)S(1)} %get-tuple-element.42), channel_id=1, source_target_pairs={{0,2},{2,4},{4,6},{6,7},{7,5},{5,3},{3,1},{1,0},{8,10},{10,12},{12... | collective-permute-start | bytes 786440 | tf_op jit(solution)/shard_map/ppermute | solution.py:405
  67.8 1.2 %collective-permute-start.25 = (bf16[64,2048]{1,0:T(8,128)(2,1)S(1)}, bf16[64,2048]{1,0:T(8,128)(2,1)S(1)}, u32[]{:S(2)}, u32[]{:S(2)}) collective-permute-start(bf16[64,2048]{1,0:T(8,128)(2,1)S(1)} %get-tuple-element.50), channel_id=1, source_target_pairs={{0,2},{2,4},{4,6},{6,7},{7,5},{5,3},{3,1},{1,0},{8,10},{10,12},{12... | collective-permute-start | bytes 786440 | tf_op jit(solution)/shard_map/ppermute | solution.py:405
  68.9 3.8 %collective-permute-done.22 = bf16[64,2048]{1,0:T(8,128)(2,1)S(1)} collective-permute-done((bf16[64,2048]{1,0:T(8,128)(2,1)S(1)}, bf16[64,2048]{1,0:T(8,128)(2,1)S(1)}, u32[]{:S(2)}, u32[]{:S(2)}) %collective-permute-start.22) | collective-permute-done | bytes 262176 | tf_op jit(solution)/shard_map/ppermute | solution.py:405
  74.9 1.2 %collective-permute-start.19 = (bf16[64,2048]{1,0:T(8,128)(2,1)S(1)}, bf16[64,2048]{1,0:T(8,128)(2,1)S(1)}, u32[]{:S(2)}, u32[]{:S(2)}) collective-permute-start(bf16[64,2048]{1,0:T(8,128)(2,1)S(1)} %add_convert_fusion.9), channel_id=1, source_target_pairs={{0,2},{2,4},{4,6},{6,7},{7,5},{5,3},{3,1},{1,0},{8,10},{10,12},{12... | collective-permute-start | bytes 786440 | tf_op jit(solution)/shard_map/ppermute | solution.py:405
  76.1 2.2 %collective-permute-done.28 = bf16[64,2048]{1,0:T(8,128)(2,1)S(1)} collective-permute-done((bf16[64,2048]{1,0:T(8,128)(2,1)S(1)}, bf16[64,2048]{1,0:T(8,128)(2,1)S(1)}, u32[]{:S(2)}, u32[]{:S(2)}) %collective-permute-start.28) | collective-permute-done | bytes 262176 | tf_op jit(solution)/shard_map/ppermute | solution.py:405
  80.5 1.2 %collective-permute-start.26 = (bf16[64,2048]{1,0:T(8,128)(2,1)S(1)}, bf16[64,2048]{1,0:T(8,128)(2,1)S(1)}, u32[]{:S(2)}, u32[]{:S(2)}) collective-permute-start(bf16[64,2048]{1,0:T(8,128)(2,1)S(1)} %add_convert_fusion.4), channel_id=1, source_target_pairs={{0,2},{2,4},{4,6},{6,7},{7,5},{5,3},{3,1},{1,0},{8,10},{10,12},{12... | collective-permute-start | bytes 786440 | tf_op jit(solution)/shard_map/ppermute | solution.py:405
  81.7 2.2 %collective-permute-done.23 = bf16[64,2048]{1,0:T(8,128)(2,1)S(1)} collective-permute-done((bf16[64,2048]{1,0:T(8,128)(2,1)S(1)}, bf16[64,2048]{1,0:T(8,128)(2,1)S(1)}, u32[]{:S(2)}, u32[]{:S(2)}) %collective-permute-start.23) | collective-permute-done | bytes 262176 | tf_op jit(solution)/shard_map/ppermute | solution.py:405
  86.1 1.2 %collective-permute-start.20 = (bf16[64,2048]{1,0:T(8,128)(2,1)S(1)}, bf16[64,2048]{1,0:T(8,128)(2,1)S(1)}, u32[]{:S(2)}, u32[]{:S(2)}) collective-permute-start(bf16[64,2048]{1,0:T(8,128)(2,1)S(1)} %add_convert_fusion.8), channel_id=1, source_target_pairs={{0,2},{2,4},{4,6},{6,7},{7,5},{5,3},{3,1},{1,0},{8,10},{10,12},{12... | collective-permute-start | bytes 786440 | tf_op jit(solution)/shard_map/ppermute | solution.py:405
  87.3 2.2 %collective-permute-done.29 = bf16[64,2048]{1,0:T(8,128)(2,1)S(1)} collective-permute-done((bf16[64,2048]{1,0:T(8,128)(2,1)S(1)}, bf16[64,2048]{1,0:T(8,128)(2,1)S(1)}, u32[]{:S(2)}, u32[]{:S(2)}) %collective-permute-start.29) | collective-permute-done | bytes 262176 | tf_op jit(solution)/shard_map/ppermute | solution.py:405
  91.8 1.2 %collective-permute-start.27 = (bf16[64,2048]{1,0:T(8,128)(2,1)S(1)}, bf16[64,2048]{1,0:T(8,128)(2,1)S(1)}, u32[]{:S(2)}, u32[]{:S(2)}) collective-permute-start(bf16[64,2048]{1,0:T(8,128)(2,1)S(1)} %add_convert_fusion.3), channel_id=1, source_target_pairs={{0,2},{2,4},{4,6},{6,7},{7,5},{5,3},{3,1},{1,0},{8,10},{10,12},{12... | collective-permute-start | bytes 786440 | tf_op jit(solution)/shard_map/ppermute | solution.py:405
  93.4 1.4 %collective-permute-start.3 = (bf16[128,2048]{1,0:T(8,128)(2,1)S(1)}, bf16[128,2048]{1,0:T(8,128)(2,1)S(1)}, u32[]{:S(2)}, u32[]{:S(2)}) collective-permute-start(bf16[128,2048]{1,0:T(8,128)(2,1)S(1)} %slice.107), channel_id=1, source_target_pairs={{0,16},{8,24},{16,0},{24,8},{1,17},{9,25},{17,1},{25,9},{2,18},{10... | collective-permute-start | bytes 1572872 | tf_op jit(solution)/shard_map/ppermute | solution.py:385
  94.8 2.5 %collective-permute-done.20 = bf16[64,2048]{1,0:T(8,128)(2,1)S(1)} collective-permute-done((bf16[64,2048]{1,0:T(8,128)(2,1)S(1)}, bf16[64,2048]{1,0:T(8,128)(2,1)S(1)}, u32[]{:S(2)}, u32[]{:S(2)}) %collective-permute-start.20) | collective-permute-done | bytes 262176 | tf_op jit(solution)/shard_map/ppermute | solution.py:405
  97.4 1.2 %collective-permute-start.21 = (bf16[64,2048]{1,0:T(8,128)(2,1)S(1)}, bf16[64,2048]{1,0:T(8,128)(2,1)S(1)}, u32[]{:S(2)}, u32[]{:S(2)}) collective-permute-start(bf16[64,2048]{1,0:T(8,128)(2,1)S(1)} %add_convert_fusion.7), channel_id=1, source_target_pairs={{0,2},{2,4},{4,6},{6,7},{7,5},{5,3},{3,1},{1,0},{8,10},{10,12},{12... | collective-permute-start | bytes 786440 | tf_op jit(solution)/shard_map/ppermute | solution.py:405
  100.3 6.0 %collective-permute-done.3 = bf16[128,2048]{1,0:T(8,128)(2,1)S(1)} collective-permute-done((bf16[128,2048]{1,0:T(8,128)(2,1)S(1)}, bf16[128,2048]{1,0:T(8,128)(2,1)S(1)}, u32[]{:S(2)}, u32[]{:S(2)}) %collective-permute-start.3) | collective-permute-done | bytes 524320 | tf_op jit(solution)/shard_map/ppermute | solution.py:385
  106.5 1.7 %collective-permute-done.21 = bf16[64,2048]{1,0:T(8,128)(2,1)S(1)} collective-permute-done((bf16[64,2048]{1,0:T(8,128)(2,1)S(1)}, bf16[64,2048]{1,0:T(8,128)(2,1)S(1)}, u32[]{:S(2)}, u32[]{:S(2)}) %collective-permute-start.21) | collective-permute-done | bytes 262176 | tf_op jit(solution)/shard_map/ppermute | solution.py:405
  (72 shorter events, 21.4 us)
Async XLA Ops:
  0.0 19.2 %collective-permute-start = (bf16[128,2048]{1,0:T(8,128)(2,1)}, bf16[128,2048]{1,0:T(8,128)(2,1)S(1)}, u32[]{:S(2)}, u32[]{:S(2)}) collective-permute-start(bf16[128,2048]{1,0:T(8,128)(2,1)} %refs_4_.3), channel_id=1, source_target_pairs={{0,16},{8,24},{16,0},{24,8},{1,17},{9,25},{17,1},{25,9},{2,18},{10... | collective-permute-start | bytes 1572872 | tf_op jit(solution)/shard_map/ppermute | solution.py:370
  4.0 9.3 %collective-permute-start.4 = (bf16[64,2048]{1,0:T(8,128)(2,1)S(1)}, bf16[64,2048]{1,0:T(8,128)(2,1)S(1)}, u32[]{:S(2)}, u32[]{:S(2)}) collective-permute-start(bf16[64,2048]{1,0:T(8,128)(2,1)S(1)} %get-tuple-element.60), channel_id=1, source_target_pairs={{0,2},{2,4},{4,6},{6,7},{7,5},{5,3},{3,1},{1,0},{8,10},{10,12},{12... | collective-permute-start | bytes 786440 | tf_op jit(solution)/shard_map/ppermute | solution.py:362
  5.7 16.1 %collective-permute-start.6 = (bf16[64,2048]{1,0:T(8,128)(2,1)S(1)}, bf16[64,2048]{1,0:T(8,128)(2,1)S(1)}, u32[]{:S(2)}, u32[]{:S(2)}) collective-permute-start(bf16[64,2048]{1,0:T(8,128)(2,1)S(1)} %get-tuple-element.60), channel_id=1, source_target_pairs={{2,0},{4,2},{6,4},{7,6},{5,7},{3,5},{1,3},{0,1},{10,8},{12,10},{14... | collective-permute-start | bytes 786440 | tf_op jit(solution)/shard_map/ppermute | solution.py:365
  6.1 14.0 %collective-permute-start.5 = (bf16[64,2048]{1,0:T(8,128)(2,1)S(1)}, bf16[64,2048]{1,0:T(8,128)(2,1)S(1)}, u32[]{:S(2)}, u32[]{:S(2)}) collective-permute-start(bf16[64,2048]{1,0:T(8,128)(2,1)S(1)} %get-tuple-element.59), channel_id=1, source_target_pairs={{0,2},{2,4},{4,6},{6,7},{7,5},{5,3},{3,1},{1,0},{8,10},{10,12},{12... | collective-permute-start | bytes 786440 | tf_op jit(solution)/shard_map/ppermute | solution.py:362
  7.7 11.1 %collective-permute-start.7 = (bf16[64,2048]{1,0:T(8,128)(2,1)S(1)}, bf16[64,2048]{1,0:T(8,128)(2,1)S(1)}, u32[]{:S(2)}, u32[]{:S(2)}) collective-permute-start(bf16[64,2048]{1,0:T(8,128)(2,1)S(1)} %get-tuple-element.59), channel_id=1, source_target_pairs={{2,0},{4,2},{6,4},{7,6},{5,7},{3,5},{1,3},{0,1},{10,8},{12,10},{14... | collective-permute-start | bytes 786440 | tf_op jit(solution)/shard_map/ppermute | solution.py:365
  13.3 9.8 %collective-permute-start.8 = (bf16[64,2048]{1,0:T(8,128)(2,1)S(1)}, bf16[64,2048]{1,0:T(8,128)(2,1)S(1)}, u32[]{:S(2)}, u32[]{:S(2)}) collective-permute-start(bf16[64,2048]{1,0:T(8,128)(2,1)S(1)} %collective-permute-done.4.refs_0_), channel_id=1, source_target_pairs={{0,2},{2,4},{4,6},{6,7},{7,5},{5,3},{3,1},{1,0},{8,10},{10,12},{12... | collective-permute-start | bytes 786440 | tf_op jit(solution)/shard_map/ppermute | solution.py:362
  20.1 23.8 %collective-permute-start.1 = (bf16[256,2048]{1,0:T(8,128)(2,1)}, bf16[256,2048]{1,0:T(8,128)(2,1)}, u32[]{:S(2)}, u32[]{:S(2)}) collective-permute-start(bf16[256,2048]{1,0:T(8,128)(2,1)} %constant_dynamic-update-slice_fusion.refs_0_), channel_id=1, source_target_pairs={{0,8},{8,0},{16,24},{24,16},{1,9},{9,1},{17,25},{25,17},{2,10},{10... | collective-permute-start | bytes 3145736 | tf_op jit(solution)/shard_map/ppermute | solution.py:374
  20.1 13.0 %collective-permute-start.9 = (bf16[64,2048]{1,0:T(8,128)(2,1)S(1)}, bf16[64,2048]{1,0:T(8,128)(2,1)S(1)}, u32[]{:S(2)}, u32[]{:S(2)}) collective-permute-start(bf16[64,2048]{1,0:T(8,128)(2,1)S(1)} %collective-permute-done.5.refs_1_), channel_id=1, source_target_pairs={{0,2},{2,4},{4,6},{6,7},{7,5},{5,3},{3,1},{1,0},{8,10},{10,12},{12... | collective-permute-start | bytes 786440 | tf_op jit(solution)/shard_map/ppermute | solution.py:362
  21.7 13.4 %collective-permute-start.10 = (bf16[64,2048]{1,0:T(8,128)(2,1)S(1)}, bf16[64,2048]{1,0:T(8,128)(2,1)S(1)}, u32[]{:S(2)}, u32[]{:S(2)}) collective-permute-start(bf16[64,2048]{1,0:T(8,128)(2,1)S(1)} %collective-permute-done.6.refs_2_), channel_id=1, source_target_pairs={{2,0},{4,2},{6,4},{7,6},{5,7},{3,5},{1,3},{0,1},{10,8},{12,10},{14... | collective-permute-start | bytes 786440 | tf_op jit(solution)/shard_map/ppermute | solution.py:365
  23.1 18.7 %collective-permute-start.12 = (bf16[64,2048]{1,0:T(8,128)(2,1)S(1)}, bf16[64,2048]{1,0:T(8,128)(2,1)S(1)}, u32[]{:S(2)}, u32[]{:S(2)}) collective-permute-start(bf16[64,2048]{1,0:T(8,128)(2,1)S(1)} %collective-permute-done.8.refs_4_), channel_id=1, source_target_pairs={{0,2},{2,4},{4,6},{6,7},{7,5},{5,3},{3,1},{1,0},{8,10},{10,12},{12... | collective-permute-start | bytes 786440 | tf_op jit(solution)/shard_map/ppermute | solution.py:362
  26.0 15.8 %collective-permute-start.15 = (bf16[64,2048]{1,0:T(8,128)(2,1)S(1)}, bf16[64,2048]{1,0:T(8,128)(2,1)S(1)}, u32[]{:S(2)}, u32[]{:S(2)}) collective-permute-start(bf16[64,2048]{1,0:T(8,128)(2,1)S(1)} %collective-permute-done.11.refs_7_), channel_id=1, source_target_pairs={{2,0},{4,2},{6,4},{7,6},{5,7},{3,5},{1,3},{0,1},{10,8},{12,10},{14... | collective-permute-start | bytes 786440 | tf_op jit(solution)/shard_map/ppermute | solution.py:365
  27.3 12.8 %all-to-all-start = ((f32[8,8,128]{2,1,0:T(8,128)}), f32[8,8,128]{2,1,0:T(8,128)S(1)}, u32[]{:S(2)}, u32[]{:S(2)}) async-start(f32[8,8,128]{2,1,0:T(8,128)} %bitcast.22), calls=%async_computation | async-start | bytes 65536 | tf_op jit(solution)/shard_map/all_to_all | solution.py:345
  33.2 17.9 %collective-permute-start.13 = (bf16[64,2048]{1,0:T(8,128)(2,1)S(1)}, bf16[64,2048]{1,0:T(8,128)(2,1)S(1)}, u32[]{:S(2)}, u32[]{:S(2)}) collective-permute-start(bf16[64,2048]{1,0:T(8,128)(2,1)S(1)} %collective-permute-done.9.refs_5_), channel_id=1, source_target_pairs={{0,2},{2,4},{4,6},{6,7},{7,5},{5,3},{3,1},{1,0},{8,10},{10,12},{12... | collective-permute-start | bytes 786440 | tf_op jit(solution)/shard_map/ppermute | solution.py:362
  35.2 15.9 %collective-permute-start.14 = (bf16[64,2048]{1,0:T(8,128)(2,1)S(1)}, bf16[64,2048]{1,0:T(8,128)(2,1)S(1)}, u32[]{:S(2)}, u32[]{:S(2)}) collective-permute-start(bf16[64,2048]{1,0:T(8,128)(2,1)S(1)} %collective-permute-done.10.refs_6_), channel_id=1, source_target_pairs={{2,0},{4,2},{6,4},{7,6},{5,7},{3,5},{1,3},{0,1},{10,8},{12,10},{14... | collective-permute-start | bytes 786440 | tf_op jit(solution)/shard_map/ppermute | solution.py:365
  41.8 9.3 %collective-permute-start.16 = (bf16[64,2048]{1,0:T(8,128)(2,1)S(1)}, bf16[64,2048]{1,0:T(8,128)(2,1)S(1)}, u32[]{:S(2)}, u32[]{:S(2)}) collective-permute-start(bf16[64,2048]{1,0:T(8,128)(2,1)S(1)} %collective-permute-done.12.refs_0_), channel_id=1, source_target_pairs={{0,2},{2,4},{4,6},{6,7},{7,5},{5,3},{3,1},{1,0},{8,10},{10,12},{12... | collective-permute-start | bytes 786440 | tf_op jit(solution)/shard_map/ppermute | solution.py:362
  42.2 8.9 %collective-permute-start.17 = (bf16[64,2048]{1,0:T(8,128)(2,1)S(1)}, bf16[64,2048]{1,0:T(8,128)(2,1)S(1)}, u32[]{:S(2)}, u32[]{:S(2)}) collective-permute-start(bf16[64,2048]{1,0:T(8,128)(2,1)S(1)} %collective-permute-done.15.refs_3_), channel_id=1, source_target_pairs={{2,0},{4,2},{6,4},{7,6},{5,7},{3,5},{1,3},{0,1},{10,8},{12,10},{14... | collective-permute-start | bytes 786440 | tf_op jit(solution)/shard_map/ppermute | solution.py:365
  64.8 7.9 %collective-permute-start.22 = (bf16[64,2048]{1,0:T(8,128)(2,1)S(1)}, bf16[64,2048]{1,0:T(8,128)(2,1)S(1)}, u32[]{:S(2)}, u32[]{:S(2)}) collective-permute-start(bf16[64,2048]{1,0:T(8,128)(2,1)S(1)} %get-tuple-element.46), channel_id=1, source_target_pairs={{2,0},{4,2},{6,4},{7,6},{5,7},{3,5},{1,3},{0,1},{10,8},{12,10},{14... | collective-permute-start | bytes 786440 | tf_op jit(solution)/shard_map/ppermute | solution.py:405
  65.7 27.2 %collective-permute-start.2 = (bf16[256,2048]{1,0:T(8,128)(2,1)S(1)}, bf16[256,2048]{1,0:T(8,128)(2,1)S(1)}, u32[]{:S(2)}, u32[]{:S(2)}) collective-permute-start(bf16[256,2048]{1,0:T(8,128)(2,1)S(1)} %copy-done.3), channel_id=1, source_target_pairs={{0,8},{8,0},{16,24},{24,16},{1,9},{9,1},{17,25},{25,17},{2,10},{10... | collective-permute-start | bytes 3145736 | tf_op jit(solution)/shard_map/ppermute | solution.py:376
  65.7 9.1 %collective-permute-start.18 = (bf16[64,2048]{1,0:T(8,128)(2,1)S(1)}, bf16[64,2048]{1,0:T(8,128)(2,1)S(1)}, u32[]{:S(2)}, u32[]{:S(2)}) collective-permute-start(bf16[64,2048]{1,0:T(8,128)(2,1)S(1)} %get-tuple-element.42), channel_id=1, source_target_pairs={{0,2},{2,4},{4,6},{6,7},{7,5},{5,3},{3,1},{1,0},{8,10},{10,12},{12... | collective-permute-start | bytes 786440 | tf_op jit(solution)/shard_map/ppermute | solution.py:405
  66.9 11.4 %collective-permute-start.28 = (bf16[64,2048]{1,0:T(8,128)(2,1)S(1)}, bf16[64,2048]{1,0:T(8,128)(2,1)S(1)}, u32[]{:S(2)}, u32[]{:S(2)}) collective-permute-start(bf16[64,2048]{1,0:T(8,128)(2,1)S(1)} %get-tuple-element.53), channel_id=1, source_target_pairs={{2,0},{4,2},{6,4},{7,6},{5,7},{3,5},{1,3},{0,1},{10,8},{12,10},{14... | collective-permute-start | bytes 786440 | tf_op jit(solution)/shard_map/ppermute | solution.py:405
  67.8 12.7 %collective-permute-start.25 = (bf16[64,2048]{1,0:T(8,128)(2,1)S(1)}, bf16[64,2048]{1,0:T(8,128)(2,1)S(1)}, u32[]{:S(2)}, u32[]{:S(2)}) collective-permute-start(bf16[64,2048]{1,0:T(8,128)(2,1)S(1)} %get-tuple-element.50), channel_id=1, source_target_pairs={{0,2},{2,4},{4,6},{6,7},{7,5},{5,3},{3,1},{1,0},{8,10},{10,12},{12... | collective-permute-start | bytes 786440 | tf_op jit(solution)/shard_map/ppermute | solution.py:405
  72.8 11.2 %collective-permute-start.23 = (bf16[64,2048]{1,0:T(8,128)(2,1)S(1)}, bf16[64,2048]{1,0:T(8,128)(2,1)S(1)}, u32[]{:S(2)}, u32[]{:S(2)}) collective-permute-start(bf16[64,2048]{1,0:T(8,128)(2,1)S(1)} %add_convert_fusion.6), channel_id=1, source_target_pairs={{2,0},{4,2},{6,4},{7,6},{5,7},{3,5},{1,3},{0,1},{10,8},{12,10},{14... | collective-permute-start | bytes 786440 | tf_op jit(solution)/shard_map/ppermute | solution.py:405
  74.9 11.2 %collective-permute-start.19 = (bf16[64,2048]{1,0:T(8,128)(2,1)S(1)}, bf16[64,2048]{1,0:T(8,128)(2,1)S(1)}, u32[]{:S(2)}, u32[]{:S(2)}) collective-permute-start(bf16[64,2048]{1,0:T(8,128)(2,1)S(1)} %add_convert_fusion.9), channel_id=1, source_target_pairs={{0,2},{2,4},{4,6},{6,7},{7,5},{5,3},{3,1},{1,0},{8,10},{10,12},{12... | collective-permute-start | bytes 786440 | tf_op jit(solution)/shard_map/ppermute | solution.py:405
  78.4 11.2 %collective-permute-start.29 = (bf16[64,2048]{1,0:T(8,128)(2,1)S(1)}, bf16[64,2048]{1,0:T(8,128)(2,1)S(1)}, u32[]{:S(2)}, u32[]{:S(2)}) collective-permute-start(bf16[64,2048]{1,0:T(8,128)(2,1)S(1)} %add_convert_fusion.2), channel_id=1, source_target_pairs={{2,0},{4,2},{6,4},{7,6},{5,7},{3,5},{1,3},{0,1},{10,8},{12,10},{14... | collective-permute-start | bytes 786440 | tf_op jit(solution)/shard_map/ppermute | solution.py:405
  80.5 11.2 %collective-permute-start.26 = (bf16[64,2048]{1,0:T(8,128)(2,1)S(1)}, bf16[64,2048]{1,0:T(8,128)(2,1)S(1)}, u32[]{:S(2)}, u32[]{:S(2)}) collective-permute-start(bf16[64,2048]{1,0:T(8,128)(2,1)S(1)} %add_convert_fusion.4), channel_id=1, source_target_pairs={{0,2},{2,4},{4,6},{6,7},{7,5},{5,3},{3,1},{1,0},{8,10},{10,12},{12... | collective-permute-start | bytes 786440 | tf_op jit(solution)/shard_map/ppermute | solution.py:405
  84.0 22.5 %collective-permute-start.24 = (bf16[64,2048]{1,0:T(8,128)(2,1)S(1)}, bf16[64,2048]{1,0:T(8,128)(2,1)S(1)}, u32[]{:S(2)}, u32[]{:S(2)}) collective-permute-start(bf16[64,2048]{1,0:T(8,128)(2,1)S(1)} %add_convert_fusion.5), channel_id=1, source_target_pairs={{2,0},{4,2},{6,4},{7,6},{5,7},{3,5},{1,3},{0,1},{10,8},{12,10},{14... | collective-permute-start | bytes 786440 | tf_op jit(solution)/shard_map/ppermute | solution.py:405
  86.1 11.2 %collective-permute-start.20 = (bf16[64,2048]{1,0:T(8,128)(2,1)S(1)}, bf16[64,2048]{1,0:T(8,128)(2,1)S(1)}, u32[]{:S(2)}, u32[]{:S(2)}) collective-permute-start(bf16[64,2048]{1,0:T(8,128)(2,1)S(1)} %add_convert_fusion.8), channel_id=1, source_target_pairs={{0,2},{2,4},{4,6},{6,7},{7,5},{5,3},{3,1},{1,0},{8,10},{10,12},{12... | collective-permute-start | bytes 786440 | tf_op jit(solution)/shard_map/ppermute | solution.py:405
  89.6 9.7 %collective-permute-start.30 = (bf16[64,2048]{1,0:T(8,128)(2,1)S(1)}, bf16[64,2048]{1,0:T(8,128)(2,1)S(1)}, u32[]{:S(2)}, u32[]{:S(2)}) collective-permute-start(bf16[64,2048]{1,0:T(8,128)(2,1)S(1)} %add_convert_fusion.1), channel_id=1, source_target_pairs={{2,0},{4,2},{6,4},{7,6},{5,7},{3,5},{1,3},{0,1},{10,8},{12,10},{14... | collective-permute-start | bytes 786440 | tf_op jit(solution)/shard_map/ppermute | solution.py:405
  91.8 14.7 %collective-permute-start.27 = (bf16[64,2048]{1,0:T(8,128)(2,1)S(1)}, bf16[64,2048]{1,0:T(8,128)(2,1)S(1)}, u32[]{:S(2)}, u32[]{:S(2)}) collective-permute-start(bf16[64,2048]{1,0:T(8,128)(2,1)S(1)} %add_convert_fusion.3), channel_id=1, source_target_pairs={{0,2},{2,4},{4,6},{6,7},{7,5},{5,3},{3,1},{1,0},{8,10},{10,12},{12... | collective-permute-start | bytes 786440 | tf_op jit(solution)/shard_map/ppermute | solution.py:405
  93.4 13.0 %collective-permute-start.3 = (bf16[128,2048]{1,0:T(8,128)(2,1)S(1)}, bf16[128,2048]{1,0:T(8,128)(2,1)S(1)}, u32[]{:S(2)}, u32[]{:S(2)}) collective-permute-start(bf16[128,2048]{1,0:T(8,128)(2,1)S(1)} %slice.107), channel_id=1, source_target_pairs={{0,16},{8,24},{16,0},{24,8},{1,17},{9,25},{17,1},{25,9},{2,18},{10... | collective-permute-start | bytes 1572872 | tf_op jit(solution)/shard_map/ppermute | solution.py:385
  97.4 10.8 %collective-permute-start.21 = (bf16[64,2048]{1,0:T(8,128)(2,1)S(1)}, bf16[64,2048]{1,0:T(8,128)(2,1)S(1)}, u32[]{:S(2)}, u32[]{:S(2)}) collective-permute-start(bf16[64,2048]{1,0:T(8,128)(2,1)S(1)} %add_convert_fusion.7), channel_id=1, source_target_pairs={{0,2},{2,4},{4,6},{6,7},{7,5},{5,3},{3,1},{1,0},{8,10},{10,12},{12... | collective-permute-start | bytes 786440 | tf_op jit(solution)/shard_map/ppermute | solution.py:405
  99.4 8.8 %collective-permute-start.31 = (bf16[64,2048]{1,0:T(8,128)(2,1)S(1)}, bf16[64,2048]{1,0:T(8,128)(2,1)S(1)}, u32[]{:S(2)}, u32[]{:S(2)}) collective-permute-start(bf16[64,2048]{1,0:T(8,128)(2,1)S(1)} %add_convert_fusion), channel_id=1, source_target_pairs={{2,0},{4,2},{6,4},{7,6},{5,7},{3,5},{1,3},{0,1},{10,8},{12,10},{14... | collective-permute-start | bytes 786440 | tf_op jit(solution)/shard_map/ppermute | solution.py:405
  (6 other events, 83.8 us)

commit v7 on v6

--- a/solution.py
+++ b/solution.py
@@ -267,10 +267,10 @@
         copy.start()
     for copy in loads[:-2]:
         copy.wait()
+    gate = dot(x[...], wg[...])
+    loads[-2].wait()
     for copy in fetches:
         copy.start()
-    gate = dot(x[...], wg[...])
-    loads[-2].wait()
     upper = dot(x[...], wu[...])
     hidden = (gate / (1.0 + jnp.exp(-gate)) * upper).astype(BF16)
     loads[-1].wait()

time: 110 us -> 110 us (level)
  starting transfers between devices: 39.3 us -> 37.3 us
  Pallas kernels: 22.6 us -> 24.1 us
  waiting for transfers between devices: 38.6 us -> 39.8 us
    ppermute x1, starting transfers between devices: 1.39 us -> 0.07 us  [on_device(): came = lax.ppermute(part.pop(r).astype(BF16), 'dp', swap)]
  transfers between devices with their start and end apart: 33 -> 33, of which waited for: 17 -> 17; matrix products, arithmetic and copies ran while one was open for 6% -> 6% of each run, Pallas kernels for 8% -> 9%
where the time goes in v7:
time: 110 us
  waiting for transfers between devices  39.8 us (36%)
  starting transfers between devices  37.3 us (34%)
  Pallas kernels  24.1 us (22%)
  local copies, waits for them, and re-layouts  5.42 us (5%)
  other arithmetic  2.37 us (2%)
    ppermute x14, waiting for transfers between devices, on_device(): came = lax.ppermute(acc, 'expert', perm)  20.2 us
    pallas_call x1, Pallas kernels, run_experts(): pl.pallas_call(functools.partial(experts_kernel, offsets, early, sizes, l...  14.5 us
    ppermute x14, starting transfers between devices, on_device(): came = lax.ppermute(acc, 'expert', perm)  14 us
    ppermute x7, starting transfers between devices, on_device(): up[h] = lax.ppermute(up[h], 'expert', forward)  10.4 us
    pallas_call x1, Pallas kernels, run_shared(): pl.pallas_call(functools.partial(shared_kernel, count), out_shape=[pltpu....  7.92 us
    ppermute x1, waiting for transfers between devices, on_device(): came = lax.ppermute(part.pop(r).astype(BF16), 'dp', swap)  6.85 us
    all_to_all x1, starting transfers between devices, on_device(): lax.all_to_all(info, 'expert', split_axis=0, concat_axis=0, tiled=True)  5.81 us
    ppermute x7, waiting for transfers between devices, on_device(): down[h] = lax.ppermute(down[h], 'expert', backward)  5.25 us
  transfers between devices with their start and end apart: 33, of which 17 were waited for; matrix products, arithmetic and copies ran while one was open for 6% of the time, Pallas kernels for 9%

profile of v7, /device:TPU:0, one launch (start us, length us, event | category | flops | bytes accessed | tf_op | source)
XLA Modules:
  0.0 110.1 jit_solution(6838971875697292657)
XLA Ops:
  0.0 3.0 %collective-permute-start = (bf16[128,2048]{1,0:T(8,128)(2,1)}, bf16[128,2048]{1,0:T(8,128)(2,1)S(1)}, u32[]{:S(2)}, u32[]{:S(2)}) collective-permute-start(bf16[128,2048]{1,0:T(8,128)(2,1)} %refs_4_.3), channel_id=1, source_target_pairs={{0,16},{8,24},{16,0},{24,8},{1,17},{9,25},{17,1},{25,9},{2,18},{10... | collective-permute-start | bytes 1572872 | tf_op jit(solution)/shard_map/ppermute | solution.py:370
  4.0 1.6 %collective-permute-start.4 = (bf16[64,2048]{1,0:T(8,128)(2,1)S(1)}, bf16[64,2048]{1,0:T(8,128)(2,1)S(1)}, u32[]{:S(2)}, u32[]{:S(2)}) collective-permute-start(bf16[64,2048]{1,0:T(8,128)(2,1)S(1)} %get-tuple-element.60), channel_id=1, source_target_pairs={{0,2},{2,4},{4,6},{6,7},{7,5},{5,3},{3,1},{1,0},{8,10},{10,12},{12... | collective-permute-start | bytes 786440 | tf_op jit(solution)/shard_map/ppermute | solution.py:362
  6.1 1.6 %collective-permute-start.5 = (bf16[64,2048]{1,0:T(8,128)(2,1)S(1)}, bf16[64,2048]{1,0:T(8,128)(2,1)S(1)}, u32[]{:S(2)}, u32[]{:S(2)}) collective-permute-start(bf16[64,2048]{1,0:T(8,128)(2,1)S(1)} %get-tuple-element.59), channel_id=1, source_target_pairs={{0,2},{2,4},{4,6},{6,7},{7,5},{5,3},{3,1},{1,0},{8,10},{10,12},{12... | collective-permute-start | bytes 786440 | tf_op jit(solution)/shard_map/ppermute | solution.py:362
  9.7 1.9 %constant_dynamic-update-slice_fusion.1 = bf16[256,2048]{1,0:T(8,128)(2,1)} fusion(bf16[128,2048]{1,0:T(8,128)(2,1)} %refs_4_.3), kind=kLoop, calls=%fused_computation.40 | loop fusion | bytes 1048576
  11.6 1.7 %collective-permute-done.4.refs_0_ = bf16[64,2048]{1,0:T(8,128)(2,1)S(1)} collective-permute-done((bf16[64,2048]{1,0:T(8,128)(2,1)S(1)}, bf16[64,2048]{1,0:T(8,128)(2,1)S(1)}, u32[]{:S(2)}, u32[]{:S(2)}) %collective-permute-start.4) | collective-permute-done | bytes 262176 | tf_op jit(solution)/shard_map/ppermute | solution.py:362
  13.3 1.6 %collective-permute-start.8 = (bf16[64,2048]{1,0:T(8,128)(2,1)S(1)}, bf16[64,2048]{1,0:T(8,128)(2,1)S(1)}, u32[]{:S(2)}, u32[]{:S(2)}) collective-permute-start(bf16[64,2048]{1,0:T(8,128)(2,1)S(1)} %collective-permute-done.4.refs_0_), channel_id=1, source_target_pairs={{0,2},{2,4},{4,6},{6,7},{7,5},{5,3},{3,1},{1,0},{8,10},{10,12},{12... | collective-permute-start | bytes 786440 | tf_op jit(solution)/shard_map/ppermute | solution.py:362
  14.9 3.9 %collective-permute-done.7.refs_3_ = bf16[64,2048]{1,0:T(8,128)(2,1)S(1)} collective-permute-done((bf16[64,2048]{1,0:T(8,128)(2,1)S(1)}, bf16[64,2048]{1,0:T(8,128)(2,1)S(1)}, u32[]{:S(2)}, u32[]{:S(2)}) %collective-permute-start.7) | collective-permute-done | bytes 262176 | tf_op jit(solution)/shard_map/ppermute | solution.py:365
  20.1 1.6 %collective-permute-start.9 = (bf16[64,2048]{1,0:T(8,128)(2,1)S(1)}, bf16[64,2048]{1,0:T(8,128)(2,1)S(1)}, u32[]{:S(2)}, u32[]{:S(2)}) collective-permute-start(bf16[64,2048]{1,0:T(8,128)(2,1)S(1)} %collective-permute-done.5.refs_1_), channel_id=1, source_target_pairs={{0,2},{2,4},{4,6},{6,7},{7,5},{5,3},{3,1},{1,0},{8,10},{10,12},{12... | collective-permute-start | bytes 786440 | tf_op jit(solution)/shard_map/ppermute | solution.py:362
  23.1 1.6 %collective-permute-start.12 = (bf16[64,2048]{1,0:T(8,128)(2,1)S(1)}, bf16[64,2048]{1,0:T(8,128)(2,1)S(1)}, u32[]{:S(2)}, u32[]{:S(2)}) collective-permute-start(bf16[64,2048]{1,0:T(8,128)(2,1)S(1)} %collective-permute-done.8.refs_4_), channel_id=1, source_target_pairs={{0,2},{2,4},{4,6},{6,7},{7,5},{5,3},{3,1},{1,0},{8,10},{10,12},{12... | collective-permute-start | bytes 786440 | tf_op jit(solution)/shard_map/ppermute | solution.py:362
  24.7 1.4 %collective-permute-done.11.refs_7_ = bf16[64,2048]{1,0:T(8,128)(2,1)S(1)} collective-permute-done((bf16[64,2048]{1,0:T(8,128)(2,1)S(1)}, bf16[64,2048]{1,0:T(8,128)(2,1)S(1)}, u32[]{:S(2)}, u32[]{:S(2)}) %collective-permute-start.11) | collective-permute-done | bytes 262176 | tf_op jit(solution)/shard_map/ppermute | solution.py:365
  27.3 5.8 %all-to-all-start = ((f32[8,8,128]{2,1,0:T(8,128)}), f32[8,8,128]{2,1,0:T(8,128)S(1)}, u32[]{:S(2)}, u32[]{:S(2)}) async-start(f32[8,8,128]{2,1,0:T(8,128)} %bitcast.22), calls=%async_computation | async-start | bytes 65536 | tf_op jit(solution)/shard_map/all_to_all | solution.py:345
  33.2 2.0 %collective-permute-start.13 = (bf16[64,2048]{1,0:T(8,128)(2,1)S(1)}, bf16[64,2048]{1,0:T(8,128)(2,1)S(1)}, u32[]{:S(2)}, u32[]{:S(2)}) collective-permute-start(bf16[64,2048]{1,0:T(8,128)(2,1)S(1)} %collective-permute-done.9.refs_5_), channel_id=1, source_target_pairs={{0,2},{2,4},{4,6},{6,7},{7,5},{5,3},{3,1},{1,0},{8,10},{10,12},{12... | collective-permute-start | bytes 786440 | tf_op jit(solution)/shard_map/ppermute | solution.py:362
  35.3 4.8 %all-to-all-done.meta = f32[8,8,128]{2,1,0:T(8,128)S(1)} async-done(((f32[8,8,128]{2,1,0:T(8,128)}), f32[8,8,128]{2,1,0:T(8,128)S(1)}, u32[]{:S(2)}, u32[]{:S(2)}) %all-to-all-start) | async-done | bytes 32800 | tf_op jit(solution)/shard_map/all_to_all | solution.py:345
  40.1 1.7 %pick.1 = (bf16[4,224,256]{2,1,0:T(8,128)(2,1)S(1)}, f32[4,320,128]{2,1,0:T(8,128)S(1)}, bf16[4,160,2048]{2,1,0:T(8,128)(2,1)S(1)}) custom-call(s32[2]{0:T(128)S(1)} %pad_add_fusion.where, f32[8,8,128]{2,1,0:T(8,128)S(1)} %all-to-all-done.meta, bf16[64,2048]{1,0:T(8,128)(2,1)S(1)} %collective-permute-done.4.refs_0_, ...), custom_call_target="tpu_custom_call" | custom-call | flops 1000 | bytes 1000 | tf_op jit(solution)/shard_map/pick/pallas_call | solution.py:121
  42.2 1.7 %collective-permute-start.17 = (bf16[64,2048]{1,0:T(8,128)(2,1)S(1)}, bf16[64,2048]{1,0:T(8,128)(2,1)S(1)}, u32[]{:S(2)}, u32[]{:S(2)}) collective-permute-start(bf16[64,2048]{1,0:T(8,128)(2,1)S(1)} %collective-permute-done.15.refs_3_), channel_id=1, source_target_pairs={{2,0},{4,2},{6,4},{7,6},{5,7},{3,5},{1,3},{0,1},{10,8},{12,10},{14... | collective-permute-start | bytes 786440 | tf_op jit(solution)/shard_map/ppermute | solution.py:365
  43.9 7.9 %shared_experts.1 = (bf16[256,2048]{1,0:T(8,128)(2,1)}, bf16[256,2048]{1,0:T(8,128)(2,1)}, bf16[704,2048]{1,0:T(8,128)(2,1)S(1)}, bf16[704,2048]{1,0:T(8,128)(2,1)S(1)}, bf16[704,2048]{1,0:T(8,128)(2,1)S(1)}) custom-call(bf16[256,2048]{1,0:T(8,128)(2,1)} %constant_dynamic-update-slice_fusion.refs_0_, bf16[256,2048]{1,0:T(8,128)(2,1)} %collective-permute-done.1.refs_1_, ...), custom_call_target="tpu_custom_call" | custom-call | flops 1000 | bytes 1000 | tf_op jit(solution)/shard_map/shared_experts/pallas_call | solution.py:293
  51.9 14.5 %routed_experts.1 = (bf16[64,2048]{1,0:T(8,128)(2,1)S(1)}, bf16[64,2048]{1,0:T(8,128)(2,1)S(1)}, bf16[64,2048]{1,0:T(8,128)(2,1)S(1)}, bf16[64,2048]{1,0:T(8,128...) custom-call(s32[2]{0:T(128)S(1)} %pad_add_fusion.where, ...), custom_call_target="tpu_custom_call" | custom-call | flops 8522825728 | bytes 34603008 | tf_op jit(solution)/shard_map/routed_experts/pallas_call | solution.py:227
  66.5 1.9 %collective-permute-start.18 = (bf16[64,2048]{1,0:T(8,128)(2,1)S(1)}, bf16[64,2048]{1,0:T(8,128)(2,1)S(1)}, u32[]{:S(2)}, u32[]{:S(2)}) collective-permute-start(bf16[64,2048]{1,0:T(8,128)(2,1)S(1)} %get-tuple-element.42), channel_id=1, source_target_pairs={{0,2},{2,4},{4,6},{6,7},{7,5},{5,3},{3,1},{1,0},{8,10},{10,12},{12... | collective-permute-start | bytes 786440 | tf_op jit(solution)/shard_map/ppermute | solution.py:405
  68.6 1.9 %collective-permute-start.25 = (bf16[64,2048]{1,0:T(8,128)(2,1)S(1)}, bf16[64,2048]{1,0:T(8,128)(2,1)S(1)}, u32[]{:S(2)}, u32[]{:S(2)}) collective-permute-start(bf16[64,2048]{1,0:T(8,128)(2,1)S(1)} %get-tuple-element.50), channel_id=1, source_target_pairs={{0,2},{2,4},{4,6},{6,7},{7,5},{5,3},{3,1},{1,0},{8,10},{10,12},{12... | collective-permute-start | bytes 786440 | tf_op jit(solution)/shard_map/ppermute | solution.py:405
  70.5 3.8 %collective-permute-done.22 = bf16[64,2048]{1,0:T(8,128)(2,1)S(1)} collective-permute-done((bf16[64,2048]{1,0:T(8,128)(2,1)S(1)}, bf16[64,2048]{1,0:T(8,128)(2,1)S(1)}, u32[]{:S(2)}, u32[]{:S(2)}) %collective-permute-start.22) | collective-permute-done | bytes 262176 | tf_op jit(solution)/shard_map/ppermute | solution.py:405
  75.7 1.9 %collective-permute-start.19 = (bf16[64,2048]{1,0:T(8,128)(2,1)S(1)}, bf16[64,2048]{1,0:T(8,128)(2,1)S(1)}, u32[]{:S(2)}, u32[]{:S(2)}) collective-permute-start(bf16[64,2048]{1,0:T(8,128)(2,1)S(1)} %add_convert_fusion.9), channel_id=1, source_target_pairs={{0,2},{2,4},{4,6},{6,7},{7,5},{5,3},{3,1},{1,0},{8,10},{10,12},{12... | collective-permute-start | bytes 786440 | tf_op jit(solution)/shard_map/ppermute | solution.py:405
  77.7 2.2 %collective-permute-done.28 = bf16[64,2048]{1,0:T(8,128)(2,1)S(1)} collective-permute-done((bf16[64,2048]{1,0:T(8,128)(2,1)S(1)}, bf16[64,2048]{1,0:T(8,128)(2,1)S(1)}, u32[]{:S(2)}, u32[]{:S(2)}) %collective-permute-start.28) | collective-permute-done | bytes 262176 | tf_op jit(solution)/shard_map/ppermute | solution.py:405
  81.4 1.9 %collective-permute-start.26 = (bf16[64,2048]{1,0:T(8,128)(2,1)S(1)}, bf16[64,2048]{1,0:T(8,128)(2,1)S(1)}, u32[]{:S(2)}, u32[]{:S(2)}) collective-permute-start(bf16[64,2048]{1,0:T(8,128)(2,1)S(1)} %add_convert_fusion.4), channel_id=1, source_target_pairs={{0,2},{2,4},{4,6},{6,7},{7,5},{5,3},{3,1},{1,0},{8,10},{10,12},{12... | collective-permute-start | bytes 786440 | tf_op jit(solution)/shard_map/ppermute | solution.py:405
  83.3 2.2 %collective-permute-done.23 = bf16[64,2048]{1,0:T(8,128)(2,1)S(1)} collective-permute-done((bf16[64,2048]{1,0:T(8,128)(2,1)S(1)}, bf16[64,2048]{1,0:T(8,128)(2,1)S(1)}, u32[]{:S(2)}, u32[]{:S(2)}) %collective-permute-start.23) | collective-permute-done | bytes 262176 | tf_op jit(solution)/shard_map/ppermute | solution.py:405
  85.6 1.3 %collective-permute-done.19 = bf16[64,2048]{1,0:T(8,128)(2,1)S(1)} collective-permute-done((bf16[64,2048]{1,0:T(8,128)(2,1)S(1)}, bf16[64,2048]{1,0:T(8,128)(2,1)S(1)}, u32[]{:S(2)}, u32[]{:S(2)}) %collective-permute-start.19) | collective-permute-done | bytes 262176 | tf_op jit(solution)/shard_map/ppermute | solution.py:405
  87.0 1.9 %collective-permute-start.20 = (bf16[64,2048]{1,0:T(8,128)(2,1)S(1)}, bf16[64,2048]{1,0:T(8,128)(2,1)S(1)}, u32[]{:S(2)}, u32[]{:S(2)}) collective-permute-start(bf16[64,2048]{1,0:T(8,128)(2,1)S(1)} %add_convert_fusion.8), channel_id=1, source_target_pairs={{0,2},{2,4},{4,6},{6,7},{7,5},{5,3},{3,1},{1,0},{8,10},{10,12},{12... | collective-permute-start | bytes 786440 | tf_op jit(solution)/shard_map/ppermute | solution.py:405
  88.9 2.2 %collective-permute-done.29 = bf16[64,2048]{1,0:T(8,128)(2,1)S(1)} collective-permute-done((bf16[64,2048]{1,0:T(8,128)(2,1)S(1)}, bf16[64,2048]{1,0:T(8,128)(2,1)S(1)}, u32[]{:S(2)}, u32[]{:S(2)}) %collective-permute-start.29) | collective-permute-done | bytes 262176 | tf_op jit(solution)/shard_map/ppermute | solution.py:405
  91.2 1.3 %collective-permute-done.26 = bf16[64,2048]{1,0:T(8,128)(2,1)S(1)} collective-permute-done((bf16[64,2048]{1,0:T(8,128)(2,1)S(1)}, bf16[64,2048]{1,0:T(8,128)(2,1)S(1)}, u32[]{:S(2)}, u32[]{:S(2)}) %collective-permute-start.26) | collective-permute-done | bytes 262176 | tf_op jit(solution)/shard_map/ppermute | solution.py:405
  92.6 1.9 %collective-permute-start.27 = (bf16[64,2048]{1,0:T(8,128)(2,1)S(1)}, bf16[64,2048]{1,0:T(8,128)(2,1)S(1)}, u32[]{:S(2)}, u32[]{:S(2)}) collective-permute-start(bf16[64,2048]{1,0:T(8,128)(2,1)S(1)} %add_convert_fusion.3), channel_id=1, source_target_pairs={{0,2},{2,4},{4,6},{6,7},{7,5},{5,3},{3,1},{1,0},{8,10},{10,12},{12... | collective-permute-start | bytes 786440 | tf_op jit(solution)/shard_map/ppermute | solution.py:405
  95.0 3.1 %collective-permute-done.20 = bf16[64,2048]{1,0:T(8,128)(2,1)S(1)} collective-permute-done((bf16[64,2048]{1,0:T(8,128)(2,1)S(1)}, bf16[64,2048]{1,0:T(8,128)(2,1)S(1)}, u32[]{:S(2)}, u32[]{:S(2)}) %collective-permute-start.20) | collective-permute-done | bytes 262176 | tf_op jit(solution)/shard_map/ppermute | solution.py:405
  98.2 1.9 %collective-permute-start.21 = (bf16[64,2048]{1,0:T(8,128)(2,1)S(1)}, bf16[64,2048]{1,0:T(8,128)(2,1)S(1)}, u32[]{:S(2)}, u32[]{:S(2)}) collective-permute-start(bf16[64,2048]{1,0:T(8,128)(2,1)S(1)} %add_convert_fusion.7), channel_id=1, source_target_pairs={{0,2},{2,4},{4,6},{6,7},{7,5},{5,3},{3,1},{1,0},{8,10},{10,12},{12... | collective-permute-start | bytes 786440 | tf_op jit(solution)/shard_map/ppermute | solution.py:405
  101.1 6.9 %collective-permute-done.3 = bf16[128,2048]{1,0:T(8,128)(2,1)S(1)} collective-permute-done((bf16[128,2048]{1,0:T(8,128)(2,1)S(1)}, bf16[128,2048]{1,0:T(8,128)(2,1)S(1)}, u32[]{:S(2)}, u32[]{:S(2)}) %collective-permute-start.3) | collective-permute-done | bytes 524320 | tf_op jit(solution)/shard_map/ppermute | solution.py:385
  (72 shorter events, 14.5 us)
Async XLA Ops:
  0.0 19.2 %collective-permute-start = (bf16[128,2048]{1,0:T(8,128)(2,1)}, bf16[128,2048]{1,0:T(8,128)(2,1)S(1)}, u32[]{:S(2)}, u32[]{:S(2)}) collective-permute-start(bf16[128,2048]{1,0:T(8,128)(2,1)} %refs_4_.3), channel_id=1, source_target_pairs={{0,16},{8,24},{16,0},{24,8},{1,17},{9,25},{17,1},{25,9},{2,18},{10... | collective-permute-start | bytes 1572872 | tf_op jit(solution)/shard_map/ppermute | solution.py:370
  4.0 9.3 %collective-permute-start.4 = (bf16[64,2048]{1,0:T(8,128)(2,1)S(1)}, bf16[64,2048]{1,0:T(8,128)(2,1)S(1)}, u32[]{:S(2)}, u32[]{:S(2)}) collective-permute-start(bf16[64,2048]{1,0:T(8,128)(2,1)S(1)} %get-tuple-element.60), channel_id=1, source_target_pairs={{0,2},{2,4},{4,6},{6,7},{7,5},{5,3},{3,1},{1,0},{8,10},{10,12},{12... | collective-permute-start | bytes 786440 | tf_op jit(solution)/shard_map/ppermute | solution.py:362
  5.7 16.1 %collective-permute-start.6 = (bf16[64,2048]{1,0:T(8,128)(2,1)S(1)}, bf16[64,2048]{1,0:T(8,128)(2,1)S(1)}, u32[]{:S(2)}, u32[]{:S(2)}) collective-permute-start(bf16[64,2048]{1,0:T(8,128)(2,1)S(1)} %get-tuple-element.60), channel_id=1, source_target_pairs={{2,0},{4,2},{6,4},{7,6},{5,7},{3,5},{1,3},{0,1},{10,8},{12,10},{14... | collective-permute-start | bytes 786440 | tf_op jit(solution)/shard_map/ppermute | solution.py:365
  6.1 14.0 %collective-permute-start.5 = (bf16[64,2048]{1,0:T(8,128)(2,1)S(1)}, bf16[64,2048]{1,0:T(8,128)(2,1)S(1)}, u32[]{:S(2)}, u32[]{:S(2)}) collective-permute-start(bf16[64,2048]{1,0:T(8,128)(2,1)S(1)} %get-tuple-element.59), channel_id=1, source_target_pairs={{0,2},{2,4},{4,6},{6,7},{7,5},{5,3},{3,1},{1,0},{8,10},{10,12},{12... | collective-permute-start | bytes 786440 | tf_op jit(solution)/shard_map/ppermute | solution.py:362
  7.7 11.1 %collective-permute-start.7 = (bf16[64,2048]{1,0:T(8,128)(2,1)S(1)}, bf16[64,2048]{1,0:T(8,128)(2,1)S(1)}, u32[]{:S(2)}, u32[]{:S(2)}) collective-permute-start(bf16[64,2048]{1,0:T(8,128)(2,1)S(1)} %get-tuple-element.59), channel_id=1, source_target_pairs={{2,0},{4,2},{6,4},{7,6},{5,7},{3,5},{1,3},{0,1},{10,8},{12,10},{14... | collective-permute-start | bytes 786440 | tf_op jit(solution)/shard_map/ppermute | solution.py:365
  13.3 9.8 %collective-permute-start.8 = (bf16[64,2048]{1,0:T(8,128)(2,1)S(1)}, bf16[64,2048]{1,0:T(8,128)(2,1)S(1)}, u32[]{:S(2)}, u32[]{:S(2)}) collective-permute-start(bf16[64,2048]{1,0:T(8,128)(2,1)S(1)} %collective-permute-done.4.refs_0_), channel_id=1, source_target_pairs={{0,2},{2,4},{4,6},{6,7},{7,5},{5,3},{3,1},{1,0},{8,10},{10,12},{12... | collective-permute-start | bytes 786440 | tf_op jit(solution)/shard_map/ppermute | solution.py:362
  20.1 23.8 %collective-permute-start.1 = (bf16[256,2048]{1,0:T(8,128)(2,1)}, bf16[256,2048]{1,0:T(8,128)(2,1)}, u32[]{:S(2)}, u32[]{:S(2)}) collective-permute-start(bf16[256,2048]{1,0:T(8,128)(2,1)} %constant_dynamic-update-slice_fusion.refs_0_), channel_id=1, source_target_pairs={{0,8},{8,0},{16,24},{24,16},{1,9},{9,1},{17,25},{25,17},{2,10},{10... | collective-permute-start | bytes 3145736 | tf_op jit(solution)/shard_map/ppermute | solution.py:374
  20.1 13.0 %collective-permute-start.9 = (bf16[64,2048]{1,0:T(8,128)(2,1)S(1)}, bf16[64,2048]{1,0:T(8,128)(2,1)S(1)}, u32[]{:S(2)}, u32[]{:S(2)}) collective-permute-start(bf16[64,2048]{1,0:T(8,128)(2,1)S(1)} %collective-permute-done.5.refs_1_), channel_id=1, source_target_pairs={{0,2},{2,4},{4,6},{6,7},{7,5},{5,3},{3,1},{1,0},{8,10},{10,12},{12... | collective-permute-start | bytes 786440 | tf_op jit(solution)/shard_map/ppermute | solution.py:362
  21.7 13.4 %collective-permute-start.10 = (bf16[64,2048]{1,0:T(8,128)(2,1)S(1)}, bf16[64,2048]{1,0:T(8,128)(2,1)S(1)}, u32[]{:S(2)}, u32[]{:S(2)}) collective-permute-start(bf16[64,2048]{1,0:T(8,128)(2,1)S(1)} %collective-permute-done.6.refs_2_), channel_id=1, source_target_pairs={{2,0},{4,2},{6,4},{7,6},{5,7},{3,5},{1,3},{0,1},{10,8},{12,10},{14... | collective-permute-start | bytes 786440 | tf_op jit(solution)/shard_map/ppermute | solution.py:365
  23.1 18.7 %collective-permute-start.12 = (bf16[64,2048]{1,0:T(8,128)(2,1)S(1)}, bf16[64,2048]{1,0:T(8,128)(2,1)S(1)}, u32[]{:S(2)}, u32[]{:S(2)}) collective-permute-start(bf16[64,2048]{1,0:T(8,128)(2,1)S(1)} %collective-permute-done.8.refs_4_), channel_id=1, source_target_pairs={{0,2},{2,4},{4,6},{6,7},{7,5},{5,3},{3,1},{1,0},{8,10},{10,12},{12... | collective-permute-start | bytes 786440 | tf_op jit(solution)/shard_map/ppermute | solution.py:362
  26.0 15.8 %collective-permute-start.15 = (bf16[64,2048]{1,0:T(8,128)(2,1)S(1)}, bf16[64,2048]{1,0:T(8,128)(2,1)S(1)}, u32[]{:S(2)}, u32[]{:S(2)}) collective-permute-start(bf16[64,2048]{1,0:T(8,128)(2,1)S(1)} %collective-permute-done.11.refs_7_), channel_id=1, source_target_pairs={{2,0},{4,2},{6,4},{7,6},{5,7},{3,5},{1,3},{0,1},{10,8},{12,10},{14... | collective-permute-start | bytes 786440 | tf_op jit(solution)/shard_map/ppermute | solution.py:365
  27.3 12.8 %all-to-all-start = ((f32[8,8,128]{2,1,0:T(8,128)}), f32[8,8,128]{2,1,0:T(8,128)S(1)}, u32[]{:S(2)}, u32[]{:S(2)}) async-start(f32[8,8,128]{2,1,0:T(8,128)} %bitcast.22), calls=%async_computation | async-start | bytes 65536 | tf_op jit(solution)/shard_map/all_to_all | solution.py:345
  33.2 18.7 %collective-permute-start.13 = (bf16[64,2048]{1,0:T(8,128)(2,1)S(1)}, bf16[64,2048]{1,0:T(8,128)(2,1)S(1)}, u32[]{:S(2)}, u32[]{:S(2)}) collective-permute-start(bf16[64,2048]{1,0:T(8,128)(2,1)S(1)} %collective-permute-done.9.refs_5_), channel_id=1, source_target_pairs={{0,2},{2,4},{4,6},{6,7},{7,5},{5,3},{3,1},{1,0},{8,10},{10,12},{12... | collective-permute-start | bytes 786440 | tf_op jit(solution)/shard_map/ppermute | solution.py:362
  35.2 16.6 %collective-permute-start.14 = (bf16[64,2048]{1,0:T(8,128)(2,1)S(1)}, bf16[64,2048]{1,0:T(8,128)(2,1)S(1)}, u32[]{:S(2)}, u32[]{:S(2)}) collective-permute-start(bf16[64,2048]{1,0:T(8,128)(2,1)S(1)} %collective-permute-done.10.refs_6_), channel_id=1, source_target_pairs={{2,0},{4,2},{6,4},{7,6},{5,7},{3,5},{1,3},{0,1},{10,8},{12,10},{14... | collective-permute-start | bytes 786440 | tf_op jit(solution)/shard_map/ppermute | solution.py:365
  41.8 10.0 %collective-permute-start.16 = (bf16[64,2048]{1,0:T(8,128)(2,1)S(1)}, bf16[64,2048]{1,0:T(8,128)(2,1)S(1)}, u32[]{:S(2)}, u32[]{:S(2)}) collective-permute-start(bf16[64,2048]{1,0:T(8,128)(2,1)S(1)} %collective-permute-done.12.refs_0_), channel_id=1, source_target_pairs={{0,2},{2,4},{4,6},{6,7},{7,5},{5,3},{3,1},{1,0},{8,10},{10,12},{12... | collective-permute-start | bytes 786440 | tf_op jit(solution)/shard_map/ppermute | solution.py:362
  42.2 9.7 %collective-permute-start.17 = (bf16[64,2048]{1,0:T(8,128)(2,1)S(1)}, bf16[64,2048]{1,0:T(8,128)(2,1)S(1)}, u32[]{:S(2)}, u32[]{:S(2)}) collective-permute-start(bf16[64,2048]{1,0:T(8,128)(2,1)S(1)} %collective-permute-done.15.refs_3_), channel_id=1, source_target_pairs={{2,0},{4,2},{6,4},{7,6},{5,7},{3,5},{1,3},{0,1},{10,8},{12,10},{14... | collective-permute-start | bytes 786440 | tf_op jit(solution)/shard_map/ppermute | solution.py:365
  66.4 7.9 %collective-permute-start.22 = (bf16[64,2048]{1,0:T(8,128)(2,1)S(1)}, bf16[64,2048]{1,0:T(8,128)(2,1)S(1)}, u32[]{:S(2)}, u32[]{:S(2)}) collective-permute-start(bf16[64,2048]{1,0:T(8,128)(2,1)S(1)} %get-tuple-element.46), channel_id=1, source_target_pairs={{2,0},{4,2},{6,4},{7,6},{5,7},{3,5},{1,3},{0,1},{10,8},{12,10},{14... | collective-permute-start | bytes 786440 | tf_op jit(solution)/shard_map/ppermute | solution.py:405
  66.5 28.1 %collective-permute-start.2 = (bf16[256,2048]{1,0:T(8,128)(2,1)S(1)}, bf16[256,2048]{1,0:T(8,128)(2,1)S(1)}, u32[]{:S(2)}, u32[]{:S(2)}) collective-permute-start(bf16[256,2048]{1,0:T(8,128)(2,1)S(1)} %copy-done.3), channel_id=1, source_target_pairs={{0,8},{8,0},{16,24},{24,16},{1,9},{9,1},{17,25},{25,17},{2,10},{10... | collective-permute-start | bytes 3145736 | tf_op jit(solution)/shard_map/ppermute | solution.py:376
  66.5 9.2 %collective-permute-start.18 = (bf16[64,2048]{1,0:T(8,128)(2,1)S(1)}, bf16[64,2048]{1,0:T(8,128)(2,1)S(1)}, u32[]{:S(2)}, u32[]{:S(2)}) collective-permute-start(bf16[64,2048]{1,0:T(8,128)(2,1)S(1)} %get-tuple-element.42), channel_id=1, source_target_pairs={{0,2},{2,4},{4,6},{6,7},{7,5},{5,3},{3,1},{1,0},{8,10},{10,12},{12... | collective-permute-start | bytes 786440 | tf_op jit(solution)/shard_map/ppermute | solution.py:405
  68.4 11.4 %collective-permute-start.28 = (bf16[64,2048]{1,0:T(8,128)(2,1)S(1)}, bf16[64,2048]{1,0:T(8,128)(2,1)S(1)}, u32[]{:S(2)}, u32[]{:S(2)}) collective-permute-start(bf16[64,2048]{1,0:T(8,128)(2,1)S(1)} %get-tuple-element.53), channel_id=1, source_target_pairs={{2,0},{4,2},{6,4},{7,6},{5,7},{3,5},{1,3},{0,1},{10,8},{12,10},{14... | collective-permute-start | bytes 786440 | tf_op jit(solution)/shard_map/ppermute | solution.py:405
  68.6 12.7 %collective-permute-start.25 = (bf16[64,2048]{1,0:T(8,128)(2,1)S(1)}, bf16[64,2048]{1,0:T(8,128)(2,1)S(1)}, u32[]{:S(2)}, u32[]{:S(2)}) collective-permute-start(bf16[64,2048]{1,0:T(8,128)(2,1)S(1)} %get-tuple-element.50), channel_id=1, source_target_pairs={{0,2},{2,4},{4,6},{6,7},{7,5},{5,3},{3,1},{1,0},{8,10},{10,12},{12... | collective-permute-start | bytes 786440 | tf_op jit(solution)/shard_map/ppermute | solution.py:405
  74.3 11.2 %collective-permute-start.23 = (bf16[64,2048]{1,0:T(8,128)(2,1)S(1)}, bf16[64,2048]{1,0:T(8,128)(2,1)S(1)}, u32[]{:S(2)}, u32[]{:S(2)}) collective-permute-start(bf16[64,2048]{1,0:T(8,128)(2,1)S(1)} %add_convert_fusion.6), channel_id=1, source_target_pairs={{2,0},{4,2},{6,4},{7,6},{5,7},{3,5},{1,3},{0,1},{10,8},{12,10},{14... | collective-permute-start | bytes 786440 | tf_op jit(solution)/shard_map/ppermute | solution.py:405
  75.7 11.2 %collective-permute-start.19 = (bf16[64,2048]{1,0:T(8,128)(2,1)S(1)}, bf16[64,2048]{1,0:T(8,128)(2,1)S(1)}, u32[]{:S(2)}, u32[]{:S(2)}) collective-permute-start(bf16[64,2048]{1,0:T(8,128)(2,1)S(1)} %add_convert_fusion.9), channel_id=1, source_target_pairs={{0,2},{2,4},{4,6},{6,7},{7,5},{5,3},{3,1},{1,0},{8,10},{10,12},{12... | collective-permute-start | bytes 786440 | tf_op jit(solution)/shard_map/ppermute | solution.py:405
  80.0 11.2 %collective-permute-start.29 = (bf16[64,2048]{1,0:T(8,128)(2,1)S(1)}, bf16[64,2048]{1,0:T(8,128)(2,1)S(1)}, u32[]{:S(2)}, u32[]{:S(2)}) collective-permute-start(bf16[64,2048]{1,0:T(8,128)(2,1)S(1)} %add_convert_fusion.2), channel_id=1, source_target_pairs={{2,0},{4,2},{6,4},{7,6},{5,7},{3,5},{1,3},{0,1},{10,8},{12,10},{14... | collective-permute-start | bytes 786440 | tf_op jit(solution)/shard_map/ppermute | solution.py:405
  81.4 11.2 %collective-permute-start.26 = (bf16[64,2048]{1,0:T(8,128)(2,1)S(1)}, bf16[64,2048]{1,0:T(8,128)(2,1)S(1)}, u32[]{:S(2)}, u32[]{:S(2)}) collective-permute-start(bf16[64,2048]{1,0:T(8,128)(2,1)S(1)} %add_convert_fusion.4), channel_id=1, source_target_pairs={{0,2},{2,4},{4,6},{6,7},{7,5},{5,3},{3,1},{1,0},{8,10},{10,12},{12... | collective-permute-start | bytes 786440 | tf_op jit(solution)/shard_map/ppermute | solution.py:405
  85.6 22.5 %collective-permute-start.24 = (bf16[64,2048]{1,0:T(8,128)(2,1)S(1)}, bf16[64,2048]{1,0:T(8,128)(2,1)S(1)}, u32[]{:S(2)}, u32[]{:S(2)}) collective-permute-start(bf16[64,2048]{1,0:T(8,128)(2,1)S(1)} %add_convert_fusion.5), channel_id=1, source_target_pairs={{2,0},{4,2},{6,4},{7,6},{5,7},{3,5},{1,3},{0,1},{10,8},{12,10},{14... | collective-permute-start | bytes 786440 | tf_op jit(solution)/shard_map/ppermute | solution.py:405
  87.0 11.2 %collective-permute-start.20 = (bf16[64,2048]{1,0:T(8,128)(2,1)S(1)}, bf16[64,2048]{1,0:T(8,128)(2,1)S(1)}, u32[]{:S(2)}, u32[]{:S(2)}) collective-permute-start(bf16[64,2048]{1,0:T(8,128)(2,1)S(1)} %add_convert_fusion.8), channel_id=1, source_target_pairs={{0,2},{2,4},{4,6},{6,7},{7,5},{5,3},{3,1},{1,0},{8,10},{10,12},{12... | collective-permute-start | bytes 786440 | tf_op jit(solution)/shard_map/ppermute | solution.py:405
  91.2 9.7 %collective-permute-start.30 = (bf16[64,2048]{1,0:T(8,128)(2,1)S(1)}, bf16[64,2048]{1,0:T(8,128)(2,1)S(1)}, u32[]{:S(2)}, u32[]{:S(2)}) collective-permute-start(bf16[64,2048]{1,0:T(8,128)(2,1)S(1)} %add_convert_fusion.1), channel_id=1, source_target_pairs={{2,0},{4,2},{6,4},{7,6},{5,7},{3,5},{1,3},{0,1},{10,8},{12,10},{14... | collective-permute-start | bytes 786440 | tf_op jit(solution)/shard_map/ppermute | solution.py:405
  92.6 15.5 %collective-permute-start.27 = (bf16[64,2048]{1,0:T(8,128)(2,1)S(1)}, bf16[64,2048]{1,0:T(8,128)(2,1)S(1)}, u32[]{:S(2)}, u32[]{:S(2)}) collective-permute-start(bf16[64,2048]{1,0:T(8,128)(2,1)S(1)} %add_convert_fusion.3), channel_id=1, source_target_pairs={{0,2},{2,4},{4,6},{6,7},{7,5},{5,3},{3,1},{1,0},{8,10},{10,12},{12... | collective-permute-start | bytes 786440 | tf_op jit(solution)/shard_map/ppermute | solution.py:405
  95.0 13.0 %collective-permute-start.3 = (bf16[128,2048]{1,0:T(8,128)(2,1)S(1)}, bf16[128,2048]{1,0:T(8,128)(2,1)S(1)}, u32[]{:S(2)}, u32[]{:S(2)}) collective-permute-start(bf16[128,2048]{1,0:T(8,128)(2,1)S(1)} %slice.107), channel_id=1, source_target_pairs={{0,16},{8,24},{16,0},{24,8},{1,17},{9,25},{17,1},{25,9},{2,18},{10... | collective-permute-start | bytes 1572872 | tf_op jit(solution)/shard_map/ppermute | solution.py:385
  98.2 10.7 %collective-permute-start.21 = (bf16[64,2048]{1,0:T(8,128)(2,1)S(1)}, bf16[64,2048]{1,0:T(8,128)(2,1)S(1)}, u32[]{:S(2)}, u32[]{:S(2)}) collective-permute-start(bf16[64,2048]{1,0:T(8,128)(2,1)S(1)} %add_convert_fusion.7), channel_id=1, source_target_pairs={{0,2},{2,4},{4,6},{6,7},{7,5},{5,3},{3,1},{1,0},{8,10},{10,12},{12... | collective-permute-start | bytes 786440 | tf_op jit(solution)/shard_map/ppermute | solution.py:405
  100.9 8.0 %collective-permute-start.31 = (bf16[64,2048]{1,0:T(8,128)(2,1)S(1)}, bf16[64,2048]{1,0:T(8,128)(2,1)S(1)}, u32[]{:S(2)}, u32[]{:S(2)}) collective-permute-start(bf16[64,2048]{1,0:T(8,128)(2,1)S(1)} %add_convert_fusion), channel_id=1, source_target_pairs={{2,0},{4,2},{6,4},{7,6},{5,7},{3,5},{1,3},{0,1},{10,8},{12,10},{14... | collective-permute-start | bytes 786440 | tf_op jit(solution)/shard_map/ppermute | solution.py:405
  (6 other events, 84.6 us)
